TPU v7x, 512 devices: a whole 4x4x16 slice. The times are simulated.
512 devices in a mesh: frag: 16 (over y, x_hi, core), band: 32 (over z, x_lo).
Axes of the slice: x: 4 (x_hi: 2, x_lo: 2; x = x_hi * 2 + x_lo), y: 4, z: 16, core: 2. Of those that a mesh axis runs over, the one named last changes fastest.
Arguments:
- bands_in: bfloat16 [16, 128, 32768], P('frag', 'band'), may hold values from -13 to 13
- potential_in: float32 [16, 64, 4096], P('frag', 'band'), may hold values from -6 to 6
- hartree: float32 [64, 128, 128], P('band', 'frag'), may hold values from -6 to 6
- patch_list: int32 [16, 3], replicated, may hold values from -1 to 127, as said below
Outputs:
- bands_out: float32 [16, 128, 32768], P('frag', 'band')
- potential_out: float32 [16, 64, 4096], P('frag', 'band')
Inputs may be any that keep to these rules, and one draw needn't show every extreme that they name: `patch_list`: column 0 is -1 or +1 and both occur; columns 1 and 2 run from 0 to 127 and the largest offset occurs.
All inputs are finite; a program needn't handle non-finite values.
Results may differ from a plain program's by a relative error of at most 0.0043.
Values may be sent and summed in bfloat16 or wider, within the bound.
No kernel may reach another device: no remote copies, remote signals or barrier semaphores. Data moves between devices by JAX's collectives and lax.ppermute only.
A program may use at most 64 MiB of HBM per device.

v0:
```python
import math

import jax
import jax.numpy as jnp
from jax import lax
from jax.sharding import PartitionSpec as P

FG = 64
NB = 128
NEWTON = 6
COEF = 16384


SLATER = 0.9847
SOFTEN = 0.25
STEP_TAU = 0.5
NORM_EPS = 1e-06


def dft_tables(grid_n):
    half_box = grid_n // 2
    quart_box = grid_n // 4
    places = jnp.arange(grid_n, dtype=jnp.float32)
    freq_xy = jnp.arange(half_box, dtype=jnp.float32) - half_box // 2
    freq_z = jnp.arange(quart_box, dtype=jnp.float32) - quart_box // 2
    angle_xy = 2.0 * math.pi / grid_n * places[:, None] * freq_xy[None, :]
    angle_z = 2.0 * math.pi / grid_n * freq_z[:, None] * places[None, :]
    cos_xy = jnp.cos(angle_xy)
    sin_xy = jnp.sin(angle_xy)
    cos_z = jnp.cos(angle_z)
    sin_z = jnp.sin(angle_z)
    fwd_xy = jnp.concatenate([cos_xy, sin_xy], axis=1)
    back_xy = jnp.concatenate([cos_xy.T, -sin_xy.T], axis=1)
    fwd_z = jnp.concatenate(
        [jnp.concatenate([cos_z, sin_z], axis=1), jnp.concatenate([-sin_z, cos_z], axis=1)], axis=0
    )
    back_z = jnp.concatenate(
        [jnp.concatenate([cos_z.T, -sin_z.T], axis=1), jnp.concatenate([sin_z.T, cos_z.T], axis=1)],
        axis=0,
    )
    return (
        fwd_z.astype(jnp.bfloat16),
        fwd_xy.astype(jnp.bfloat16),
        back_xy.astype(jnp.bfloat16),
        back_z.astype(jnp.bfloat16),
    )


def kinetic(grid_n):
    half_box = grid_n // 2
    quart_box = grid_n // 4
    freq_xy = jnp.arange(half_box, dtype=jnp.float32) - half_box // 2
    freq_z = jnp.arange(quart_box, dtype=jnp.float32) - quart_box // 2
    squares = (
        freq_xy[:, None, None, None] ** 2
        + freq_xy[None, :, None, None] ** 2
        + freq_z[None, None, None, :] ** 2
    )
    squares = jnp.broadcast_to(squares, (half_box, half_box, 2, quart_box))
    return (16.0 * squares / (grid_n * grid_n)).reshape(-1)


def swap_parts(values, half_n):
    return jnp.concatenate([-values[..., half_n:], values[..., :half_n]], axis=-1)


def first_sections(band_row, tables, grid_n):
    fwd_z, fwd_xy, back_xy, back_z = tables
    half_box = grid_n // 2
    quart_box = grid_n // 4
    section_out = jnp.dot(
        band_row.reshape(half_box * half_box, 2 * quart_box),
        fwd_z,
        preferred_element_type=jnp.float32,
    )
    section_out = section_out.astype(jnp.bfloat16).reshape(half_box, half_box, 2 * grid_n)
    stacked = jnp.concatenate([section_out, swap_parts(section_out, grid_n)], axis=1)
    section_out = jnp.einsum(
        "yj,xjc->xyc", fwd_xy, stacked, preferred_element_type=jnp.float32
    ).astype(jnp.bfloat16)
    return jnp.concatenate([section_out, swap_parts(section_out, grid_n)], axis=0).reshape(
        2 * half_box, 2 * grid_n * grid_n
    )


def to_grid(band_row, tables, grid_n):
    fwd_z, fwd_xy, back_xy, back_z = tables
    stacked = first_sections(band_row, tables, grid_n)
    grid_vals = jnp.dot(fwd_xy, stacked, preferred_element_type=jnp.float32) * (4.0 / grid_n**1.5)
    return grid_vals.reshape(grid_n, grid_n, 2 * grid_n)


def to_box(field, tables, grid_n):
    fwd_z, fwd_xy, back_xy, back_z = tables
    half_box = grid_n // 2
    stacked = jnp.concatenate([field, swap_parts(field, grid_n)], axis=0).reshape(
        2 * grid_n, 2 * grid_n * grid_n
    )
    section_out = jnp.dot(back_xy, stacked, preferred_element_type=jnp.float32)
    section_out = section_out.astype(jnp.bfloat16).reshape(half_box, grid_n, 2 * grid_n)
    stacked = jnp.concatenate([section_out, swap_parts(section_out, grid_n)], axis=1)
    section_out = jnp.einsum(
        "yj,xjc->xyc", back_xy, stacked, preferred_element_type=jnp.float32
    ).astype(jnp.bfloat16)
    box_vals = jnp.dot(
        section_out.reshape(half_box * half_box, 2 * grid_n),
        back_z,
        preferred_element_type=jnp.float32,
    )
    return (box_vals * (0.25 / grid_n**1.5)).reshape(-1)


def step_band(band_row, potential, tables, kinetic_diag, grid_n):
    grid_vals = to_grid(band_row, tables, grid_n)
    weighted = (grid_vals.reshape(grid_n, grid_n, 2, grid_n) * potential[:, :, None, :]).reshape(
        grid_n, grid_n, 2 * grid_n
    )
    image = to_box(weighted.astype(jnp.bfloat16), tables, grid_n)
    widened = band_row.astype(jnp.float32)
    return (widened - STEP_TAU * (kinetic_diag * widened + image)).astype(jnp.bfloat16)


def conj_parts(band_rows, quart_box):
    rows_n, width_n = band_rows.shape
    blocks = band_rows.reshape(rows_n, width_n // (2 * quart_box), 2, quart_box)
    return jnp.stack([blocks[:, :, 1], -blocks[:, :, 0]], axis=2).reshape(rows_n, width_n)


def real_dot(left_mat, right_mat):
    return jnp.dot(
        left_mat, right_mat, precision=lax.Precision.HIGHEST, preferred_element_type=jnp.float32
    )


def complex_mul(left_pair, right_pair):
    return (
        real_dot(left_pair[0], right_pair[0]) - real_dot(left_pair[1], right_pair[1]),
        real_dot(left_pair[0], right_pair[1]) + real_dot(left_pair[1], right_pair[0]),
    )


def newton(gram_re, gram_im, steps_n):
    size_n = gram_re.shape[0]
    scale = jnp.sqrt(jnp.sum(gram_re * gram_re + gram_im * gram_im) + NORM_EPS)
    identity = jnp.eye(size_n, dtype=jnp.float32)
    iter_y = (gram_re / scale, gram_im / scale)
    iter_z = (identity, jnp.zeros_like(identity))
    for newton_step in range(steps_n):
        product = complex_mul(iter_z, iter_y)
        factor = (1.5 * identity - 0.5 * product[0], -0.5 * product[1])
        iter_y = complex_mul(iter_y, factor)
        iter_z = complex_mul(factor, iter_z)
    root = jnp.sqrt(scale)
    return (iter_z[0] / root, iter_z[1] / root)


def band_density(band_rows, tables, grid_n):

    def add_band(carry, band_row):
        grid_vals = to_grid(band_row, tables, grid_n)
        return (carry + grid_vals * grid_vals, None)

    summed, unused = lax.scan(
        add_band, jnp.zeros((grid_n, grid_n, 2 * grid_n), jnp.float32), band_rows
    )
    return summed.reshape(grid_n, grid_n, 2, grid_n).sum(axis=2)


def xc_potential(values):
    return -SLATER * values / jnp.power(values * values + SOFTEN, 1.0 / 3.0)


def contract_first(left_mat, right_mat):
    return lax.dot_general(
        left_mat,
        right_mat,
        (((0,), (0,)), ((), ())),
        precision=lax.Precision.HIGHEST,
        preferred_element_type=jnp.float32,
    )


def contract_last(left_mat, right_mat):
    return lax.dot_general(
        left_mat, right_mat, (((1,), (1,)), ((), ())), preferred_element_type=jnp.float32
    )


def rows_onehot(global_rows, shift, period, width_n):
    return (jnp.mod(global_rows[:, None] - shift, period) == jnp.arange(width_n)[None, :]).astype(
        jnp.float32
    )


def cols_onehot(shift, period, width_n):
    return (
        jnp.mod(shift + jnp.arange(width_n)[:, None], period) == jnp.arange(period)[None, :]
    ).astype(jnp.float32)


def per_device(bands_in, potential_in, hartree, patch_list):
    tables = dft_tables(FG)
    kinetic_diag = kinetic(FG)
    period_y = 2 * FG
    period_z = 2 * FG
    whole_pot = lax.all_gather(potential_in, "band", axis=1, tiled=True)
    potential = whole_pot.reshape(FG, FG, FG)

    def step_one(band_row):
        return step_band(band_row, potential, tables, kinetic_diag, FG)

    stepped_local = lax.map(step_one, bands_in[0])
    stepped = lax.all_to_all(stepped_local, "band", split_axis=1, concat_axis=0, tiled=True)
    swapped = conj_parts(stepped, FG // 4)
    part_re = contract_last(stepped, stepped) / COEF
    part_im = contract_last(stepped, swapped) / COEF
    stepped_wide = stepped.astype(jnp.float32)
    swapped_wide = swapped.astype(jnp.float32)
    gram_re, gram_im = lax.psum((part_re, part_im), "band")
    inv_re, inv_im = newton(gram_re, gram_im, NEWTON)
    phi_coef = contract_first(inv_re, stepped_wide) - contract_first(inv_im, swapped_wide)
    phi_local = lax.all_to_all(phi_coef, "band", split_axis=0, concat_axis=1, tiled=True)
    planes = FG // lax.axis_size("band")
    partial_value = (band_density(phi_local, tables, FG) * (2.0 / NB)).reshape(FG, FG * FG)
    slab_flat = lax.psum_scatter(partial_value, "band", scatter_dimension=0, tiled=True)
    slab = slab_flat.reshape(planes, FG, FG)
    tile_rows_n = hartree.shape[1]
    frag_idx = lax.axis_index("frag")
    own_entry = lax.dynamic_slice_in_dim(patch_list, frag_idx, 1, 0)[0]
    tile_rows = frag_idx * tile_rows_n + jnp.arange(tile_rows_n)
    own_cols = cols_onehot(own_entry[2], period_z, FG)

    def row_table(shift):
        return rows_onehot(tile_rows, shift, period_y, FG)

    def col_table(shift):
        return cols_onehot(shift, period_z, FG)

    pieces = lax.all_gather(slab[None], "frag", axis=0, tiled=True)
    row_sel = jax.vmap(row_table)(patch_list[:, 1])
    col_sel = jax.vmap(col_table)(patch_list[:, 2])
    signs = patch_list[:, 0].astype(jnp.float32)
    picked = jnp.einsum("irj,ixjl->ixrl", row_sel, pieces, precision=lax.Precision.HIGHEST)
    picked = picked * signs[:, None, None, None]
    tile = jnp.einsum("ixrl,ilz->xrz", picked, col_sel, precision=lax.Precision.HIGHEST)
    total = hartree + xc_potential(tile)
    piece = lax.all_gather(total, "frag", axis=1, tiled=True)
    span = piece.shape[1]
    row_sel = rows_onehot(jnp.arange(span), own_entry[1], period_y, FG)
    back = jnp.einsum("yj,xyz,lz->xjl", row_sel, piece, own_cols, precision=lax.Precision.HIGHEST)
    return (phi_local[None], back.reshape(1, planes, FG * FG))


def solution(mesh):
    in_specs = (P("frag", "band", None), P("frag", "band", None), P("band", "frag", None), P())
    out_specs = (P("frag", "band", None), P("frag", "band", None))
    return jax.shard_map(
        per_device, mesh=mesh, in_specs=in_specs, out_specs=out_specs, check_vma=False
    )
```

profile of v0, /device:TPU:1, one launch (start us, length us, event | category | flops | bytes accessed | tf_op | source)
XLA Modules:
  0.0 975.0 jit_solution(3456538491956432838)
XLA Ops:
  7.2 1.4 copy.22
  10.8 114.6 %all-gather.2.cloned.1.call-done = f32[1,64,4096]{2,0,1:T(1,128)} async-done(((f32[1,2,4096]{2,0,1:T(1,128)}), f32[1,64,4096]{2,0,1:T(1,128)}) %all-gather.2.cloned.1.call-update) | async-done | bytes 1048592 | tf_op jit(solution)/shard_map/all_gather | solution.py:206
  125.4 1.8 copy.24
  127.2 112.8 %while.22 = (s32[]{:T(128)}, bf16[4,32768]{1,0:T(4,128)(2,1)}, bf16[4,32768]{1,0:T(4,128)(2,1)S(1)}, bf16[32,128]{1,0:T(8,128)(2,1)S(1)}, bf16[64,64]{1,0:T(8,12...) while((s32[]{:T(128)}, bf16[4,32768]{1,0:T(4,128)(2,1)}, ...), condition=%wide.region_1.2_spmd.clone, body=%wide.region_0.1_spmd.clone.sunk | while | flops 236486656 | bytes 60735764 | solution.py:212
  128.1 3.5 mul.471
  131.6 5.4 mul.472
  137.0 5.4 mul.473
  145.6 1.2 copy-done
  151.4 1.4 reshape.342
  153.2 1.6 dynamic_update_slice.6
  156.3 3.5 mul.471
  159.7 5.4 mul.472
  165.1 5.4 mul.473
  173.8 1.2 copy-done
  179.6 1.4 reshape.342
  181.3 1.6 dynamic_update_slice.6
  184.4 3.5 mul.471
  187.9 5.4 mul.472
  193.3 5.4 mul.473
  207.7 1.4 reshape.342
  209.5 1.6 dynamic_update_slice.6
  212.6 3.5 mul.471
  216.1 5.4 mul.472
  221.5 5.4 mul.473
  235.9 1.4 reshape.342
  237.6 1.6 dynamic_update_slice.6
  240.1 26.3 %all_to_all.38 = bf16[4,32,1024]{2,0,1:T(4,128)(2,1)S(1)} all-to-all(bf16[4,32,1024]{2,0,1:T(4,128)(2,1)} %bitcast.310), channel_id=1, replica_groups=mesh['frag'=16,'band'=32] {'band'}, dimensions={1} | all-to-all | bytes 524288 | tf_op jit(solution)/shard_map/all_to_all | solution.py:213
  266.5 1.6 reshape.303
  268.0 5.8 fusion.105
  273.9 4.6 copy.33
  278.5 1.5 copy.28
  281.8 252.7 %all-reduce.7.cloned.1.call-done = (f32[128,128]{1,0:T(8,128)}, f32[128,128]{1,0:T(8,128)}) async-done(((f32[128,128]{1,0:T(8,128)}, f32[128,128]{1,0:T(8,128)}), (f32[128,128]{1,0:T(8,128)}, f32[128,128]{1,0:T(8,128)})) %all-reduce.7.cloned.1.call-update) | async-done | bytes 131088 | tf_op jit(solution)/shard_map/psum | solution.py:219
  534.6 1.5 add_reduce_fusion
  558.5 7.0 all-to-all-start.1
  565.6 21.9 %all-to-all-done.1 = f32[32,4,1024]{2,1,0:T(4,128)S(1)} async-done(((f32[32,4,1024]{2,1,0:T(4,128)}), f32[32,4,1024]{2,1,0:T(4,128)S(1)}, u32[]{:S(2)}, u32[]{:S(2)}) %all-to-all-start.1) | async-done | bytes 524320 | tf_op jit(solution)/shard_map/all_to_all | solution.py:222
  587.5 25.4 %while.23 = (s32[]{:T(128)}, f32[64,64,128]{2,1,0:T(8,128)}, f32[4,32768]{1,0:T(4,128)S(1)}, bf16[32,128]{1,0:T(8,128)(2,1)S(1)}, bf16[64,64]{1,0:T(8,128)(2,1)S(1)}, /*index=5*/s32[]{:T(128)}, s32[]{:T(128)}) while((s32[]{:T(128)}, f32[64,64,128]{2,1,0:T(8,128)}, f32[4,32768]{1,0:T(4,128)S(1)}, bf16[32,128]{1,0:T(8,128)(2,1)S(1)}, ...), condition=%wide.region_8.9_spmd.clone, body=%wide.region_7.8_spmd.clone.sunk | while | flops 116326400 | bytes 19030116 | solution.py:163
  590.9 2.0 bitcast_add_fusion.2
  596.0 3.5 bitcast_add_fusion.2
  602.7 3.5 bitcast_add_fusion.2
  609.4 3.5 bitcast_add_fusion.2
  612.9 5.6 reshape.305
  618.6 7.7 reduce_sum.19
  626.3 1.5 broadcast_multiply_fusion
  627.8 2.9 mul.305
  630.7 1.3 dynamic-slice
  634.6 258.8 %all-reduce.5.cloned.1.call-done = f32[64,4096]{1,0:T(8,128)} async-done(((f32[64,4096]{1,0:T(8,128)}), f32[64,4096]{1,0:T(8,128)}) %all-reduce.5.cloned.1.call-update) | async-done | bytes 1048592
  894.5 50.9 %all_gather.10 = f32[16,2,64,64]{3,2,1,0:T(8,128)S(1)} all-gather(f32[1,2,64,64]{3,2,1,0:T(8,128)S(1)} %broadcast_in_dim_reshape.4), channel_id=1, replica_groups=mesh['frag'=16,'band'=32] {'frag'}, dimensions={0}, use_global_device_ids=true | all-gather | bytes 557056 | tf_op jit(solution)/shard_map/all_gather | solution.py:239
  946.4 19.8 %all_gather.11 = f32[2,128,128]{2,1,0:T(8,128)S(1)} all-gather(f32[2,8,128]{2,1,0:T(8,128)S(1)} %multiply_add_fusion), channel_id=1, replica_groups=mesh['frag'=16,'band'=32] {'frag'}, dimensions={1}, use_global_device_ids=true | all-gather | bytes 139264 | tf_op jit(solution)/shard_map/all_gather | solution.py:247
  (292 shorter events, 83.6 us)
Async XLA Ops:
  7.2 120.1 %copy-start.3 = (bf16[1,4,32768]{2,1,0:T(4,128)(2,1)S(1)}, bf16[1,4,32768]{2,1,0:T(4,128)(2,1)}, u32[]{:S(2)}) copy-start(bf16[1,4,32768]{2,1,0:T(4,128)(2,1)} %param.8) | copy-start | bytes 786436
  7.2 118.2 %all-gather.2.cloned.1.call-start = ((), (), s32[]{:S(2)}) async-start(), calls=%async_computation.2 | async-start | bytes 1081344 | tf_op jit(solution)/shard_map/all_gather | solution.py:206
  8.7 525.9 %all-reduce.7.cloned.1.call-start = ((), (), s32[]{:S(2)}) async-start(), calls=%async_computation.4 | async-start | bytes 262144 | tf_op jit(solution)/shard_map/psum | solution.py:219
  145.2 1.6 copy-start
  149.8 1.2 copy-start.1
  150.5 2.3 copy-start.4
  150.7 2.4 copy-start.6
  154.7 0.7 copy-start.7
  173.4 1.6 copy-start
  178.0 1.2 copy-start.1
  178.7 2.3 copy-start.4
  178.9 2.4 copy-start.6
  182.9 0.7 copy-start.7
  201.6 1.6 copy-start
  206.2 1.2 copy-start.1
  206.8 2.3 copy-start.4
  207.1 2.4 copy-start.6
  211.0 0.7 copy-start.7
  229.7 1.6 copy-start
  234.3 1.2 copy-start.1
  235.0 2.3 copy-start.4
  235.2 2.4 copy-start.6
  239.2 0.7 copy-start.7
  273.8 4.7 copy-start.2
  534.6 10.0 %copy-start.5 = (f32[128,128]{1,0:T(8,128)S(1)}, f32[128,128]{1,0:T(8,128)}, u32[]{:S(2)}) copy-start(f32[128,128]{1,0:T(8,128)} %get-tuple-element.168) | copy-start | bytes 196612
  556.5 9.1 copy-start.8
  558.5 29.0 %all-to-all-start.1 = ((f32[32,4,1024]{2,1,0:T(4,128)}), f32[32,4,1024]{2,1,0:T(4,128)S(1)}, u32[]{:S(2)}, u32[]{:S(2)}) async-start(f32[32,4,1024]{2,1,0:T(4,128)} %all_to_all.32), calls=%async_computation.1 | async-start | bytes 1048576 | tf_op jit(solution)/shard_map/all_to_all | solution.py:222
  565.5 328.0 %all-reduce.5.cloned.1.call-start = ((), (), s32[]{:S(2)}) async-start(), calls=%async_computation.3 | async-start | bytes 2097152
  630.7 315.3 %copy-start.9 = (f32[2,8,128]{2,1,0:T(8,128)S(1)}, f32[2,8,128]{2,1,0:T(8,128)}, u32[]{:S(2)}) copy-start(f32[2,8,128]{2,1,0:T(8,128)} %param.10) | copy-start | bytes 24580
Sparse Core Ops, SparseCore 0:
  10.6 114.7 all-gather.1
  282.0 252.5 all-reduce.6
  630.8 262.6 all-reduce.4
where the time goes:
time: 988 us; the launch traced here: 975 us
  waiting for transfers between devices  648 us (66%)
  local copies, waits for them, and re-layouts  125 us (13%)
  blocking collectives  97.1 us (10%)
  other arithmetic  42.1 us (4%)
  matrix products  37.9 us (4%)
  between operations  16.3 us (2%)
    unnamed x4, waiting for transfers between devices  259 us
    psum x1, waiting for transfers between devices, per_device(): gram_re, gram_im = lax.psum((part_re, part_im), 'band')  253 us
    all_gather x1, waiting for transfers between devices, per_device(): whole_pot = lax.all_gather(potential_in, 'band', axis=1, tiled=True)  115 us
    mul x16, local copies, waits for them, and re-layouts, step_band(): grid_vals.reshape(grid_n, grid_n, 2, grid_n) * potential[:, :, None, :]  60.5 us
    all_gather x1, blocking collectives, per_device(): pieces = lax.all_gather(slab[None], 'frag', axis=0, tiled=True)  50.9 us
    all_to_all x1, blocking collectives, per_device(): lax.all_to_all(stepped_local, 'band', split_axis=1, concat_axis=0, tiled=...  26.3 us
    all_to_all x1, waiting for transfers between devices, per_device(): lax.all_to_all(phi_coef, 'band', split_axis=0, concat_axis=1, tiled=True)  21.9 us
    all_gather x1, blocking collectives, per_device(): piece = lax.all_gather(total, 'frag', axis=1, tiled=True)  19.8 us
  transfers between devices with their start and end apart: 4, of which 4 were waited for; matrix products, arithmetic and copies ran while one was open for 1% of the time, Pallas kernels for 0%

commit v1 on v0

v1 whole, which is shorter than its diff:
```python
import math

import numpy as np

import jax
import jax.numpy as jnp
from jax import lax
from jax.experimental import pallas as pl
from jax.experimental.pallas import tpu as pltpu
from jax.sharding import PartitionSpec as P

FG = 64
NB = 128
NEWTON = 6
COEF = 16384
FRAGS = 16
GY = 128
GZ = 128
HB = FG // 2
QB = FG // 4

SLATER = 0.9847
SOFTEN = 0.25
STEP_TAU = 0.5
NORM_EPS = 1e-06

F32 = jnp.float32
BF16 = jnp.bfloat16
LOCAL = 4
LANES = 128


def dft_tables():
    places = np.arange(FG)
    freq_xy = np.arange(HB) - HB // 2
    freq_z = np.arange(QB) - QB // 2
    turn_xy = 2.0 * math.pi / FG * ((places[:, None] * freq_xy[None, :]) % FG)
    turn_z = 2.0 * math.pi / FG * ((freq_z[:, None] * places[None, :]) % FG)
    cos_xy, sin_xy = np.cos(turn_xy), np.sin(turn_xy)
    cos_z, sin_z = np.cos(turn_z), np.sin(turn_z)
    same = np.eye(LOCAL)
    fwd_x = np.stack([np.einsum("ab,xk->axbk", same, t) for t in (cos_xy, sin_xy)], axis=2)
    fwd_x = fwd_x.reshape(LOCAL * FG, 2 * LOCAL * HB)
    fwd_x_send = (
        fwd_x.reshape(LOCAL, FG // 2, 2, -1).transpose(1, 2, 0, 3).reshape(LOCAL * FG, -1)
    )
    back_x = np.stack([np.einsum("ab,xk->akbx", same, t) for t in (cos_xy, -sin_xy)], axis=2)
    back_x = back_x.reshape(LOCAL * HB, 2 * LOCAL * FG)
    fwd_y = np.stack(
        [np.stack([cos_xy.T, sin_xy.T], axis=2), np.stack([-sin_xy.T, cos_xy.T], axis=2)], axis=1
    ).reshape(2 * HB, 2 * FG)
    one_z = np.block([[cos_z, sin_z], [-sin_z, cos_z]])
    fwd_z = np.einsum("ab,kz->akbz", same, one_z).reshape(LOCAL * 2 * QB, LOCAL * 2 * FG)
    send = np.einsum("ab,kl->kabl", same, np.eye(HB)).reshape(LOCAL * HB, LOCAL * HB)
    return tuple(
        jnp.asarray(t, dtype=F32).astype(BF16)
        for t in (fwd_x, fwd_x_send, back_x, fwd_y, fwd_z, send)
    )


def iota(shape, axis):
    return lax.broadcasted_iota(jnp.int32, shape, axis)


def dot(left, right):
    return jnp.dot(left, right, preferred_element_type=F32)


def dot_t(left, right):
    return lax.dot_general(left, right, (((1,), (1,)), ((), ())), preferred_element_type=F32)


def times_i(block):
    first = iota(block.shape, 1) % (2 * QB) < QB
    ahead = pltpu.roll(block, LANES - QB, 1)
    behind = pltpu.roll(block, QB, 1)
    return jnp.where(first, -ahead, behind)


def halves(values):
    upper = values.astype(BF16)
    return upper, (values - upper.astype(F32)).astype(BF16)


def forward_kernel(bands_ref, fwd_x_ref, fwd_y_ref, big_y_ref, out_ref, rows_ref, stack_ref):
    width = FG * 2 * QB
    spread = (iota((2 * FG, width), 1) // QB == iota((2 * FG, width), 0)).astype(F32).astype(BF16)
    rows_ref[...] = dot(fwd_y_ref[...], spread)
    same = iota((QB, width), 1) % QB == iota((QB, width), 0)

    @pl.loop(0, 2 * HB)
    def _(row):
        line = jnp.broadcast_to(rows_ref[pl.ds(row, 1), :], (QB, width))
        start = pl.multiple_of(row * QB, QB)
        big_y_ref[pl.ds(start, QB), :] = jnp.where(same, line, 0.0).astype(BF16)

    rows_n = LOCAL * HB
    stack_ref[:rows_n, :] = bands_ref[...]
    for start in range(0, HB * 2 * QB, LANES):
        block = bands_ref[:, start : start + LANES].astype(F32)
        stack_ref[rows_n:, start : start + LANES] = times_i(block).astype(BF16)
    after_x = dot(fwd_x_ref[...], stack_ref[...]).astype(BF16)

    @pl.loop(0, width // 512)
    def _(at):
        span = pl.ds(pl.multiple_of(at * 512, 512), 512)
        out_ref[:, span] = dot(after_x, big_y_ref[:, span]).astype(BF16)


def spread_parts(pair):
    low = iota(pair.shape, 1) < FG
    turned = pltpu.roll(pair, FG, 1)
    return jnp.where(low, pair, turned), jnp.where(low, turned, pair)


def step_kernel(
    after_y_ref, pot_ref, bands_ref, big_y_ref, fwd_z_ref, back_x_ref, fwd_x_ref, send_ref,
    stepped_ref, image_ref, back_ref, stack_ref, stack2_ref,
):
    fwd_z = fwd_z_ref[...]

    @pl.loop(0, FG // LOCAL)
    def _(at):
        span = pl.ds(pl.multiple_of(at * LANES, LANES), LANES)
        grid_vals = dot(after_y_ref[:, span], fwd_z) * (4.0 / FG**1.5)
        pot = pot_ref[:, pl.ds(pl.multiple_of(at * 2 * LANES, 2 * LANES), 2 * LANES)].astype(F32)
        pots = jnp.concatenate(
            [*spread_parts(pot[:, :LANES]), *spread_parts(pot[:, LANES:])], axis=1
        )
        pots = jnp.concatenate([pots] * LOCAL, axis=0)
        weighted = (grid_vals * pots).astype(BF16)
        back_ref[:, span] = dot_t(weighted, fwd_z).astype(BF16)

    rows_n = LOCAL * FG

    @pl.loop(0, HB * 2 * QB // LANES)
    def _(at):
        span = pl.ds(pl.multiple_of(at * LANES, LANES), LANES)
        block = dot_t(back_ref[...], big_y_ref[span, :])
        stack_ref[:rows_n, span] = block.astype(BF16)
        stack_ref[rows_n:, span] = times_i(block).astype(BF16)

    half_n = LOCAL * HB
    for start in range(0, HB * 2 * QB, LANES):
        image = dot(back_x_ref[...], stack_ref[:, start : start + LANES]) * (0.25 / FG**1.5)
        shape = (half_n, LANES)
        row, lane = iota(shape, 0), iota(shape, 1) + start
        mx, my = row % HB - HB // 2, lane // (2 * QB) - HB // 2
        mz = lane % QB - QB // 2
        kinetic = (mx * mx + my * my + mz * mz).astype(F32) * (16.0 / FG**2)
        wide = bands_ref[:, start : start + LANES].astype(F32)
        stepped = (wide - STEP_TAU * (kinetic * wide + image)).astype(BF16)
        stack2_ref[:half_n, start : start + LANES] = stepped
        stack2_ref[half_n:, start : start + LANES] = times_i(stepped.astype(F32)).astype(BF16)
    stepped_ref[...] = dot(send_ref[...], stack2_ref[:half_n, :]).astype(BF16)
    image_ref[...] = dot(fwd_x_ref[...], stack2_ref[...]).astype(BF16)


def gram_kernel(stepped_ref, out_ref, conj_ref):
    for start in range(0, HB * 2 * QB, LANES):
        block = stepped_ref[:, start : start + LANES].astype(F32)
        conj_ref[:, start : start + LANES] = (-times_i(block)).astype(BF16)
    stepped = stepped_ref[...]
    gram_re = dot_t(stepped, stepped)
    gram_im = dot_t(stepped, conj_ref[...])
    shape = (NB, NB)
    out_ref[...] = jnp.where(iota(shape, 0) >= iota(shape, 1), gram_re, gram_im) * (1.0 / COEF)


def complex_mul(left, right):
    turned = jnp.concatenate([-left[NB:], left[:NB]], axis=0)
    left_hi, left_lo = halves(jnp.concatenate([left, turned], axis=1))
    right_hi, right_lo = halves(right)
    first = dot(left_hi, jnp.concatenate([right_hi, right_lo], axis=1))
    return first[:, :NB] + (first[:, NB:] + dot(left_lo, right_hi))


def newton_kernel(gram_ref, stepped_ref, phi_ref, inv_ref, stack_ref):
    packed = gram_ref[...]
    flipped = packed.T
    shape = (NB, NB)
    row, col = iota(shape, 0), iota(shape, 1)
    gram_re = jnp.where(row >= col, packed, flipped)
    gram_im = jnp.where(row < col, packed, jnp.where(row > col, -flipped, 0.0))
    total = jnp.sum(gram_re * gram_re + gram_im * gram_im, axis=1, keepdims=True)
    scale = jnp.sqrt(jnp.sum(total, axis=0, keepdims=True) + NORM_EPS)
    eye = (row == col).astype(F32)
    identity = jnp.concatenate([eye, jnp.zeros(shape, F32)], axis=0)
    iter_y = jnp.concatenate([gram_re, gram_im], axis=0) / scale
    iter_z = identity
    for at in range(NEWTON):
        product = complex_mul(iter_z, iter_y) if at else iter_y
        factor = 1.5 * identity - 0.5 * product
        if at < NEWTON - 1:
            iter_y = complex_mul(iter_y, factor)
        iter_z = complex_mul(factor, iter_z) if at else factor
    inverse = iter_z / jnp.sqrt(scale)
    inv_re, inv_im = inverse[:NB].T, inverse[NB:].T
    re_hi, re_lo = halves(inv_re)
    im_hi, im_lo = halves(inv_im)
    inv_ref[...] = jnp.concatenate([re_hi, im_hi, re_lo, im_lo], axis=0)
    stack_ref[:NB, :] = stepped_ref[...]
    for start in range(0, HB * 2 * QB, LANES):
        block = stepped_ref[:, start : start + LANES].astype(F32)
        stack_ref[NB:, start : start + LANES] = times_i(block).astype(BF16)
    left = jnp.concatenate(
        [jnp.concatenate([re_hi, im_hi], axis=1), jnp.concatenate([re_lo, im_lo], axis=1)], axis=0
    )
    both = dot(left, stack_ref[...])
    phi_ref[...] = (both[:NB] + both[NB:]).astype(BF16)


def density_kernel(
    place_ref, own_ref, image_ref, inv_ref, big_y_ref, fwd_z_ref,
    out_ref, stack_ref, phi_ref, after_y_ref, dens_ref, wide_ref,
):
    rows_n = 2 * NB
    shape = (NB, 2 * rows_n)
    row, col = iota(shape, 0), iota(shape, 1)
    inner = col % rows_n
    picks = (inner // 8 * LOCAL + inner % LOCAL == row) & (inner // LOCAL % 2 == col // rows_n)
    spread = dot(inv_ref[...], picks.astype(F32).astype(BF16)).astype(BF16)
    stack_ref[:rows_n, :] = image_ref[...]
    for start in range(0, HB * 2 * QB, LANES):
        block = image_ref[:, start : start + LANES].astype(F32)
        stack_ref[rows_n:, start : start + LANES] = times_i(block).astype(BF16)
    left = jnp.concatenate(
        [
            jnp.concatenate(
                [
                    spread[base : base + NB, at * rows_n : (at + 1) * rows_n]
                    for base in (low, low + NB)
                ],
                axis=1,
            )
            for low in (0, 2 * NB)
            for at in (0, 1)
        ],
        axis=0,
    )
    both = dot(left, stack_ref[...])
    phi_ref[...] = (both[:rows_n] + both[rows_n:]).astype(BF16)
    width = FG * 2 * QB

    @pl.loop(0, width // 512)
    def _(at):
        span = pl.ds(pl.multiple_of(at * 512, 512), 512)
        after_y_ref[:, span] = dot(phi_ref[...], big_y_ref[:, span]).astype(BF16)

    low = iota((1, LANES), 1) < FG

    @pl.loop(0, FG // LOCAL)
    def _(at):
        span = pl.ds(pl.multiple_of(at * LANES, LANES), LANES)
        grid_vals = dot(after_y_ref[:, span], fwd_z_ref[...]) * (4.0 / FG**1.5)
        square = grid_vals * grid_vals
        sums = [
            jnp.sum(square[plane * NB : (plane + 1) * NB], axis=0, keepdims=True) * (2.0 / NB)
            for plane in (0, 1)
        ]
        for y_lo in range(LOCAL):
            parts = [s[:, y_lo * LANES : (y_lo + 1) * LANES] for s in sums]
            full = [p + pltpu.roll(p, FG, 1) for p in parts]
            dens_ref[pl.ds(at * LOCAL + y_lo, 1), :] = jnp.where(low, full[0], full[1])

    own = own_ref[0]
    own_y, own_z = place_ref[own, 1], place_ref[own, 2]
    sign = place_ref[own, 0].astype(F32)
    dens = (dens_ref[...] * sign).astype(BF16)
    shape = (LANES, LANES)
    row, col = iota(shape, 0), iota(shape, 1)
    same_plane = row // FG == col // FG
    rows_shape = (FG, FG)
    rows_row, rows_col = iota(rows_shape, 0), iota(rows_shape, 1)
    for to in range(FRAGS):
        shift_y = place_ref[to, 1] - own_y + GY
        shift_z = place_ref[to, 2] - own_z + GZ
        cols = same_plane & ((col % FG + shift_z) % GZ == row % FG)
        moved = dot(dens, cols.astype(F32).astype(BF16)).astype(BF16)
        rows = (rows_row + shift_y) % GY == rows_col
        out_ref[to] = dot(rows.astype(F32).astype(BF16), moved).astype(BF16)


def hartree_kernel(place_ref, own_ref, tiles_ref, out_ref):
    own = own_ref[0]
    own_y, own_z = place_ref[own, 1], place_ref[own, 2]
    rows = (iota((FG, GY), 0) + own_y) % GY == iota((FG, GY), 1)
    rows = rows.astype(F32).astype(BF16)
    shape = (GZ, LANES)
    row, col = iota(shape, 0), iota(shape, 1)
    total = jnp.zeros((FG, LANES), F32)
    for plane in (0, 1):
        cols = (col // FG == plane) & ((col % FG + own_z) % GZ == row)
        cols = cols.astype(F32).astype(BF16)
        rest = tiles_ref[:, plane].reshape(GY, GZ)
        for _ in range(3):
            part = rest.astype(BF16)
            total += dot(dot(rows, part).astype(BF16), cols)
            rest = rest - part.astype(F32)
    out_ref[...] = total


def xc_potential(values):
    return -SLATER * values / jnp.power(values * values + SOFTEN, 1.0 / 3.0)


VM = pl.BlockSpec(memory_space=pltpu.VMEM)
SM = pl.BlockSpec(memory_space=pltpu.SMEM)


def sds(shape, dtype):
    return jax.ShapeDtypeStruct(shape, dtype)


def call(kernel, outs, in_specs, scratch, flops, moved, name):
    return pl.pallas_call(
        kernel,
        out_shape=outs,
        in_specs=in_specs,
        out_specs=jax.tree.map(lambda _: VM, outs),
        scratch_shapes=[pltpu.VMEM(s, d) for s, d in scratch],
        cost_estimate=pl.CostEstimate(flops=flops, bytes_accessed=moved, transcendentals=0),
        name=name,
    )


def stages():
    coefs = HB * 2 * QB
    width = FG * 2 * QB
    mega = 1 << 20
    forward = call(
        forward_kernel,
        (sds((coefs, width), BF16), sds((LOCAL * FG, width), BF16)),
        [VM] * 3,
        [((2 * HB, width), F32), ((2 * LOCAL * HB, coefs), BF16)],
        2 * 10**9, 6 * mega, "forward",
    )
    step = call(
        step_kernel,
        (sds((LOCAL * HB, coefs), BF16), sds((LOCAL * FG, coefs), BF16)),
        [VM] * 8,
        [
            ((LOCAL * FG, width), BF16),
            ((2 * LOCAL * FG, coefs), BF16),
            ((2 * LOCAL * HB, coefs), BF16),
        ],
        4 * 10**9, 8 * mega, "step",
    )
    gram = call(
        gram_kernel, sds((NB, NB), F32), [VM], [((NB, coefs), BF16)], 10**8, mega // 2, "gram"
    )
    newton = call(
        newton_kernel,
        (sds((NB, coefs), BF16), sds((4 * NB, NB), BF16)),
        [VM] * 2,
        [((2 * NB, coefs), BF16)],
        10**9, mega, "newton",
    )
    density = call(
        density_kernel,
        sds((FRAGS, FG, LANES), BF16),
        [SM, SM] + [VM] * 4,
        [
            ((4 * NB, coefs), BF16),
            ((2 * NB, coefs), BF16),
            ((2 * NB, width), BF16),
            ((FG, LANES), F32),
            ((8, LANES), F32),
        ],
        4 * 10**9, 6 * mega, "density",
    )
    hartree = call(
        hartree_kernel, sds((FG, LANES), F32), [SM, SM, VM], [], 10**7, mega // 4, "hartree"
    )
    return forward, step, gram, newton, density, hartree


def exchange(values, axis):
    return lax.all_to_all(values, axis, split_axis=0, concat_axis=0, tiled=True)


def per_device(bands_in, potential_in, hartree, patch_list):
    fwd_x, fwd_x_send, back_x, fwd_y, fwd_z, send = dft_tables()
    forward, step, gram, newton, density, hartree_window = stages()
    coefs = HB * 2 * QB
    groups = lax.axis_size("band")
    planes = FG // groups
    own = lax.axis_index("frag").astype(jnp.int32).reshape(1)

    pot_send = jnp.broadcast_to(potential_in.astype(BF16), (groups, planes, FG * FG))
    pot = exchange(pot_send, "band").reshape(FG, FG * FG)
    tiles = exchange(jnp.broadcast_to(hartree[None], (FRAGS, *hartree.shape)), "frag")
    bands = bands_in.reshape(LOCAL * HB, coefs)
    big_y, after_y = forward(bands, fwd_x, fwd_y)
    stepped_send, image_send = step(
        after_y, pot, bands, big_y, fwd_z, back_x, fwd_x_send, send
    )
    stepped = exchange(stepped_send.reshape(groups, LOCAL, coefs), "band").reshape(NB, coefs)
    image = exchange(image_send.reshape(groups, planes * LOCAL, coefs), "band")
    image = image.reshape(2 * NB, coefs)
    window = hartree_window(patch_list, own, tiles)
    part = gram(stepped)
    rows = exchange(part.reshape(groups, LOCAL, NB), "band").sum(axis=0)
    whole = exchange(jnp.broadcast_to(rows[None], (groups, LOCAL, NB)), "band").reshape(NB, NB)
    phi, inverse = newton(whole, stepped)
    phi_local = exchange(phi.reshape(groups, LOCAL, coefs), "band")
    pieces = exchange(density(patch_list, own, image, inverse, big_y, fwd_z), "frag")
    patched = pieces.astype(F32).sum(axis=0)
    total = window + xc_potential(patched)
    back = total.reshape(FG, planes, FG).transpose(1, 0, 2).reshape(1, planes, FG * FG)
    bands_out = phi_local.transpose(1, 0, 2).astype(F32).reshape(1, LOCAL, HB * coefs)
    return (bands_out, back)


def solution(mesh):
    in_specs = (P("frag", "band", None), P("frag", "band", None), P("band", "frag", None), P())
    out_specs = (P("frag", "band", None), P("frag", "band", None))
    return jax.shard_map(
        per_device, mesh=mesh, in_specs=in_specs, out_specs=out_specs, check_vma=False
    )
```

time: 988 us -> 229 us (0.23); the launches traced: 975 us -> 228 us
  waiting for transfers between devices: 648 us -> 70.8 us
  local copies, waits for them, and re-layouts: 125 us -> 8.98 us
  Pallas kernels: 0 us -> 42.3 us
  other arithmetic: 42.1 us -> 2.53 us
  blocking collectives: 97.1 us -> 57.8 us
  matrix products: 37.9 us -> 0 us
  starting transfers between devices: 7.1 us -> 44.6 us
  between operations: 16.3 us -> 0.73 us
    unnamed x4 -> x0, waiting for transfers between devices: 259 us -> none
    psum x1 -> x0, waiting for transfers between devices: 253 us -> none  [per_device(): gram_re, gram_im = lax.psum((part_re, part_im), 'band')]
    all_gather x1 -> x0, waiting for transfers between devices: 115 us -> none  [per_device(): whole_pot = lax.all_gather(potential_in, 'band', axis=1, tiled=True)]
    all_gather x2 -> x0, blocking collectives: 70.7 us -> none  [the longest x1 50.9 us: per_device(): pieces = lax.all_gather(slab[None], 'frag', axis=0, tiled=True)]
    mul x21 -> x0, local copies, waits for them, and re-layouts: 64.2 us -> none  [the longest x16 60.5 us: step_band(): grid_vals.reshape(grid_n, grid_n, 2, grid_n) * potential[:, :, None, :]]
    all_to_all x1 -> x5, waiting for transfers between devices: 21.9 us -> 70.8 us  [exchange(): return lax.all_to_all(values, axis, split_axis=0, concat_axis=0, tiled=True)]
    pallas_call x0 -> x6, Pallas kernels: none -> 42.3 us  [the longest x1 14.4 us: per_device(): step(after_y, pot, bands, big_y, fwd_z, back_x, fwd_x_send, send)]
    dot_general x110 -> x0, matrix products: 37.9 us -> none  [the longest x66 17.5 us: real_dot(): jnp.dot(left_mat, right_mat, precision=lax.Precision.HIGHEST, preferred_e...]
  transfers between devices with their start and end apart: 4 -> 5, of which waited for: 4 -> 4; matrix products, arithmetic and copies ran while one was open for 1% -> 2% of each run, Pallas kernels for 0% -> 11%
where the time goes in v1:
time: 229 us; the launch traced here: 228 us
  waiting for transfers between devices  70.8 us (31%)
  blocking collectives  57.8 us (25%)
  starting transfers between devices  44.6 us (19%)
  Pallas kernels  42.3 us (18%)
  local copies, waits for them, and re-layouts  8.98 us (4%)
  other arithmetic  2.53 us (1%)
    all_to_all x5, waiting for transfers between devices, exchange(): return lax.all_to_all(values, axis, split_axis=0, concat_axis=0, tiled=True)  70.8 us
    all_to_all x3, blocking collectives, exchange(): return lax.all_to_all(values, axis, split_axis=0, concat_axis=0, tiled=True)  57.8 us
    all_to_all x5, starting transfers between devices, exchange(): return lax.all_to_all(values, axis, split_axis=0, concat_axis=0, tiled=True)  44.6 us
    pallas_call x1, Pallas kernels, per_device(): step(after_y, pot, bands, big_y, fwd_z, back_x, fwd_x_send, send)  14.4 us
    pallas_call x1, Pallas kernels, per_device(): density(patch_list, own, image, inverse, big_y, fwd_z)  12.9 us
    pallas_call x1, Pallas kernels, per_device(): big_y, after_y = forward(bands, fwd_x, fwd_y)  6.48 us
    pallas_call x1, Pallas kernels, per_device(): phi, inverse = newton(whole, stepped)  4.7 us
  transfers between devices with their start and end apart: 5, of which 4 were waited for; matrix products, arithmetic and copies ran while one was open for 2% of the time, Pallas kernels for 11%

profile of v1, /device:TPU:1, one launch (start us, length us, event | category | flops | bytes accessed | tf_op | source)
XLA Modules:
  0.0 227.7 jit_solution(13225060876057820178)
XLA Ops:
  0.6 0.8 convert_bitcast_fusion
  1.4 1.3 broadcast_in_dim.9
  2.7 16.9 %all-to-all-start = ((bf16[32,2,4096]{2,1,0:T(2,128)(2,1)}), bf16[32,2,4096]{2,1,0:T(2,128)(2,1)S(1)}, u32[]{:S(2)}, u32[]{:S(2)}) async-start(bf16[32,2,4096]{2,1,0:T(2,128)(2,1)} %broadcast_in_dim.9), calls=%async_computation | async-start | bytes 1048576 | tf_op jit(solution)/shard_map/all_to_all | solution.py:379
  19.6 1.8 reshape.48.bands_ref
  21.5 6.5 %forward.1 = (bf16[1024,2048]{1,0:T(8,128)(2,1)}, bf16[256,2048]{1,0:T(8,128)(2,1)}) custom-call(bf16[128,1024]{1,0:T(8,128)(2,1)} %reshape.48.bands_ref, bf16[256,256]{1,0:T(8,128)(2,1)} %constant.36.fwd_x_ref, bf16[64,128]{1,0:T(8,128)(2,1)} %constant.37.fwd_y_ref), custom_call_target="tpu_custom_call" | custom-call | flops 2000000000 | bytes 6291456 | tf_op jit(solution)/shard_map/forward/pallas_call | solution.py:394
  27.9 23.0 %all-to-all-done = bf16[32,2,4096]{2,1,0:T(2,128)(2,1)S(1)} async-done(((bf16[32,2,4096]{2,1,0:T(2,128)(2,1)}), bf16[32,2,4096]{2,1,0:T(2,128)(2,1)S(1)}, u32[]{:S(2)}, u32[]{:S(2)}) %all-to-all-start) | async-done | bytes 524320 | tf_op jit(solution)/shard_map/all_to_all | solution.py:379
  51.0 1.0 reshape.49.pot_ref
  52.0 0.0 copy-start.4
  52.0 14.4 %step.1 = (bf16[128,1024]{1,0:T(8,128)(2,1)}, bf16[256,1024]{1,0:T(8,128)(2,1)}) custom-call(bf16[256,2048]{1,0:T(8,128)(2,1)} %get-tuple-element.8.after_y_ref, bf16[64,4096]{1,0:T(8,128)(2,1)} %reshape.49.pot_ref, bf16[128,1024]{1,0:T(8,128)(2,1)} %reshape.48.bands_ref, bf16[1024,2048]{1,0:T(8,128)(2,1)} %get-tuple-element.9.big_y_ref, ...), custom_call_target="tpu_custom_call" | custom-call | flops 4000000000 | bytes 8388608 | tf_op jit(solution)/shard_map/step/pallas_call | solution.py:395
  66.3 0.0 copy-start.3
  66.3 1.1 reshape.50
  67.4 25.0 %all_to_all.40 = bf16[32,4,1024]{2,1,0:T(4,128)(2,1)S(1)} all-to-all(bf16[32,4,1024]{2,1,0:T(4,128)(2,1)S(1)} %reshape.50), channel_id=1, replica_groups=mesh['frag'=16,'band'=32] {'band'}, dimensions={0} | all-to-all | bytes 524288 | tf_op jit(solution)/shard_map/all_to_all | solution.py:379
  92.3 0.8 reshape.51.stepped_ref
  93.1 2.0 gram.1
  95.1 16.7 %all_to_all.41 = f32[32,4,128]{2,1,0:T(4,128)S(1)} all-to-all(f32[32,4,128]{2,1,0:T(4,128)} %bitcast.16), channel_id=1, replica_groups=mesh['frag'=16,'band'=32] {'band'}, dimensions={0} | all-to-all | bytes 131072 | tf_op jit(solution)/shard_map/all_to_all | solution.py:379
  111.9 16.1 %all_to_all.42 = f32[32,4,128]{2,1,0:T(4,128)} all-to-all(f32[32,4,128]{2,1,0:T(4,128)S(1)} %broadcast_in_dim.10), channel_id=1, replica_groups=mesh['frag'=16,'band'=32] {'band'}, dimensions={0} | all-to-all | bytes 131072 | tf_op jit(solution)/shard_map/all_to_all | solution.py:379
  128.0 3.9 %all-to-all-start.6 = ((bf16[32,8,1024]{2,1,0:T(8,128)(2,1)}), bf16[32,8,1024]{2,1,0:T(8,128)(2,1)S(1)}, u32[]{:S(2)}, u32[]{:S(2)}) async-start(bf16[32,8,1024]{2,1,0:T(8,128)(2,1)} %bitcast.12), calls=%async_computation.6 | async-start | bytes 1048576 | tf_op jit(solution)/shard_map/all_to_all | solution.py:379
  131.9 0.0 copy-done.4
  131.9 0.7 copy.13.place_ref
  132.6 4.7 %newton.1 = (bf16[128,1024]{1,0:T(8,128)(2,1)}, bf16[512,128]{1,0:T(8,128)(2,1)}) custom-call(f32[128,128]{1,0:T(8,128)} %bitcast.15, bf16[128,1024]{1,0:T(8,128)(2,1)} %reshape.51.stepped_ref), custom_call_target="tpu_custom_call" | custom-call | flops 1000000000 | bytes 1048576 | tf_op jit(solution)/shard_map/newton/pallas_call | solution.py:405
  137.3 22.6 %all-to-all-done.6 = bf16[32,8,1024]{2,1,0:T(8,128)(2,1)S(1)} async-done(((bf16[32,8,1024]{2,1,0:T(8,128)(2,1)}), bf16[32,8,1024]{2,1,0:T(8,128)(2,1)S(1)}, u32[]{:S(2)}, u32[]{:S(2)}) %all-to-all-start.6) | async-done | bytes 524320 | tf_op jit(solution)/shard_map/all_to_all | solution.py:379
  159.9 0.0 copy-done.3
  159.9 0.0 copy-start
  159.9 0.7 broadcast_in_dim.22
  160.6 12.6 %all-to-all-start.5 = ((f32[16,2,8,128]{3,2,1,0:T(8,128)}), f32[16,2,8,128]{3,2,1,0:T(8,128)S(1)}, u32[]{:S(2)}, u32[]{:S(2)}) async-start(f32[16,2,8,128]{3,2,1,0:T(8,128)} %broadcast_in_dim.22), calls=%async_computation.5 | async-start | bytes 262144 | tf_op jit(solution)/shard_map/all_to_all | solution.py:379
  173.2 0.0 copy-done
  173.2 0.0 copy-start.2
  173.2 12.9 %density.1 = bf16[16,64,128]{2,1,0:T(8,128)(2,1)} custom-call(s32[16,3]{1,0:T(8,128)} %copy.13.place_ref, s32[1]{0:T(128)} %bitcast.5.own_ref, bf16[256,1024]{1,0:T(8,128)(2,1)} %bitcast.13, bf16[512,128]{1,0:T(8,128)(2,1)} %get-tuple-element.13.inv_ref, bf16[1024,2048]{1,0:T(8,128)(2,1)} %get-tuple-element.9.big_y_ref, bf16[128,512]{1,0:T(8,128)(2,1)} %constant.38.fwd_z_ref), custom_call_target="tpu_custom_call" | custom-call | flops 4000000000 | bytes 6291456 | tf_op jit(solution)/shard_map/density/pallas_call | solution.py:407
  186.1 0.0 all-to-all-done.5.tiles_ref
  186.1 0.0 copy-start.1
  186.1 7.2 %all-to-all-start.7 = ((bf16[16,64,128]{2,1,0:T(8,128)(2,1)}), bf16[16,64,128]{2,1,0:T(8,128)(2,1)S(1)}, u32[]{:S(2)}, u32[]{:S(2)}) async-start(bf16[16,64,128]{2,1,0:T(8,128)(2,1)} %density.1), calls=%async_computation.7 | async-start | bytes 524288 | tf_op jit(solution)/shard_map/all_to_all | solution.py:379
  193.4 0.0 copy-done.2
  193.4 0.8 reshape.54
  194.2 7.9 %all-to-all-done.7 = bf16[16,64,128]{2,1,0:T(8,128)(2,1)S(1)} async-done(((bf16[16,64,128]{2,1,0:T(8,128)(2,1)}), bf16[16,64,128]{2,1,0:T(8,128)(2,1)S(1)}, u32[]{:S(2)}, u32[]{:S(2)}) %all-to-all-start.7) | async-done | bytes 262176 | tf_op jit(solution)/shard_map/all_to_all | solution.py:379
  202.1 3.9 %all-to-all-start.4 = ((bf16[32,4,1024]{2,1,0:T(4,128)(2,1)}), bf16[32,4,1024]{2,1,0:T(4,128)(2,1)S(1)}, u32[]{:S(2)}, u32[]{:S(2)}) async-start(bf16[32,4,1024]{2,1,0:T(4,128)(2,1)} %reshape.54), calls=%async_computation.4 | async-start | bytes 524288 | tf_op jit(solution)/shard_map/all_to_all | solution.py:379
  205.9 0.0 copy-done.1
  206.0 1.9 hartree.1
  207.9 0.8 multiply_add_fusion
  208.7 0.1 reshape.60
  208.8 0.7 reshape.61
  209.5 17.4 %all-to-all-done.4 = bf16[32,4,1024]{2,1,0:T(4,128)(2,1)S(1)} async-done(((bf16[32,4,1024]{2,1,0:T(4,128)(2,1)}), bf16[32,4,1024]{2,1,0:T(4,128)(2,1)S(1)}, u32[]{:S(2)}, u32[]{:S(2)}) %all-to-all-start.4) | async-done | bytes 262176 | tf_op jit(solution)/shard_map/all_to_all | solution.py:379
  226.9 0.9 reshape.64
  (4 shorter events, 0.1 us)
Async XLA Ops:
  2.7 48.3 %all-to-all-start = ((bf16[32,2,4096]{2,1,0:T(2,128)(2,1)}), bf16[32,2,4096]{2,1,0:T(2,128)(2,1)S(1)}, u32[]{:S(2)}, u32[]{:S(2)}) async-start(bf16[32,2,4096]{2,1,0:T(2,128)(2,1)} %broadcast_in_dim.9), calls=%async_computation | async-start | bytes 1048576 | tf_op jit(solution)/shard_map/all_to_all | solution.py:379
  52.0 80.0 %copy-start.4 = (s32[16,3]{0,1:T(4,128)S(1)}, s32[16,3]{0,1:T(4,128)}, u32[]{:S(2)}) copy-start(s32[16,3]{0,1:T(4,128)} %param.13) | copy-start | bytes 580
  66.3 93.6 %copy-start.3 = (f32[2,8,128]{2,1,0:T(8,128)S(1)}, f32[2,8,128]{2,1,0:T(8,128)}, u32[]{:S(2)}) copy-start(f32[2,8,128]{2,1,0:T(8,128)} %param.12) | copy-start | bytes 24580
  128.0 31.9 %all-to-all-start.6 = ((bf16[32,8,1024]{2,1,0:T(8,128)(2,1)}), bf16[32,8,1024]{2,1,0:T(8,128)(2,1)S(1)}, u32[]{:S(2)}, u32[]{:S(2)}) async-start(bf16[32,8,1024]{2,1,0:T(8,128)(2,1)} %bitcast.12), calls=%async_computation.6 | async-start | bytes 1048576 | tf_op jit(solution)/shard_map/all_to_all | solution.py:379
  159.9 13.4 %copy-start = (bf16[32,8,1024]{2,1,0:T(8,128)(2,1)}, bf16[32,8,1024]{2,1,0:T(8,128)(2,1)S(1)}, u32[]{:S(2)}) copy-start(bf16[32,8,1024]{2,1,0:T(8,128)(2,1)S(1)} %all-to-all-done.6) | copy-start | bytes 1572868
  160.6 25.5 %all-to-all-start.5 = ((f32[16,2,8,128]{3,2,1,0:T(8,128)}), f32[16,2,8,128]{3,2,1,0:T(8,128)S(1)}, u32[]{:S(2)}, u32[]{:S(2)}) async-start(f32[16,2,8,128]{3,2,1,0:T(8,128)} %broadcast_in_dim.22), calls=%async_computation.5 | async-start | bytes 262144 | tf_op jit(solution)/shard_map/all_to_all | solution.py:379
  173.2 20.1 %copy-start.2 = (bf16[128,1024]{1,0:T(8,128)(2,1)S(1)}, bf16[128,1024]{1,0:T(8,128)(2,1)}, u32[]{:S(2)}) copy-start(bf16[128,1024]{1,0:T(8,128)(2,1)} %get-tuple-element.11) | copy-start | bytes 786436
  186.1 19.8 %copy-start.1 = (f32[16,2,8,128]{3,2,1,0:T(8,128)}, f32[16,2,8,128]{3,2,1,0:T(8,128)S(1)}, u32[]{:S(2)}) copy-start(f32[16,2,8,128]{3,2,1,0:T(8,128)S(1)} %all-to-all-done.5.tiles_ref) | copy-start | bytes 393220
  186.1 15.9 %all-to-all-start.7 = ((bf16[16,64,128]{2,1,0:T(8,128)(2,1)}), bf16[16,64,128]{2,1,0:T(8,128)(2,1)S(1)}, u32[]{:S(2)}, u32[]{:S(2)}) async-start(bf16[16,64,128]{2,1,0:T(8,128)(2,1)} %density.1), calls=%async_computation.7 | async-start | bytes 524288 | tf_op jit(solution)/shard_map/all_to_all | solution.py:379
  202.1 24.8 %all-to-all-start.4 = ((bf16[32,4,1024]{2,1,0:T(4,128)(2,1)}), bf16[32,4,1024]{2,1,0:T(4,128)(2,1)S(1)}, u32[]{:S(2)}, u32[]{:S(2)}) async-start(bf16[32,4,1024]{2,1,0:T(4,128)(2,1)} %reshape.54), calls=%async_computation.4 | async-start | bytes 524288 | tf_op jit(solution)/shard_map/all_to_all | solution.py:379

commit v2 on v1

--- a/solution.py
+++ b/solution.py
@@ -8,6 +8,7 @@
 from jax.experimental import pallas as pl
 from jax.experimental.pallas import tpu as pltpu
 from jax.sharding import PartitionSpec as P
+
 
 FG = 64
 NB = 128
@@ -40,18 +41,19 @@
     cos_z, sin_z = np.cos(turn_z), np.sin(turn_z)
     same = np.eye(LOCAL)
     fwd_x = np.stack([np.einsum("ab,xk->axbk", same, t) for t in (cos_xy, sin_xy)], axis=2)
-    fwd_x = fwd_x.reshape(LOCAL * FG, 2 * LOCAL * HB)
-    fwd_x_send = (
-        fwd_x.reshape(LOCAL, FG // 2, 2, -1).transpose(1, 2, 0, 3).reshape(LOCAL * FG, -1)
-    )
+    fwd_x = fwd_x.reshape(LOCAL, FG // 4, 2, 2, 2 * LOCAL * HB)
+    fwd_x_send = fwd_x.transpose(1, 2, 3, 0, 4).reshape(LOCAL * FG, -1)
+    fwd_x = fwd_x.transpose(2, 0, 1, 3, 4).reshape(LOCAL * FG, -1)
     back_x = np.stack([np.einsum("ab,xk->akbx", same, t) for t in (cos_xy, -sin_xy)], axis=2)
+    back_x = back_x.reshape(LOCAL * HB, 2, LOCAL, FG // 4, 2, 2).transpose(0, 1, 4, 2, 3, 5)
     back_x = back_x.reshape(LOCAL * HB, 2 * LOCAL * FG)
     fwd_y = np.stack(
         [np.stack([cos_xy.T, sin_xy.T], axis=2), np.stack([-sin_xy.T, cos_xy.T], axis=2)], axis=1
     ).reshape(2 * HB, 2 * FG)
     one_z = np.block([[cos_z, sin_z], [-sin_z, cos_z]])
     fwd_z = np.einsum("ab,kz->akbz", same, one_z).reshape(LOCAL * 2 * QB, LOCAL * 2 * FG)
-    send = np.einsum("ab,kl->kabl", same, np.eye(HB)).reshape(LOCAL * HB, LOCAL * HB)
+    send = np.einsum("gh,ab,kl->kgahbl", np.eye(2), same, np.eye(HB))
+    send = send.reshape(2 * LOCAL * HB, 2 * LOCAL * HB)
     return tuple(
         jnp.asarray(t, dtype=F32).astype(BF16)
         for t in (fwd_x, fwd_x_send, back_x, fwd_y, fwd_z, send)
@@ -114,57 +116,109 @@
 
 
 def step_kernel(
-    after_y_ref, pot_ref, bands_ref, big_y_ref, fwd_z_ref, back_x_ref, fwd_x_ref, send_ref,
-    stepped_ref, image_ref, back_ref, stack_ref, stack2_ref,
+    place_ref, after_y_ref, near_ref, far_ref, bands_ref, big_y_ref, fwd_z_ref, back_x_ref, send_ref,
+    stepped_ref, sent_ref, back_ref, stack_ref, pots_ref,
 ):
     fwd_z = fwd_z_ref[...]
+    near = place_ref[0]
+    quarter = FG * FG // 4
+    pick_shape = (FG // 2, 2 * FG)
+    for at in range(4):
+        pick = (iota(pick_shape, 0) * 4 + at == iota(pick_shape, 1)).astype(F32).astype(BF16)
+        span = slice(at * quarter, (at + 1) * quarter)
+        pots_ref[near, :, span] = dot(pick, near_ref[...])
+        pots_ref[1 - near, :, span] = dot(pick, far_ref[...])
 
     @pl.loop(0, FG // LOCAL)
     def _(at):
         span = pl.ds(pl.multiple_of(at * LANES, LANES), LANES)
         grid_vals = dot(after_y_ref[:, span], fwd_z) * (4.0 / FG**1.5)
-        pot = pot_ref[:, pl.ds(pl.multiple_of(at * 2 * LANES, 2 * LANES), 2 * LANES)].astype(F32)
-        pots = jnp.concatenate(
-            [*spread_parts(pot[:, :LANES]), *spread_parts(pot[:, LANES:])], axis=1
-        )
-        pots = jnp.concatenate([pots] * LOCAL, axis=0)
-        weighted = (grid_vals * pots).astype(BF16)
+        wide = pl.ds(pl.multiple_of(at * 2 * LANES, 2 * LANES), 2 * LANES)
+        pots = []
+        for half in (0, 1):
+            pot = pots_ref[half, :, wide]
+            parts = [*spread_parts(pot[:, :LANES]), *spread_parts(pot[:, LANES:])]
+            pots += [jnp.concatenate(parts, axis=1)] * LOCAL
+        weighted = (grid_vals * jnp.concatenate(pots, axis=0)).astype(BF16)
         back_ref[:, span] = dot_t(weighted, fwd_z).astype(BF16)
 
     rows_n = LOCAL * FG
-
-    @pl.loop(0, HB * 2 * QB // LANES)
+    half_n = LOCAL * HB
+    block_n = 2 * LANES
+
+    @pl.loop(0, HB * 2 * QB // block_n)
     def _(at):
-        span = pl.ds(pl.multiple_of(at * LANES, LANES), LANES)
+        start = pl.multiple_of(at * block_n, block_n)
+        span = pl.ds(start, block_n)
         block = dot_t(back_ref[...], big_y_ref[span, :])
-        stack_ref[:rows_n, span] = block.astype(BF16)
-        stack_ref[rows_n:, span] = times_i(block).astype(BF16)
-
-    half_n = LOCAL * HB
-    for start in range(0, HB * 2 * QB, LANES):
-        image = dot(back_x_ref[...], stack_ref[:, start : start + LANES]) * (0.25 / FG**1.5)
-        shape = (half_n, LANES)
+        stack_ref[:rows_n, :] = block.astype(BF16)
+        for low in (0, LANES):
+            turned = times_i(block[:, low : low + LANES])
+            stack_ref[rows_n:, low : low + LANES] = turned.astype(BF16)
+        image = dot(back_x_ref[...], stack_ref[...]) * (0.25 / FG**1.5)
+        shape = (half_n, block_n)
         row, lane = iota(shape, 0), iota(shape, 1) + start
         mx, my = row % HB - HB // 2, lane // (2 * QB) - HB // 2
         mz = lane % QB - QB // 2
         kinetic = (mx * mx + my * my + mz * mz).astype(F32) * (16.0 / FG**2)
-        wide = bands_ref[:, start : start + LANES].astype(F32)
-        stepped = (wide - STEP_TAU * (kinetic * wide + image)).astype(BF16)
-        stack2_ref[:half_n, start : start + LANES] = stepped
-        stack2_ref[half_n:, start : start + LANES] = times_i(stepped.astype(F32)).astype(BF16)
-    stepped_ref[...] = dot(send_ref[...], stack2_ref[:half_n, :]).astype(BF16)
-    image_ref[...] = dot(fwd_x_ref[...], stack2_ref[...]).astype(BF16)
-
-
-def gram_kernel(stepped_ref, out_ref, conj_ref):
+        bands = bands_ref[:, span].astype(F32)
+        stepped_ref[:, span] = (bands - STEP_TAU * (kinetic * bands + image)).astype(BF16)
+
+    half_w = HB * QB
+    halves_of = jnp.concatenate([stepped_ref[:, :half_w], stepped_ref[:, half_w:]], axis=0)
+    sent_ref[...] = dot(send_ref[...], halves_of).astype(BF16)
+
+
+def image_kernel(stepped_ref, fwd_x_ref, image_ref, stack_ref):
+    half_n = LOCAL * HB
+    stack_ref[:half_n, :] = stepped_ref[...]
     for start in range(0, HB * 2 * QB, LANES):
         block = stepped_ref[:, start : start + LANES].astype(F32)
-        conj_ref[:, start : start + LANES] = (-times_i(block)).astype(BF16)
+        stack_ref[half_n:, start : start + LANES] = times_i(block).astype(BF16)
+    image_ref[...] = dot(fwd_x_ref[...], stack_ref[...]).astype(BF16)
+
+
+def onehot(matches):
+    return matches.astype(F32).astype(BF16)
+
+
+def gram_kernel(received_ref, image_ref, out_ref, stepped_ref, conj_ref):
+    coefs = HB * 2 * QB
+    half_w = coefs // 2
+    shape = (NB, 2 * NB)
+    row, col = iota(shape, 0), iota(shape, 1)
+    at = row // LOCAL * 2 * LOCAL + row % LOCAL
+    for half in (0, 1):
+        pick = onehot(col == at + half * LOCAL)
+        rows = dot(pick, received_ref[...])
+        stepped_ref[:, half * half_w : (half + 1) * half_w] = rows.astype(BF16)
+        for start in range(0, half_w, LANES):
+            block = -times_i(rows[:, start : start + LANES])
+            conj_ref[:, half * half_w + start : half * half_w + start + LANES] = block.astype(BF16)
     stepped = stepped_ref[...]
     gram_re = dot_t(stepped, stepped)
     gram_im = dot_t(stepped, conj_ref[...])
     shape = (NB, NB)
-    out_ref[...] = jnp.where(iota(shape, 0) >= iota(shape, 1), gram_re, gram_im) * (1.0 / COEF)
+    gram = jnp.where(iota(shape, 0) >= iota(shape, 1), gram_re, gram_im) * (1.0 / COEF)
+    first, _ = halves(gram)
+    second = (gram - first.astype(F32)).astype(BF16)
+    third = (gram - first.astype(F32) - second.astype(F32)).astype(BF16)
+    shape = (2 * NB, NB)
+    row, col = iota(shape, 0), iota(shape, 1)
+    at = col // LOCAL * 2 * LOCAL + col % LOCAL
+    upper, lower = onehot(row == at), onehot(row == at + LOCAL)
+    out_ref[:, :coefs] = image_ref[...]
+    out_ref[:, coefs : coefs + NB] = (dot(upper, first) + dot(lower, second)).astype(BF16)
+    out_ref[:, coefs + NB :] = dot(upper, third).astype(BF16)
+
+
+def sum_kernel(parts_ref, out_ref):
+    parts = parts_ref[...].astype(F32).reshape(HB, 2 * LOCAL, 2 * NB).sum(axis=0)
+    swapped = pltpu.roll(parts, LOCAL, 0)
+    whole = (parts + swapped)[:, :NB]
+    third = parts[:, NB:] + swapped[:, NB:]
+    whole = whole + third
+    out_ref[...] = jnp.broadcast_to(whole[None], (NB // 8, 8, NB)).reshape(NB, NB)
 
 
 def complex_mul(left, right):
@@ -211,8 +265,8 @@
 
 
 def density_kernel(
-    place_ref, own_ref, image_ref, inv_ref, big_y_ref, fwd_z_ref,
-    out_ref, stack_ref, phi_ref, after_y_ref, dens_ref, wide_ref,
+    place_ref, own_ref, image_ref, inv_ref, big_y_ref, fwd_z_ref, tile_ref,
+    out_ref, stack_ref, phi_ref, after_y_ref, dens_ref,
 ):
     rows_n = 2 * NB
     shape = (NB, 2 * rows_n)
@@ -220,7 +274,7 @@
     inner = col % rows_n
     picks = (inner // 8 * LOCAL + inner % LOCAL == row) & (inner // LOCAL % 2 == col // rows_n)
     spread = dot(inv_ref[...], picks.astype(F32).astype(BF16)).astype(BF16)
-    stack_ref[:rows_n, :] = image_ref[...]
+    stack_ref[:rows_n, :] = image_ref[:, : HB * 2 * QB]
     for start in range(0, HB * 2 * QB, LANES):
         block = image_ref[:, start : start + LANES].astype(F32)
         stack_ref[rows_n:, start : start + LANES] = times_i(block).astype(BF16)
@@ -278,30 +332,35 @@
         cols = same_plane & ((col % FG + shift_z) % GZ == row % FG)
         moved = dot(dens, cols.astype(F32).astype(BF16)).astype(BF16)
         rows = (rows_row + shift_y) % GY == rows_col
-        out_ref[to] = dot(rows.astype(F32).astype(BF16), moved).astype(BF16)
-
-
-def hartree_kernel(place_ref, own_ref, tiles_ref, out_ref):
+        out_ref[to, :FG, :] = dot(rows.astype(F32).astype(BF16), moved).astype(BF16)
+        for at, part in enumerate(halves(tile_ref[...].reshape(2 * 8, GZ))):
+            out_ref[to, FG + at * 16 : FG + (at + 1) * 16, :] = part
+
+
+def last_kernel(place_ref, own_ref, pieces_ref, out_ref, total_ref):
     own = own_ref[0]
     own_y, own_z = place_ref[own, 1], place_ref[own, 2]
-    rows = (iota((FG, GY), 0) + own_y) % GY == iota((FG, GY), 1)
-    rows = rows.astype(F32).astype(BF16)
+    patched = jnp.zeros((FG, LANES), F32)
+    for at in range(FRAGS):
+        patched += pieces_ref[at, :FG, :].astype(F32)
+    rows = onehot((iota((FG, GY), 0) + own_y) % GY == iota((FG, GY), 1))
     shape = (GZ, LANES)
     row, col = iota(shape, 0), iota(shape, 1)
     total = jnp.zeros((FG, LANES), F32)
+    tiles = pieces_ref[:, FG:, :].astype(F32)
     for plane in (0, 1):
-        cols = (col // FG == plane) & ((col % FG + own_z) % GZ == row)
-        cols = cols.astype(F32).astype(BF16)
-        rest = tiles_ref[:, plane].reshape(GY, GZ)
-        for _ in range(3):
-            part = rest.astype(BF16)
-            total += dot(dot(rows, part).astype(BF16), cols)
-            rest = rest - part.astype(F32)
-    out_ref[...] = total
-
-
-def xc_potential(values):
-    return -SLATER * values / jnp.power(values * values + SOFTEN, 1.0 / 3.0)
+        cols = onehot((col // FG == plane) & ((col % FG + own_z) % GZ == row))
+        for part in (0, 1):
+            start = part * 16 + plane * 8
+            tile = tiles[:, start : start + 8, :].reshape(GY, GZ).astype(BF16)
+            total += dot(dot(rows, tile).astype(BF16), cols)
+    power = jnp.exp(jnp.log(patched * patched + SOFTEN) * (-1.0 / 3.0))
+    total_ref[...] = total - SLATER * patched * power
+    even = total_ref[pl.ds(0, FG // 2, stride=2), :]
+    odd = total_ref[pl.ds(1, FG // 2, stride=2), :]
+    low = iota(even.shape, 1) < FG
+    out_ref[0] = jnp.where(low, even, pltpu.roll(odd, FG, 1))
+    out_ref[1] = jnp.where(low, pltpu.roll(even, FG, 1), odd)
 
 
 VM = pl.BlockSpec(memory_space=pltpu.VMEM)
@@ -312,7 +371,7 @@
     return jax.ShapeDtypeStruct(shape, dtype)
 
 
-def call(kernel, outs, in_specs, scratch, flops, moved, name):
+def call(kernel, outs, in_specs, scratch, flops, moved):
     return pl.pallas_call(
         kernel,
         out_shape=outs,
@@ -320,7 +379,6 @@
         out_specs=jax.tree.map(lambda _: VM, outs),
         scratch_shapes=[pltpu.VMEM(s, d) for s, d in scratch],
         cost_estimate=pl.CostEstimate(flops=flops, bytes_accessed=moved, transcendentals=0),
-        name=name,
     )
 
 
@@ -333,81 +391,98 @@
         (sds((coefs, width), BF16), sds((LOCAL * FG, width), BF16)),
         [VM] * 3,
         [((2 * HB, width), F32), ((2 * LOCAL * HB, coefs), BF16)],
-        2 * 10**9, 6 * mega, "forward",
+        2 * 10**9, 6 * mega,
     )
     step = call(
         step_kernel,
-        (sds((LOCAL * HB, coefs), BF16), sds((LOCAL * FG, coefs), BF16)),
-        [VM] * 8,
+        (sds((LOCAL * HB, coefs), BF16), sds((2 * NB, coefs // 2), BF16)),
+        [SM] + [VM] * 8,
         [
             ((LOCAL * FG, width), BF16),
-            ((2 * LOCAL * FG, coefs), BF16),
-            ((2 * LOCAL * HB, coefs), BF16),
+            ((2 * LOCAL * FG, 2 * LANES), BF16),
+            ((2, FG // 2, FG * FG), F32),
         ],
-        4 * 10**9, 8 * mega, "step",
+        4 * 10**9, 8 * mega,
+    )
+    image = call(
+        image_kernel, sds((LOCAL * FG, coefs), BF16), [VM] * 2, [((2 * LOCAL * HB, coefs), BF16)],
+        10**8, mega,
     )
     gram = call(
-        gram_kernel, sds((NB, NB), F32), [VM], [((NB, coefs), BF16)], 10**8, mega // 2, "gram"
+        gram_kernel,
+        (sds((2 * NB, coefs + 2 * NB), BF16), sds((NB, coefs), BF16)),
+        [VM] * 2, [((NB, coefs), BF16)], 2 * 10**8, 2 * mega,
+    )
+    total = pl.pallas_call(
+        sum_kernel,
+        grid=(1,),
+        out_shape=sds((NB, NB), F32),
+        in_specs=[pl.BlockSpec((2 * NB, 2 * NB), lambda i: (0, coefs // (2 * NB)))],
+        out_specs=pl.BlockSpec((NB, NB), lambda i: (0, 0)),
+        name="total",
     )
     newton = call(
         newton_kernel,
         (sds((NB, coefs), BF16), sds((4 * NB, NB), BF16)),
         [VM] * 2,
         [((2 * NB, coefs), BF16)],
-        10**9, mega, "newton",
+        10**9, mega,
     )
     density = call(
         density_kernel,
-        sds((FRAGS, FG, LANES), BF16),
-        [SM, SM] + [VM] * 4,
+        sds((FRAGS, FG + 32, LANES), BF16),
+        [SM, SM] + [VM] * 5,
         [
             ((4 * NB, coefs), BF16),
             ((2 * NB, coefs), BF16),
             ((2 * NB, width), BF16),
             ((FG, LANES), F32),
-            ((8, LANES), F32),
         ],
-        4 * 10**9, 6 * mega, "density",
-    )
-    hartree = call(
-        hartree_kernel, sds((FG, LANES), F32), [SM, SM, VM], [], 10**7, mega // 4, "hartree"
-    )
-    return forward, step, gram, newton, density, hartree
-
-
-def exchange(values, axis):
-    return lax.all_to_all(values, axis, split_axis=0, concat_axis=0, tiled=True)
+        4 * 10**9, 6 * mega,
+    )
+    last = call(
+        last_kernel, sds((2, FG // 2, LANES), F32), [SM, SM, VM], [((FG, LANES), F32)],
+        10**7, mega // 2,
+    )
+    return forward, step, image, gram, total, newton, density, last
+
+
+def exchange(values, axis, groups=None):
+    return lax.all_to_all(
+        values, axis, split_axis=0, concat_axis=0, tiled=True, axis_index_groups=groups
+    )
 
 
 def per_device(bands_in, potential_in, hartree, patch_list):
     fwd_x, fwd_x_send, back_x, fwd_y, fwd_z, send = dft_tables()
-    forward, step, gram, newton, density, hartree_window = stages()
+    forward, step, image, gram, total, newton, density, last = stages()
     coefs = HB * 2 * QB
     groups = lax.axis_size("band")
+    chips = groups // 2
     planes = FG // groups
     own = lax.axis_index("frag").astype(jnp.int32).reshape(1)
-
-    pot_send = jnp.broadcast_to(potential_in.astype(BF16), (groups, planes, FG * FG))
-    pot = exchange(pot_send, "band").reshape(FG, FG * FG)
-    tiles = exchange(jnp.broadcast_to(hartree[None], (FRAGS, *hartree.shape)), "frag")
+    near = (lax.axis_index("band") % 2).astype(jnp.int32).reshape(1)
+
+    pot = potential_in.astype(BF16).reshape(1, planes * 4, FG * FG // 4)
+    along = [[2 * z + x for z in range(chips)] for x in (0, 1)]
+    pot_near = exchange(jnp.broadcast_to(pot, (chips, *pot.shape[1:])), "band", along)
+    pot_near = pot_near.reshape(2 * FG, FG * FG // 4)
+    pot_far = lax.ppermute(pot_near, "band", [(i, i ^ 1) for i in range(groups)])
     bands = bands_in.reshape(LOCAL * HB, coefs)
     big_y, after_y = forward(bands, fwd_x, fwd_y)
-    stepped_send, image_send = step(
-        after_y, pot, bands, big_y, fwd_z, back_x, fwd_x_send, send
-    )
-    stepped = exchange(stepped_send.reshape(groups, LOCAL, coefs), "band").reshape(NB, coefs)
-    image = exchange(image_send.reshape(groups, planes * LOCAL, coefs), "band")
-    image = image.reshape(2 * NB, coefs)
-    window = hartree_window(patch_list, own, tiles)
-    part = gram(stepped)
-    rows = exchange(part.reshape(groups, LOCAL, NB), "band").sum(axis=0)
-    whole = exchange(jnp.broadcast_to(rows[None], (groups, LOCAL, NB)), "band").reshape(NB, NB)
+    stepped_own, stepped_send = step(
+        near, after_y, pot_near, pot_far, bands, big_y, fwd_z, back_x, send
+    )
+    received = exchange(stepped_send.reshape(groups, 2 * LOCAL, coefs // 2), "band")
+    image_send = image(stepped_own, fwd_x_send)
+    parts, stepped = gram(received.reshape(2 * NB, coefs // 2), image_send)
+    parts = exchange(parts.reshape(groups, planes * LOCAL, -1), "band").reshape(2 * NB, -1)
+    whole = exchange(total(parts).reshape(groups, LOCAL, NB), "band").reshape(NB, NB)
     phi, inverse = newton(whole, stepped)
     phi_local = exchange(phi.reshape(groups, LOCAL, coefs), "band")
-    pieces = exchange(density(patch_list, own, image, inverse, big_y, fwd_z), "frag")
-    patched = pieces.astype(F32).sum(axis=0)
-    total = window + xc_potential(patched)
-    back = total.reshape(FG, planes, FG).transpose(1, 0, 2).reshape(1, planes, FG * FG)
+    pieces = density(patch_list, own, parts, inverse, big_y, fwd_z, hartree)
+    pieces, phi_local = lax.optimization_barrier((pieces, phi_local))
+    back = last(patch_list, own, exchange(pieces, "frag")).reshape(1, planes, FG * FG)
     bands_out = phi_local.transpose(1, 0, 2).astype(F32).reshape(1, LOCAL, HB * coefs)
     return (bands_out, back)
 
@@ -415,6 +490,7 @@
 def solution(mesh):
     in_specs = (P("frag", "band", None), P("frag", "band", None), P("band", "frag", None), P())
     out_specs = (P("frag", "band", None), P("frag", "band", None))
+
     return jax.shard_map(
         per_device, mesh=mesh, in_specs=in_specs, out_specs=out_specs, check_vma=False
     )

time: 229 us -> 205 us (0.90)
  waiting for transfers between devices: 70.8 us -> 30.5 us
  blocking collectives: 57.8 us -> 87.9 us
  starting transfers between devices: 44.6 us -> 29.9 us
  Pallas kernels: 42.3 us -> 45.9 us
    all_to_all x5 -> x3, waiting for transfers between devices: 70.8 us -> 30.5 us  [exchange(): lax.all_to_all(values, axis, split_axis=0, concat_axis=0, tiled=True, axi...]
    all_to_all x3, blocking collectives: 57.8 us -> 87.9 us  [exchange(): lax.all_to_all(values, axis, split_axis=0, concat_axis=0, tiled=True, axi...]
    all_to_all x5 -> x3, starting transfers between devices: 44.6 us -> 26.8 us  [exchange(): lax.all_to_all(values, axis, split_axis=0, concat_axis=0, tiled=True, axi...]
    pallas_call x4 -> x6, Pallas kernels: 31.1 us -> 34.7 us  [the longest x1 13 us: per_device(): pieces = density(patch_list, own, parts, inverse, big_y, fwd_z, hartree)]
    ppermute x0 -> x1, starting transfers between devices: none -> 3.11 us  [per_device(): lax.ppermute(pot_near, 'band', [(i, i ^ 1) for i in range(groups)])]
  transfers between devices with their start and end apart: 5 -> 4, of which waited for: 4 -> 3; matrix products, arithmetic and copies ran while one was open for 2% -> 2% of each run, Pallas kernels for 11% -> 11%
where the time goes in v2:
time: 205 us; the launch traced here: 204 us
  blocking collectives  87.9 us (43%)
  Pallas kernels  45.9 us (22%)
  waiting for transfers between devices  30.5 us (15%)
  starting transfers between devices  29.9 us (15%)
  local copies, waits for them, and re-layouts  7.87 us (4%)
    all_to_all x3, blocking collectives, exchange(): lax.all_to_all(values, axis, split_axis=0, concat_axis=0, tiled=True, axi...  87.9 us
    all_to_all x3, waiting for transfers between devices, exchange(): lax.all_to_all(values, axis, split_axis=0, concat_axis=0, tiled=True, axi...  30.5 us
    all_to_all x3, starting transfers between devices, exchange(): lax.all_to_all(values, axis, split_axis=0, concat_axis=0, tiled=True, axi...  26.8 us
    pallas_call x1, Pallas kernels, per_device(): pieces = density(patch_list, own, parts, inverse, big_y, fwd_z, hartree)  13 us
    pallas_call x1, Pallas kernels, per_device(): step(near, after_y, pot_near, pot_far, bands, big_y, fwd_z, back_x, send)  13 us
    pallas_call x1, Pallas kernels, per_device(): big_y, after_y = forward(bands, fwd_x, fwd_y)  6.48 us
    pallas_call x1, Pallas kernels, per_device(): phi, inverse = newton(whole, stepped)  4.7 us
  transfers between devices with their start and end apart: 4, of which 3 were waited for; matrix products, arithmetic and copies ran while one was open for 2% of the time, Pallas kernels for 11%

profile of v2, /device:TPU:1, one launch (start us, length us, event | category | flops | bytes accessed | tf_op | source)
XLA Modules:
  0.0 204.5 jit_solution(8252190196247695194)
XLA Ops:
  0.6 0.8 convert_element_type.27
  1.4 29.3 %all_to_all.30 = bf16[16,8,1024]{2,1,0:T(8,128)(2,1)S(1)} all-to-all(bf16[16,8,1024]{2,1,0:T(8,128)(2,1)S(1)} %broadcast_in_dim.8), channel_id=1, replica_groups={{0,2,4,6,8,10,12,14,16,18,20,22,24,26,28,30},{1,3,5,7,9,11,13,15,17,19,..., dimensions={0} | all-to-all | bytes 524288 | tf_op jit(solution)/shard_map/all_to_all | solution.py:451
  30.8 0.0 copy-start.2
  30.8 3.1 %collective-permute-start = (bf16[128,1024]{1,0:T(8,128)(2,1)S(1)}, bf16[128,1024]{1,0:T(8,128)(2,1)S(1)}, u32[]{:S(2)}, u32[]{:S(2)}) collective-permute-start(bf16[128,1024]{1,0:T(8,128)(2,1)S(1)} %bitcast.17), channel_id=1, source_target_pairs={{0,1},{1,0},{2,3},{3,2},{4,5},{5,4},{6,7},{7,6},{8,9},{9,8},{10,11... | collective-permute-start | bytes 786440 | tf_op jit(solution)/shard_map/ppermute | solution.py:470
  33.9 1.8 reshape.50.bands_ref
  35.7 6.5 %shard_map.113 = (bf16[1024,2048]{1,0:T(8,128)(2,1)}, bf16[256,2048]{1,0:T(8,128)(2,1)}) custom-call(bf16[128,1024]{1,0:T(8,128)(2,1)} %reshape.50.bands_ref, bf16[256,256]{1,0:T(8,128)(2,1)} %constant.43.fwd_x_ref, bf16[64,128]{1,0:T(8,128)(2,1)} %constant.44.fwd_y_ref), custom_call_target="tpu_custom_call" | custom-call | flops 2000000000 | bytes 6291456 | tf_op jit(solution)/shard_map/pallas_call | solution.py:472
  42.2 0.0 collective-permute-done.far_ref
  42.2 0.0 copy-start.4
  42.2 0.0 copy-done.2
  42.2 0.7 copy-done.4
  42.9 13.0 %shard_map.114 = (bf16[128,1024]{1,0:T(8,128)(2,1)}, bf16[256,512]{1,0:T(8,128)(2,1)}) custom-call(s32[1]{0:T(128)} %bitcast.1.place_ref, bf16[256,2048]{1,0:T(8,128)(2,1)} %get-tuple-element.12.after_y_ref, bf16[128,1024]{1,0:T(8,128)(2,1)} %bitcast.18, bf16[128,1024]{1,0:T(8,128)(2,1)} %copy-done.4, bf16[128,1024]{1,0:T(8,128)(2,1)} %reshape.50.bands_ref, ...), custom_call_target="tpu_custom_call" | custom-call | flops 4000000000 | bytes 8388608 | tf_op jit(solution)/shard_map/pallas_call | solution.py:473
  55.9 10.6 %all-to-all-start.1 = ((bf16[32,8,512]{2,1,0:T(8,128)(2,1)}), bf16[32,8,512]{2,1,0:T(8,128)(2,1)S(1)}, u32[]{:S(2)}, u32[]{:S(2)}) async-start(bf16[32,8,512]{2,1,0:T(8,128)(2,1)} %bitcast.19), calls=%async_computation.1 | async-start | bytes 524288 | tf_op jit(solution)/shard_map/all_to_all | solution.py:451
  66.5 0.0 copy-start.3
  66.5 2.2 %shard_map.115.image_ref = bf16[256,1024]{1,0:T(8,128)(2,1)} custom-call(bf16[128,1024]{1,0:T(8,128)(2,1)} %get-tuple-element.15.stepped_ref, bf16[256,256]{1,0:T(8,128)(2,1)} %constant.48.fwd_x_ref), custom_call_target="tpu_custom_call" | custom-call | flops 100000000 | bytes 1048576 | tf_op jit(solution)/shard_map/pallas_call | solution.py:477
  68.7 17.8 %all-to-all-done.1 = bf16[32,8,512]{2,1,0:T(8,128)(2,1)S(1)} async-done(((bf16[32,8,512]{2,1,0:T(8,128)(2,1)}), bf16[32,8,512]{2,1,0:T(8,128)(2,1)S(1)}, u32[]{:S(2)}, u32[]{:S(2)}) %all-to-all-start.1) | async-done | bytes 262176 | tf_op jit(solution)/shard_map/all_to_all | solution.py:451
  86.6 0.0 copy-start.1
  86.6 0.7 copy-done.1
  87.3 2.9 %shard_map.116 = (bf16[256,1280]{1,0:T(8,128)(2,1)}, bf16[128,1024]{1,0:T(8,128)(2,1)}) custom-call(bf16[256,512]{1,0:T(8,128)(2,1)} %bitcast.14, bf16[256,1024]{1,0:T(8,128)(2,1)} %shard_map.115.image_ref), custom_call_target="tpu_custom_call" | custom-call | flops 200000000 | bytes 2097152 | tf_op jit(solution)/shard_map/pallas_call | solution.py:478
  90.2 40.4 %all_to_all.31 = bf16[32,8,1280]{2,1,0:T(8,128)(2,1)} all-to-all(bf16[32,8,1280]{2,1,0:T(8,128)(2,1)} %bitcast.15), channel_id=1, replica_groups=mesh['frag'=16,'band'=32] {'band'}, dimensions={0} | all-to-all | bytes 1310720 | tf_op jit(solution)/shard_map/all_to_all | solution.py:451
  130.6 1.6 total.1
  132.1 18.3 %all_to_all.32 = f32[32,4,128]{2,1,0:T(4,128)} all-to-all(f32[32,4,128]{2,1,0:T(4,128)} %bitcast.20), channel_id=1, replica_groups=mesh['frag'=16,'band'=32] {'band'}, dimensions={0} | all-to-all | bytes 131072 | tf_op jit(solution)/shard_map/all_to_all | solution.py:451
  150.4 4.7 %shard_map.117 = (bf16[128,1024]{1,0:T(8,128)(2,1)}, bf16[512,128]{1,0:T(8,128)(2,1)}) custom-call(f32[128,128]{1,0:T(8,128)} %bitcast.21, bf16[128,1024]{1,0:T(8,128)(2,1)} %get-tuple-element.17.stepped_ref), custom_call_target="tpu_custom_call" | custom-call | flops 1000000000 | bytes 1048576 | tf_op jit(solution)/shard_map/pallas_call | solution.py:481
  155.1 1.8 reshape.58
  156.9 3.9 %all-to-all-start.4 = ((bf16[32,4,1024]{2,1,0:T(4,128)(2,1)}), bf16[32,4,1024]{2,1,0:T(4,128)(2,1)S(1)}, u32[]{:S(2)}, u32[]{:S(2)}) async-start(bf16[32,4,1024]{2,1,0:T(4,128)(2,1)} %reshape.58), calls=%async_computation.4 | async-start | bytes 524288 | tf_op jit(solution)/shard_map/all_to_all | solution.py:451
  160.7 0.0 copy-done.3
  160.8 0.7 copy.12.place_ref
  161.4 13.0 %shard_map.118 = bf16[16,96,128]{2,1,0:T(8,128)(2,1)} custom-call(s32[16,3]{1,0:T(8,128)} %copy.12.place_ref, s32[1]{0:T(128)} %bitcast.own_ref, bf16[256,1280]{1,0:T(8,128)(2,1)} %bitcast.13, bf16[512,128]{1,0:T(8,128)(2,1)} %get-tuple-element.18.inv_ref, bf16[1024,2048]{1,0:T(8,128)(2,1)} %get-tuple-element.13.big_y_ref, ...), custom_call_target="tpu_custom_call" | custom-call | flops 4000000000 | bytes 6291456 | tf_op jit(solution)/shard_map/pallas_call | solution.py:483
  174.4 3.8 %all-to-all-done.4 = bf16[32,4,1024]{2,1,0:T(4,128)(2,1)S(1)} async-done(((bf16[32,4,1024]{2,1,0:T(4,128)(2,1)}), bf16[32,4,1024]{2,1,0:T(4,128)(2,1)S(1)}, u32[]{:S(2)}, u32[]{:S(2)}) %all-to-all-start.4) | async-done | bytes 262176 | tf_op jit(solution)/shard_map/all_to_all | solution.py:451
  178.2 12.3 %all-to-all-start.5 = ((bf16[16,96,128]{2,1,0:T(8,128)(2,1)}), bf16[16,96,128]{2,1,0:T(8,128)(2,1)S(1)}, u32[]{:S(2)}, u32[]{:S(2)}) async-start(bf16[16,96,128]{2,1,0:T(8,128)(2,1)} %shard_map.118), calls=%async_computation.5 | async-start | bytes 786432 | tf_op jit(solution)/shard_map/all_to_all | solution.py:451
  190.6 0.9 reshape.64
  191.4 8.9 %all-to-all-done.5.pieces_ref = bf16[16,96,128]{2,1,0:T(8,128)(2,1)S(1)} async-done(((bf16[16,96,128]{2,1,0:T(8,128)(2,1)}), bf16[16,96,128]{2,1,0:T(8,128)(2,1)S(1)}, u32[]{:S(2)}, u32[]{:S(2)}) %all-to-all-start.5) | async-done | bytes 393248 | tf_op jit(solution)/shard_map/all_to_all | solution.py:451
  200.3 0.0 copy-start
  200.3 0.7 copy-done
  201.1 2.0 shard_map.119
  203.1 1.4 reshape.61
  (2 shorter events, 0.0 us)
Async XLA Ops:
  30.8 11.5 %copy-start.2 = (bf16[16,8,1024]{2,1,0:T(8,128)(2,1)}, bf16[16,8,1024]{2,1,0:T(8,128)(2,1)S(1)}, u32[]{:S(2)}) copy-start(bf16[16,8,1024]{2,1,0:T(8,128)(2,1)S(1)} %all_to_all.30) | copy-start | bytes 786436
  30.8 11.4 %collective-permute-start = (bf16[128,1024]{1,0:T(8,128)(2,1)S(1)}, bf16[128,1024]{1,0:T(8,128)(2,1)S(1)}, u32[]{:S(2)}, u32[]{:S(2)}) collective-permute-start(bf16[128,1024]{1,0:T(8,128)(2,1)S(1)} %bitcast.17), channel_id=1, source_target_pairs={{0,1},{1,0},{2,3},{3,2},{4,5},{5,4},{6,7},{7,6},{8,9},{9,8},{10,11... | collective-permute-start | bytes 786440 | tf_op jit(solution)/shard_map/ppermute | solution.py:470
  42.2 0.7 copy-start.4
  55.9 30.7 %all-to-all-start.1 = ((bf16[32,8,512]{2,1,0:T(8,128)(2,1)}), bf16[32,8,512]{2,1,0:T(8,128)(2,1)S(1)}, u32[]{:S(2)}, u32[]{:S(2)}) async-start(bf16[32,8,512]{2,1,0:T(8,128)(2,1)} %bitcast.19), calls=%async_computation.1 | async-start | bytes 524288 | tf_op jit(solution)/shard_map/all_to_all | solution.py:451
  66.5 94.2 %copy-start.3 = (s32[16,3]{0,1:T(4,128)S(1)}, s32[16,3]{0,1:T(4,128)}, u32[]{:S(2)}) copy-start(s32[16,3]{0,1:T(4,128)} %param.13) | copy-start | bytes 580
  86.6 0.7 copy-start.1
  156.9 21.4 %all-to-all-start.4 = ((bf16[32,4,1024]{2,1,0:T(4,128)(2,1)}), bf16[32,4,1024]{2,1,0:T(4,128)(2,1)S(1)}, u32[]{:S(2)}, u32[]{:S(2)}) async-start(bf16[32,4,1024]{2,1,0:T(4,128)(2,1)} %reshape.58), calls=%async_computation.4 | async-start | bytes 524288 | tf_op jit(solution)/shard_map/all_to_all | solution.py:451
  178.2 22.1 %all-to-all-start.5 = ((bf16[16,96,128]{2,1,0:T(8,128)(2,1)}), bf16[16,96,128]{2,1,0:T(8,128)(2,1)S(1)}, u32[]{:S(2)}, u32[]{:S(2)}) async-start(bf16[16,96,128]{2,1,0:T(8,128)(2,1)} %shard_map.118), calls=%async_computation.5 | async-start | bytes 786432 | tf_op jit(solution)/shard_map/all_to_all | solution.py:451
  200.3 0.7 copy-start

commit v3 on v2

--- a/solution.py
+++ b/solution.py
@@ -72,6 +72,10 @@
     return lax.dot_general(left, right, (((1,), (1,)), ((), ())), preferred_element_type=F32)
 
 
+def onehot(matches):
+    return matches.astype(F32).astype(BF16)
+
+
 def times_i(block):
     first = iota(block.shape, 1) % (2 * QB) < QB
     ahead = pltpu.roll(block, LANES - QB, 1)
@@ -90,7 +94,7 @@
     rows_ref[...] = dot(fwd_y_ref[...], spread)
     same = iota((QB, width), 1) % QB == iota((QB, width), 0)
 
-    @pl.loop(0, 2 * HB)
+    @pl.loop(0, 2 * HB, unroll=8)
     def _(row):
         line = jnp.broadcast_to(rows_ref[pl.ds(row, 1), :], (QB, width))
         start = pl.multiple_of(row * QB, QB)
@@ -103,7 +107,7 @@
         stack_ref[rows_n:, start : start + LANES] = times_i(block).astype(BF16)
     after_x = dot(fwd_x_ref[...], stack_ref[...]).astype(BF16)
 
-    @pl.loop(0, width // 512)
+    @pl.loop(0, width // 512, unroll=4)
     def _(at):
         span = pl.ds(pl.multiple_of(at * 512, 512), 512)
         out_ref[:, span] = dot(after_x, big_y_ref[:, span]).astype(BF16)
@@ -116,46 +120,51 @@
 
 
 def step_kernel(
-    place_ref, after_y_ref, near_ref, far_ref, bands_ref, big_y_ref, fwd_z_ref, back_x_ref, send_ref,
-    stepped_ref, sent_ref, back_ref, stack_ref, pots_ref,
+    near_at_ref, after_y_ref, near_any, far_any, bands_ref, big_y_any, fwd_z_ref, back_x_ref,
+    send_ref, stepped_ref, sent_ref, back_ref, stack_ref, pots_ref, near_ref, far_ref, big_y_ref,
+    sems,
 ):
+    table_copy = pltpu.make_async_copy(big_y_any, big_y_ref, sems.at[0])
+    near_copy = pltpu.make_async_copy(near_any, near_ref, sems.at[1])
+    far_copy = pltpu.make_async_copy(far_any, far_ref, sems.at[2])
+    near_copy.start()
+    far_copy.start()
+    table_copy.start()
     fwd_z = fwd_z_ref[...]
-    near = place_ref[0]
+    near = near_at_ref[0]
     quarter = FG * FG // 4
     pick_shape = (FG // 2, 2 * FG)
+    near_copy.wait()
+    far_copy.wait()
     for at in range(4):
-        pick = (iota(pick_shape, 0) * 4 + at == iota(pick_shape, 1)).astype(F32).astype(BF16)
+        pick = onehot(iota(pick_shape, 0) * 4 + at == iota(pick_shape, 1))
         span = slice(at * quarter, (at + 1) * quarter)
         pots_ref[near, :, span] = dot(pick, near_ref[...])
         pots_ref[1 - near, :, span] = dot(pick, far_ref[...])
 
-    @pl.loop(0, FG // LOCAL)
-    def _(at):
-        span = pl.ds(pl.multiple_of(at * LANES, LANES), LANES)
+    for at in range(FG // LOCAL):
+        span = slice(at * LANES, (at + 1) * LANES)
         grid_vals = dot(after_y_ref[:, span], fwd_z) * (4.0 / FG**1.5)
-        wide = pl.ds(pl.multiple_of(at * 2 * LANES, 2 * LANES), 2 * LANES)
         pots = []
         for half in (0, 1):
-            pot = pots_ref[half, :, wide]
+            pot = pots_ref[half, :, at * 2 * LANES : (at + 1) * 2 * LANES]
             parts = [*spread_parts(pot[:, :LANES]), *spread_parts(pot[:, LANES:])]
             pots += [jnp.concatenate(parts, axis=1)] * LOCAL
         weighted = (grid_vals * jnp.concatenate(pots, axis=0)).astype(BF16)
         back_ref[:, span] = dot_t(weighted, fwd_z).astype(BF16)
 
+    table_copy.wait()
     rows_n = LOCAL * FG
     half_n = LOCAL * HB
     block_n = 2 * LANES
-
-    @pl.loop(0, HB * 2 * QB // block_n)
-    def _(at):
-        start = pl.multiple_of(at * block_n, block_n)
-        span = pl.ds(start, block_n)
+    for start in range(0, HB * 2 * QB, block_n):
+        span = slice(start, start + block_n)
         block = dot_t(back_ref[...], big_y_ref[span, :])
-        stack_ref[:rows_n, :] = block.astype(BF16)
-        for low in (0, LANES):
-            turned = times_i(block[:, low : low + LANES])
+        stack_ref[:rows_n, span] = block.astype(BF16)
+        for low in range(start, start + block_n, LANES):
+            turned = times_i(block[:, low - start : low - start + LANES])
             stack_ref[rows_n:, low : low + LANES] = turned.astype(BF16)
-        image = dot(back_x_ref[...], stack_ref[...]) * (0.25 / FG**1.5)
+        image = dot(back_x_ref[...], stack_ref[:, span]) * (0.25 / FG**1.5)
         shape = (half_n, block_n)
         row, lane = iota(shape, 0), iota(shape, 1) + start
         mx, my = row % HB - HB // 2, lane // (2 * QB) - HB // 2
@@ -175,22 +184,23 @@
     for start in range(0, HB * 2 * QB, LANES):
         block = stepped_ref[:, start : start + LANES].astype(F32)
         stack_ref[half_n:, start : start + LANES] = times_i(block).astype(BF16)
-    image_ref[...] = dot(fwd_x_ref[...], stack_ref[...]).astype(BF16)
-
-
-def onehot(matches):
-    return matches.astype(F32).astype(BF16)
-
-
-def gram_kernel(received_ref, image_ref, out_ref, stepped_ref, conj_ref):
+    coefs = HB * 2 * QB
+    image_ref[:, :coefs] = dot(fwd_x_ref[...], stack_ref[...]).astype(BF16)
+    image_ref[:, coefs:] = jnp.zeros((2 * NB, NB), BF16)
+
+
+def gram_kernel(received_any, image_any, out_any, stepped_ref, conj_ref, extra_ref, received_ref, sems):
+    received_copy = pltpu.make_async_copy(received_any, received_ref, sems.at[0])
+    received_copy.start()
     coefs = HB * 2 * QB
     half_w = coefs // 2
     shape = (NB, 2 * NB)
     row, col = iota(shape, 0), iota(shape, 1)
     at = row // LOCAL * 2 * LOCAL + row % LOCAL
+    picks = [onehot(col == at + half * LOCAL) for half in (0, 1)]
+    received_copy.wait()
     for half in (0, 1):
-        pick = onehot(col == at + half * LOCAL)
-        rows = dot(pick, received_ref[...])
+        rows = dot(picks[half], received_ref[...])
         stepped_ref[:, half * half_w : (half + 1) * half_w] = rows.astype(BF16)
         for start in range(0, half_w, LANES):
             block = -times_i(rows[:, start : start + LANES])
@@ -200,24 +210,20 @@
     gram_im = dot_t(stepped, conj_ref[...])
     shape = (NB, NB)
     gram = jnp.where(iota(shape, 0) >= iota(shape, 1), gram_re, gram_im) * (1.0 / COEF)
-    first, _ = halves(gram)
-    second = (gram - first.astype(F32)).astype(BF16)
-    third = (gram - first.astype(F32) - second.astype(F32)).astype(BF16)
+    upper, lower = halves(gram)
     shape = (2 * NB, NB)
     row, col = iota(shape, 0), iota(shape, 1)
     at = col // LOCAL * 2 * LOCAL + col % LOCAL
-    upper, lower = onehot(row == at), onehot(row == at + LOCAL)
-    out_ref[:, :coefs] = image_ref[...]
-    out_ref[:, coefs : coefs + NB] = (dot(upper, first) + dot(lower, second)).astype(BF16)
-    out_ref[:, coefs + NB :] = dot(upper, third).astype(BF16)
+    spread = dot(onehot(row == at), upper) + dot(onehot(row == at + LOCAL), lower)
+    extra_ref[...] = spread.astype(BF16)
+    extra_copy = pltpu.make_async_copy(extra_ref, out_any.at[:, coefs:], sems.at[1])
+    extra_copy.start()
+    extra_copy.wait()
 
 
 def sum_kernel(parts_ref, out_ref):
-    parts = parts_ref[...].astype(F32).reshape(HB, 2 * LOCAL, 2 * NB).sum(axis=0)
-    swapped = pltpu.roll(parts, LOCAL, 0)
-    whole = (parts + swapped)[:, :NB]
-    third = parts[:, NB:] + swapped[:, NB:]
-    whole = whole + third
+    parts = parts_ref[...].astype(F32).reshape(HB, 2 * LOCAL, NB).sum(axis=0)
+    whole = parts + pltpu.roll(parts, LOCAL, 0)
     out_ref[...] = jnp.broadcast_to(whole[None], (NB // 8, 8, NB)).reshape(NB, NB)
 
 
@@ -261,7 +267,14 @@
         [jnp.concatenate([re_hi, im_hi], axis=1), jnp.concatenate([re_lo, im_lo], axis=1)], axis=0
     )
     both = dot(left, stack_ref[...])
-    phi_ref[...] = (both[:NB] + both[NB:]).astype(BF16)
+    phi = (both[:NB] + both[NB:]).astype(BF16)
+    half_w = HB * QB
+    shape = (2 * NB, NB)
+    row, col = iota(shape, 0), iota(shape, 1)
+    same = row // (2 * LOCAL) * LOCAL + row % LOCAL == col
+    picks = [onehot(same & (row // LOCAL % 2 == half)) for half in (0, 1)]
+    sent = dot(picks[0], phi[:, :half_w]) + dot(picks[1], phi[:, half_w:])
+    phi_ref[...] = sent.astype(BF16)
 
 
 def density_kernel(
@@ -296,14 +309,14 @@
     phi_ref[...] = (both[:rows_n] + both[rows_n:]).astype(BF16)
     width = FG * 2 * QB
 
-    @pl.loop(0, width // 512)
+    @pl.loop(0, width // 512, unroll=4)
     def _(at):
         span = pl.ds(pl.multiple_of(at * 512, 512), 512)
         after_y_ref[:, span] = dot(phi_ref[...], big_y_ref[:, span]).astype(BF16)
 
     low = iota((1, LANES), 1) < FG
 
-    @pl.loop(0, FG // LOCAL)
+    @pl.loop(0, FG // LOCAL, unroll=4)
     def _(at):
         span = pl.ds(pl.multiple_of(at * LANES, LANES), LANES)
         grid_vals = dot(after_y_ref[:, span], fwd_z_ref[...]) * (4.0 / FG**1.5)
@@ -337,9 +350,12 @@
             out_ref[to, FG + at * 16 : FG + (at + 1) * 16, :] = part
 
 
-def last_kernel(place_ref, own_ref, pieces_ref, out_ref, total_ref):
+def last_kernel(place_ref, own_ref, pieces_any, out_ref, total_ref, pieces_ref, sem):
+    pieces_copy = pltpu.make_async_copy(pieces_any, pieces_ref, sem)
+    pieces_copy.start()
     own = own_ref[0]
     own_y, own_z = place_ref[own, 1], place_ref[own, 2]
+    pieces_copy.wait()
     patched = jnp.zeros((FG, LANES), F32)
     for at in range(FRAGS):
         patched += pieces_ref[at, :FG, :].astype(F32)
@@ -359,27 +375,37 @@
     even = total_ref[pl.ds(0, FG // 2, stride=2), :]
     odd = total_ref[pl.ds(1, FG // 2, stride=2), :]
     low = iota(even.shape, 1) < FG
-    out_ref[0] = jnp.where(low, even, pltpu.roll(odd, FG, 1))
-    out_ref[1] = jnp.where(low, pltpu.roll(even, FG, 1), odd)
+    planes = [jnp.where(low, even, pltpu.roll(odd, FG, 1)), jnp.where(low, pltpu.roll(even, FG, 1), odd)]
+    for plane in (0, 1):
+        for at in range(FG // 2):
+            out_ref[plane : plane + 1, at * LANES : (at + 1) * LANES] = planes[plane][at : at + 1]
 
 
 VM = pl.BlockSpec(memory_space=pltpu.VMEM)
 SM = pl.BlockSpec(memory_space=pltpu.SMEM)
+ANY = pl.BlockSpec(memory_space=pl.ANY)
+HBM = pl.BlockSpec(memory_space=pltpu.HBM)
 
 
 def sds(shape, dtype):
     return jax.ShapeDtypeStruct(shape, dtype)
 
 
-def call(kernel, outs, in_specs, scratch, flops, moved):
+def call(kernel, outs, in_specs, scratch, flops, moved, name, copies=0, out_specs=None, aliases=None):
     return pl.pallas_call(
         kernel,
         out_shape=outs,
         in_specs=in_specs,
-        out_specs=jax.tree.map(lambda _: VM, outs),
-        scratch_shapes=[pltpu.VMEM(s, d) for s, d in scratch],
+        out_specs=out_specs or jax.tree.map(lambda _: VM, outs),
+        scratch_shapes=[pltpu.VMEM(s, d) for s, d in scratch]
+        + ([pltpu.SemaphoreType.DMA((copies,) if copies > 1 else ())] if copies else []),
+        input_output_aliases=aliases or {},
         cost_estimate=pl.CostEstimate(flops=flops, bytes_accessed=moved, transcendentals=0),
-    )
+        compiler_params=pltpu.CompilerParams(vmem_limit_bytes=GRANT.get(name, 8) << 20),
+    )
+
+
+GRANT = {"forward": 16, "step": 24, "density": 24}
 
 
 def stages():
@@ -391,42 +417,47 @@
         (sds((coefs, width), BF16), sds((LOCAL * FG, width), BF16)),
         [VM] * 3,
         [((2 * HB, width), F32), ((2 * LOCAL * HB, coefs), BF16)],
-        2 * 10**9, 6 * mega,
+        2 * 10**9, 6 * mega, "forward",
     )
     step = call(
         step_kernel,
         (sds((LOCAL * HB, coefs), BF16), sds((2 * NB, coefs // 2), BF16)),
-        [SM] + [VM] * 8,
+        [SM, VM, ANY, ANY, VM, HBM, VM, VM, VM],
         [
             ((LOCAL * FG, width), BF16),
-            ((2 * LOCAL * FG, 2 * LANES), BF16),
+            ((2 * LOCAL * FG, coefs), BF16),
             ((2, FG // 2, FG * FG), F32),
+            ((2 * FG, FG * FG // 4), BF16),
+            ((2 * FG, FG * FG // 4), BF16),
+            ((coefs, width), BF16),
         ],
-        4 * 10**9, 8 * mega,
+        4 * 10**9, 8 * mega, "step", 3,
     )
     image = call(
-        image_kernel, sds((LOCAL * FG, coefs), BF16), [VM] * 2, [((2 * LOCAL * HB, coefs), BF16)],
-        10**8, mega,
+        image_kernel, sds((LOCAL * FG, coefs + NB), BF16), [VM] * 2,
+        [((2 * LOCAL * HB, coefs), BF16)], 10**8, mega, "image",
     )
     gram = call(
         gram_kernel,
-        (sds((2 * NB, coefs + 2 * NB), BF16), sds((NB, coefs), BF16)),
-        [VM] * 2, [((NB, coefs), BF16)], 2 * 10**8, 2 * mega,
+        (sds((2 * NB, coefs + NB), BF16), sds((NB, coefs), BF16)),
+        [ANY, ANY],
+        [((NB, coefs), BF16), ((2 * NB, NB), BF16), ((2 * NB, coefs // 2), BF16)],
+        2 * 10**8, 2 * mega, "gram", 2, (ANY, VM), {1: 0},
     )
     total = pl.pallas_call(
         sum_kernel,
         grid=(1,),
         out_shape=sds((NB, NB), F32),
-        in_specs=[pl.BlockSpec((2 * NB, 2 * NB), lambda i: (0, coefs // (2 * NB)))],
+        in_specs=[pl.BlockSpec((2 * NB, NB), lambda i: (0, coefs // NB))],
         out_specs=pl.BlockSpec((NB, NB), lambda i: (0, 0)),
         name="total",
     )
     newton = call(
         newton_kernel,
-        (sds((NB, coefs), BF16), sds((4 * NB, NB), BF16)),
+        (sds((2 * NB, coefs // 2), BF16), sds((4 * NB, NB), BF16)),
         [VM] * 2,
         [((2 * NB, coefs), BF16)],
-        10**9, mega,
+        10**9, mega, "newton",
     )
     density = call(
         density_kernel,
@@ -438,11 +469,11 @@
             ((2 * NB, width), BF16),
             ((FG, LANES), F32),
         ],
-        4 * 10**9, 6 * mega,
+        4 * 10**9, 6 * mega, "density",
     )
     last = call(
-        last_kernel, sds((2, FG // 2, LANES), F32), [SM, SM, VM], [((FG, LANES), F32)],
-        10**7, mega // 2,
+        last_kernel, sds((2, FG * FG), F32), [SM, SM, ANY],
+        [((FG, LANES), F32), ((FRAGS, FG + 32, LANES), BF16)], 10**7, mega // 2, "last", 1,
     )
     return forward, step, image, gram, total, newton, density, last
 
@@ -461,7 +492,7 @@
     chips = groups // 2
     planes = FG // groups
     own = lax.axis_index("frag").astype(jnp.int32).reshape(1)
-    near = (lax.axis_index("band") % 2).astype(jnp.int32).reshape(1)
+    near = (lax.axis_index("band") & 1).astype(jnp.int32).reshape(1)
 
     pot = potential_in.astype(BF16).reshape(1, planes * 4, FG * FG // 4)
     along = [[2 * z + x for z in range(chips)] for x in (0, 1)]
@@ -479,11 +510,12 @@
     parts = exchange(parts.reshape(groups, planes * LOCAL, -1), "band").reshape(2 * NB, -1)
     whole = exchange(total(parts).reshape(groups, LOCAL, NB), "band").reshape(NB, NB)
     phi, inverse = newton(whole, stepped)
-    phi_local = exchange(phi.reshape(groups, LOCAL, coefs), "band")
+    phi_local = exchange(phi.reshape(groups, 2 * LOCAL, coefs // 2), "band")
     pieces = density(patch_list, own, parts, inverse, big_y, fwd_z, hartree)
     pieces, phi_local = lax.optimization_barrier((pieces, phi_local))
     back = last(patch_list, own, exchange(pieces, "frag")).reshape(1, planes, FG * FG)
-    bands_out = phi_local.transpose(1, 0, 2).astype(F32).reshape(1, LOCAL, HB * coefs)
+    bands_out = phi_local.reshape(groups, 2, LOCAL, coefs // 2).transpose(2, 0, 1, 3)
+    bands_out = bands_out.astype(F32).reshape(1, LOCAL, HB * coefs)
     return (bands_out, back)
 
 

time: 205 us -> 187 us (0.912)
  Pallas kernels: 45.9 us -> 27.2 us
  waiting for transfers between devices: 30.5 us -> 35 us
  blocking collectives: 87.9 us -> 85.5 us
    pallas_call x1, Pallas kernels: 13 us -> 7.77 us  [per_device(): step(near, after_y, pot_near, pot_far, bands, big_y, fwd_z, back_x, send)]
    pallas_call x1, Pallas kernels: 13 us -> 7.79 us  [per_device(): pieces = density(patch_list, own, parts, inverse, big_y, fwd_z, hartree)]
    all_to_all x3, waiting for transfers between devices: 30.5 us -> 35 us  [exchange(): lax.all_to_all(values, axis, split_axis=0, concat_axis=0, tiled=True, axi...]
    pallas_call x1, Pallas kernels: 6.48 us -> 2.81 us  [per_device(): big_y, after_y = forward(bands, fwd_x, fwd_y)]
    all_to_all x3, blocking collectives: 87.9 us -> 85.5 us  [exchange(): lax.all_to_all(values, axis, split_axis=0, concat_axis=0, tiled=True, axi...]
  transfers between devices with their start and end apart: 4 -> 4, of which waited for: 3 -> 3; matrix products, arithmetic and copies ran while one was open for 2% -> 2% of each run, Pallas kernels for 11% -> 6%
where the time goes in v3:
time: 187 us; the launch traced here: 186 us
  blocking collectives  85.5 us (46%)
  waiting for transfers between devices  35 us (19%)
  starting transfers between devices  29.9 us (16%)
  Pallas kernels  27.2 us (15%)
  local copies, waits for them, and re-layouts  6.88 us (4%)
    all_to_all x3, blocking collectives, exchange(): lax.all_to_all(values, axis, split_axis=0, concat_axis=0, tiled=True, axi...  85.5 us
    all_to_all x3, waiting for transfers between devices, exchange(): lax.all_to_all(values, axis, split_axis=0, concat_axis=0, tiled=True, axi...  35 us
    all_to_all x3, starting transfers between devices, exchange(): lax.all_to_all(values, axis, split_axis=0, concat_axis=0, tiled=True, axi...  26.8 us
    pallas_call x1, Pallas kernels, per_device(): pieces = density(patch_list, own, parts, inverse, big_y, fwd_z, hartree)  7.79 us
    pallas_call x1, Pallas kernels, per_device(): step(near, after_y, pot_near, pot_far, bands, big_y, fwd_z, back_x, send)  7.77 us
    pallas_call x1, Pallas kernels, per_device(): phi, inverse = newton(whole, stepped)  4 us
    unnamed x23, local copies, waits for them, and re-layouts  3.94 us
  transfers between devices with their start and end apart: 4, of which 3 were waited for; matrix products, arithmetic and copies ran while one was open for 2% of the time, Pallas kernels for 6%

profile of v3, /device:TPU:1, one launch (start us, length us, event | category | flops | bytes accessed | tf_op | source)
XLA Modules:
  0.0 186.3 jit_solution(16190418986617748055)
XLA Ops:
  0.6 0.8 convert_element_type.30
  1.4 0.0 copy-start.3
  1.5 0.0 copy-start.4
  1.5 0.0 copy-start.5
  1.5 29.4 %all_to_all.30 = bf16[16,8,1024]{2,1,0:T(8,128)(2,1)S(1)} all-to-all(bf16[16,8,1024]{2,1,0:T(8,128)(2,1)S(1)} %broadcast_in_dim.8), channel_id=1, replica_groups={{0,2,4,6,8,10,12,14,16,18,20,22,24,26,28,30},{1,3,5,7,9,11,13,15,17,19,..., dimensions={0} | all-to-all | bytes 524288 | tf_op jit(solution)/shard_map/all_to_all | solution.py:482
  30.9 3.1 %collective-permute-start = (bf16[128,1024]{1,0:T(8,128)(2,1)S(1)}, bf16[128,1024]{1,0:T(8,128)(2,1)S(1)}, u32[]{:S(2)}, u32[]{:S(2)}) collective-permute-start(bf16[128,1024]{1,0:T(8,128)(2,1)S(1)} %bitcast.18), channel_id=1, source_target_pairs={{0,1},{1,0},{2,3},{3,2},{4,5},{5,4},{6,7},{7,6},{8,9},{9,8},{10,11... | collective-permute-start | bytes 786440 | tf_op jit(solution)/shard_map/ppermute | solution.py:501
  34.0 1.1 reshape.53.bands_ref
  35.2 0.0 copy-start.6
  35.2 0.9 copy-done.6
  36.1 0.0 copy-start.7
  36.1 0.7 copy-done.7
  36.8 2.8 %shard_map.113 = (bf16[1024,2048]{1,0:T(8,128)(2,1)S(1)}, bf16[256,2048]{1,0:T(8,128)(2,1)S(1)}) custom-call(bf16[128,1024]{1,0:T(8,128)(2,1)S(1)} %reshape.53.bands_ref, bf16[256,256]{1,0:T(8,128)(2,1)S(1)} %copy-done.6, bf16[64,128]{1,0:T(8,128)(2,1)S(1)} %copy-done.7), custom_call_target="tpu_custom_call" | custom-call | flops 2000000000 | bytes 6291456 | tf_op jit(solution)/shard_map/pallas_call | solution.py:503
  39.6 0.0 copy-start.8
  39.6 0.0 collective-permute-done.far_any
  39.6 0.0 copy-done.3
  39.7 0.0 copy-done.4
  39.7 0.0 copy-done.5
  39.7 0.0 copy-start.1
  39.7 7.8 %shard_map.114 = (bf16[128,1024]{1,0:T(8,128)(2,1)S(1)}, bf16[256,512]{1,0:T(8,128)(2,1)}) custom-call(s32[1]{0:T(128)} %bitcast.1.near_at_ref, bf16[256,2048]{1,0:T(8,128)(2,1)S(1)} %get-tuple-element.12.after_y_ref, bf16[128,1024]{1,0:T(8,128)(2,1)S(1)} %bitcast.19, bf16[128,1024]{1,0:T(8,128)(2,1)S(1)} %collective-permute-done.far_any, ...), custom_call_target="tpu_custom_call" | custom-call | flops 4000000000 | bytes 8388608 | tf_op jit(solution)/shard_map/pallas_call | solution.py:504
  47.5 0.0 copy-done.8
  47.5 0.0 copy-start.10
  47.5 0.0 copy-start.2
  47.5 11.8 %all-to-all-start.1 = ((bf16[32,8,512]{2,1,0:T(8,128)(2,1)}), bf16[32,8,512]{2,1,0:T(8,128)(2,1)S(1)}, u32[]{:S(2)}, u32[]{:S(2)}) async-start(bf16[32,8,512]{2,1,0:T(8,128)(2,1)} %bitcast.3), calls=%async_computation.1 | async-start | bytes 524288 | tf_op jit(solution)/shard_map/all_to_all | solution.py:482
  59.3 0.0 copy-done.1
  59.3 0.4 shard_map.115.image_any
  59.8 18.7 %all-to-all-done.1 = bf16[32,8,512]{2,1,0:T(8,128)(2,1)S(1)} async-done(((bf16[32,8,512]{2,1,0:T(8,128)(2,1)}), bf16[32,8,512]{2,1,0:T(8,128)(2,1)S(1)}, u32[]{:S(2)}, u32[]{:S(2)}) %all-to-all-start.1) | async-done | bytes 262176 | tf_op jit(solution)/shard_map/all_to_all | solution.py:482
  78.5 1.0 shard_map.116
  79.4 38.3 %all_to_all.31 = bf16[32,8,1152]{2,1,0:T(8,128)(2,1)} all-to-all(bf16[32,8,1152]{2,1,0:T(8,128)(2,1)S(1)} %bitcast.14), channel_id=1, replica_groups=mesh['frag'=16,'band'=32] {'band'}, dimensions={0} | all-to-all | bytes 1179648 | tf_op jit(solution)/shard_map/all_to_all | solution.py:482
  117.7 0.0 copy-start
  117.7 1.6 total.1
  119.3 17.8 %all_to_all.32 = f32[32,4,128]{2,1,0:T(4,128)S(1)} all-to-all(f32[32,4,128]{2,1,0:T(4,128)} %bitcast.22), channel_id=1, replica_groups=mesh['frag'=16,'band'=32] {'band'}, dimensions={0} | all-to-all | bytes 131072 | tf_op jit(solution)/shard_map/all_to_all | solution.py:482
  137.1 4.0 %shard_map.117 = (bf16[256,512]{1,0:T(8,128)(2,1)}, bf16[512,128]{1,0:T(8,128)(2,1)S(1)}) custom-call(f32[128,128]{1,0:T(8,128)S(1)} %bitcast.20, bf16[128,1024]{1,0:T(8,128)(2,1)S(1)} %get-tuple-element.17.stepped_ref), custom_call_target="tpu_custom_call" | custom-call | flops 1000000000 | bytes 1048576 | tf_op jit(solution)/shard_map/pallas_call | solution.py:512
  141.1 3.9 %all-to-all-start.4 = ((bf16[32,8,512]{2,1,0:T(8,128)(2,1)}), bf16[32,8,512]{2,1,0:T(8,128)(2,1)S(1)}, u32[]{:S(2)}, u32[]{:S(2)}) async-start(bf16[32,8,512]{2,1,0:T(8,128)(2,1)} %bitcast.9), calls=%async_computation.4 | async-start | bytes 524288 | tf_op jit(solution)/shard_map/all_to_all | solution.py:482
  144.9 0.0 copy-done.10
  145.0 0.1 copy.13.place_ref
  145.0 0.0 copy-done.2
  145.0 0.0 copy-done
  145.0 0.0 copy-start.9
  145.0 2.2 %copy-done.9 = bf16[1024,2048]{1,0:T(8,128)(2,1)S(1)} copy-done((bf16[1024,2048]{1,0:T(8,128)(2,1)S(1)}, bf16[1024,2048]{1,0:T(8,128)(2,1)}, u32[]{:S(2)}) %copy-start.9) | copy-done | bytes 4194328
  147.2 7.8 %shard_map.118 = bf16[16,96,128]{2,1,0:T(8,128)(2,1)} custom-call(s32[16,3]{1,0:T(8,128)S(1)} %copy.13.place_ref, s32[1]{0:T(128)} %bitcast.own_ref, bf16[256,1152]{1,0:T(8,128)(2,1)S(1)} %bitcast.16, bf16[512,128]{1,0:T(8,128)(2,1)S(1)} %get-tuple-element.18.inv_ref, bf16[1024,2048]{1,0:T(8,128)(2,1)S(1)} %copy-done.9, bf16[128,512]{1,0:T(8,128)(2,1)S(1)} %copy-done.3, ...), custom_call_target="tpu_custom_call" | custom-call | flops 4000000000 | bytes 6291456 | tf_op jit(solution)/shard_map/pallas_call | solution.py:514
  155.0 8.4 %all-to-all-done.4 = bf16[32,8,512]{2,1,0:T(8,128)(2,1)S(1)} async-done(((bf16[32,8,512]{2,1,0:T(8,128)(2,1)}), bf16[32,8,512]{2,1,0:T(8,128)(2,1)S(1)}, u32[]{:S(2)}, u32[]{:S(2)}) %all-to-all-start.4) | async-done | bytes 262176 | tf_op jit(solution)/shard_map/all_to_all | solution.py:482
  163.4 11.1 %all-to-all-start.5 = ((bf16[16,96,128]{2,1,0:T(8,128)(2,1)}), bf16[16,96,128]{2,1,0:T(8,128)(2,1)S(1)}, u32[]{:S(2)}, u32[]{:S(2)}) async-start(bf16[16,96,128]{2,1,0:T(8,128)(2,1)} %shard_map.118), calls=%async_computation.5 | async-start | bytes 786432 | tf_op jit(solution)/shard_map/all_to_all | solution.py:482
  174.5 0.2 reshape.69
  174.7 0.3 copy.17
  174.9 1.3 reshape.66
  176.3 8.0 %all-to-all-done.5.pieces_any = bf16[16,96,128]{2,1,0:T(8,128)(2,1)S(1)} async-done(((bf16[16,96,128]{2,1,0:T(8,128)(2,1)}), bf16[16,96,128]{2,1,0:T(8,128)(2,1)S(1)}, u32[]{:S(2)}, u32[]{:S(2)}) %all-to-all-start.5) | async-done | bytes 393248 | tf_op jit(solution)/shard_map/all_to_all | solution.py:482
  184.3 1.9 %shard_map.119 = f32[2,4096]{1,0:T(2,128)} custom-call(s32[16,3]{1,0:T(8,128)S(1)} %copy.13.place_ref, s32[1]{0:T(128)} %bitcast.own_ref, bf16[16,96,128]{2,1,0:T(8,128)(2,1)S(1)} %all-to-all-done.5.pieces_any), custom_call_target="tpu_custom_call" | custom-call | flops 10000000 | bytes 524288 | tf_op jit(solution)/shard_map/pallas_call | solution.py:516
  (2 shorter events, 0.0 us)
Async XLA Ops:
  1.4 38.2 %copy-start.3 = (bf16[128,512]{1,0:T(8,128)(2,1)S(1)}, bf16[128,512]{1,0:T(8,128)(2,1)}, u32[]{:S(2)}) copy-start(bf16[128,512]{1,0:T(8,128)(2,1)} %constant.34.fwd_z_ref) | copy-start | bytes 393220
  1.5 38.2 %copy-start.4 = (bf16[128,512]{1,0:T(8,128)(2,1)S(1)}, bf16[128,512]{1,0:T(8,128)(2,1)}, u32[]{:S(2)}) copy-start(bf16[128,512]{1,0:T(8,128)(2,1)} %constant.35.back_x_ref) | copy-start | bytes 393220
  1.5 38.2 %copy-start.5 = (bf16[256,256]{1,0:T(8,128)(2,1)S(1)}, bf16[256,256]{1,0:T(8,128)(2,1)}, u32[]{:S(2)}) copy-start(bf16[256,256]{1,0:T(8,128)(2,1)} %constant.36.send_ref) | copy-start | bytes 393220
  30.9 8.7 %collective-permute-start = (bf16[128,1024]{1,0:T(8,128)(2,1)S(1)}, bf16[128,1024]{1,0:T(8,128)(2,1)S(1)}, u32[]{:S(2)}, u32[]{:S(2)}) collective-permute-start(bf16[128,1024]{1,0:T(8,128)(2,1)S(1)} %bitcast.18), channel_id=1, source_target_pairs={{0,1},{1,0},{2,3},{3,2},{4,5},{5,4},{6,7},{7,6},{8,9},{9,8},{10,11... | collective-permute-start | bytes 786440 | tf_op jit(solution)/shard_map/ppermute | solution.py:501
  35.2 0.9 copy-start.6
  36.1 0.7 copy-start.7
  39.6 7.8 %copy-start.8 = (bf16[1024,2048]{1,0:T(8,128)(2,1)}, bf16[1024,2048]{1,0:T(8,128)(2,1)S(1)}, u32[]{:S(2)}) copy-start(bf16[1024,2048]{1,0:T(8,128)(2,1)S(1)} %get-tuple-element.13.big_y_any.big_y_ref) | copy-start | bytes 12582916
  39.7 19.6 %copy-start.1 = (bf16[256,256]{1,0:T(8,128)(2,1)S(1)}, bf16[256,256]{1,0:T(8,128)(2,1)}, u32[]{:S(2)}) copy-start(bf16[256,256]{1,0:T(8,128)(2,1)} %constant.37.fwd_x_ref) | copy-start | bytes 393220
  47.5 97.5 %copy-start.10 = (s32[16,3]{0,1:T(4,128)S(1)}, s32[16,3]{0,1:T(4,128)}, u32[]{:S(2)}) copy-start(s32[16,3]{0,1:T(4,128)} %param.13) | copy-start | bytes 580
  47.5 97.6 %copy-start.2 = (f32[2,8,128]{2,1,0:T(8,128)S(1)}, f32[2,8,128]{2,1,0:T(8,128)}, u32[]{:S(2)}) copy-start(f32[2,8,128]{2,1,0:T(8,128)} %tile_ref.1) | copy-start | bytes 24580
  47.5 31.0 %all-to-all-start.1 = ((bf16[32,8,512]{2,1,0:T(8,128)(2,1)}), bf16[32,8,512]{2,1,0:T(8,128)(2,1)S(1)}, u32[]{:S(2)}, u32[]{:S(2)}) async-start(bf16[32,8,512]{2,1,0:T(8,128)(2,1)} %bitcast.3), calls=%async_computation.1 | async-start | bytes 524288 | tf_op jit(solution)/shard_map/all_to_all | solution.py:482
  117.7 27.3 %copy-start = (bf16[32,8,1152]{2,1,0:T(8,128)(2,1)S(1)}, bf16[32,8,1152]{2,1,0:T(8,128)(2,1)}, u32[]{:S(2)}) copy-start(bf16[32,8,1152]{2,1,0:T(8,128)(2,1)} %all_to_all.31) | copy-start | bytes 1769476
  141.1 22.3 %all-to-all-start.4 = ((bf16[32,8,512]{2,1,0:T(8,128)(2,1)}), bf16[32,8,512]{2,1,0:T(8,128)(2,1)S(1)}, u32[]{:S(2)}, u32[]{:S(2)}) async-start(bf16[32,8,512]{2,1,0:T(8,128)(2,1)} %bitcast.9), calls=%async_computation.4 | async-start | bytes 524288 | tf_op jit(solution)/shard_map/all_to_all | solution.py:482
  145.0 2.2 %copy-start.9 = (bf16[1024,2048]{1,0:T(8,128)(2,1)S(1)}, bf16[1024,2048]{1,0:T(8,128)(2,1)}, u32[]{:S(2)}) copy-start(bf16[1024,2048]{1,0:T(8,128)(2,1)} %copy-done.8) | copy-start | bytes 12582916
  163.4 20.9 %all-to-all-start.5 = ((bf16[16,96,128]{2,1,0:T(8,128)(2,1)}), bf16[16,96,128]{2,1,0:T(8,128)(2,1)S(1)}, u32[]{:S(2)}, u32[]{:S(2)}) async-start(bf16[16,96,128]{2,1,0:T(8,128)(2,1)} %shard_map.118), calls=%async_computation.5 | async-start | bytes 786432 | tf_op jit(solution)/shard_map/all_to_all | solution.py:482

commit v4 on v3

--- a/solution.py
+++ b/solution.py
@@ -45,8 +45,8 @@
     fwd_x_send = fwd_x.transpose(1, 2, 3, 0, 4).reshape(LOCAL * FG, -1)
     fwd_x = fwd_x.transpose(2, 0, 1, 3, 4).reshape(LOCAL * FG, -1)
     back_x = np.stack([np.einsum("ab,xk->akbx", same, t) for t in (cos_xy, -sin_xy)], axis=2)
-    back_x = back_x.reshape(LOCAL * HB, 2, LOCAL, FG // 4, 2, 2).transpose(0, 1, 4, 2, 3, 5)
-    back_x = back_x.reshape(LOCAL * HB, 2 * LOCAL * FG)
+    back_x = back_x.reshape(LOCAL * HB, 2, LOCAL, FG // 4, 2, 2).transpose(4, 0, 1, 2, 3, 5)
+    back_x = back_x.reshape(2, LOCAL * HB, LOCAL * FG)
     fwd_y = np.stack(
         [np.stack([cos_xy.T, sin_xy.T], axis=2), np.stack([-sin_xy.T, cos_xy.T], axis=2)], axis=1
     ).reshape(2 * HB, 2 * FG)
@@ -106,11 +106,14 @@
         block = bands_ref[:, start : start + LANES].astype(F32)
         stack_ref[rows_n:, start : start + LANES] = times_i(block).astype(BF16)
     after_x = dot(fwd_x_ref[...], stack_ref[...]).astype(BF16)
+    half_n = LOCAL * FG // 2
 
     @pl.loop(0, width // 512, unroll=4)
     def _(at):
         span = pl.ds(pl.multiple_of(at * 512, 512), 512)
-        out_ref[:, span] = dot(after_x, big_y_ref[:, span]).astype(BF16)
+        block = dot(after_x, big_y_ref[:, span]).astype(BF16)
+        out_ref[0, :, span] = block[:half_n]
+        out_ref[1, :, span] = block[half_n:]
 
 
 def spread_parts(pair):
@@ -119,43 +122,23 @@
     return jnp.where(low, pair, turned), jnp.where(low, turned, pair)
 
 
-def step_kernel(
-    near_at_ref, after_y_ref, near_any, far_any, bands_ref, big_y_any, fwd_z_ref, back_x_ref,
-    send_ref, stepped_ref, sent_ref, back_ref, stack_ref, pots_ref, near_ref, far_ref, big_y_ref,
-    sems,
-):
-    table_copy = pltpu.make_async_copy(big_y_any, big_y_ref, sems.at[0])
-    near_copy = pltpu.make_async_copy(near_any, near_ref, sems.at[1])
-    far_copy = pltpu.make_async_copy(far_any, far_ref, sems.at[2])
-    near_copy.start()
-    far_copy.start()
-    table_copy.start()
+def weigh_rows(at_half, after_y_ref, pot_ref, big_y_ref, fwd_z_ref, stack_ref, back_ref, pots_ref):
     fwd_z = fwd_z_ref[...]
-    near = near_at_ref[0]
     quarter = FG * FG // 4
     pick_shape = (FG // 2, 2 * FG)
-    near_copy.wait()
-    far_copy.wait()
     for at in range(4):
         pick = onehot(iota(pick_shape, 0) * 4 + at == iota(pick_shape, 1))
-        span = slice(at * quarter, (at + 1) * quarter)
-        pots_ref[near, :, span] = dot(pick, near_ref[...])
-        pots_ref[1 - near, :, span] = dot(pick, far_ref[...])
+        pots_ref[:, at * quarter : (at + 1) * quarter] = dot(pick, pot_ref[...])
 
     for at in range(FG // LOCAL):
         span = slice(at * LANES, (at + 1) * LANES)
-        grid_vals = dot(after_y_ref[:, span], fwd_z) * (4.0 / FG**1.5)
-        pots = []
-        for half in (0, 1):
-            pot = pots_ref[half, :, at * 2 * LANES : (at + 1) * 2 * LANES]
-            parts = [*spread_parts(pot[:, :LANES]), *spread_parts(pot[:, LANES:])]
-            pots += [jnp.concatenate(parts, axis=1)] * LOCAL
-        weighted = (grid_vals * jnp.concatenate(pots, axis=0)).astype(BF16)
-        back_ref[:, span] = dot_t(weighted, fwd_z).astype(BF16)
-
-    table_copy.wait()
-    rows_n = LOCAL * FG
-    half_n = LOCAL * HB
+        grid_vals = dot(after_y_ref[at_half, :, span], fwd_z) * (4.0 / FG**1.5)
+        pot = pots_ref[:, at * 2 * LANES : (at + 1) * 2 * LANES]
+        parts = [*spread_parts(pot[:, :LANES]), *spread_parts(pot[:, LANES:])]
+        pots = jnp.concatenate([jnp.concatenate(parts, axis=1)] * LOCAL, axis=0)
+        back_ref[:, span] = dot_t((grid_vals * pots).astype(BF16), fwd_z).astype(BF16)
+
+    rows_n = LOCAL * FG // 2
     block_n = 2 * LANES
     for start in range(0, HB * 2 * QB, block_n):
         span = slice(start, start + block_n)
@@ -164,7 +147,30 @@
         for low in range(start, start + block_n, LANES):
             turned = times_i(block[:, low - start : low - start + LANES])
             stack_ref[rows_n:, low : low + LANES] = turned.astype(BF16)
-        image = dot(back_x_ref[...], stack_ref[:, span]) * (0.25 / FG**1.5)
+
+
+def near_kernel(
+    near_at_ref, after_y_ref, pot_ref, big_y_ref, fwd_z_ref, stack_ref, back_ref, pots_ref
+):
+    weigh_rows(
+        near_at_ref[0], after_y_ref, pot_ref, big_y_ref, fwd_z_ref, stack_ref, back_ref, pots_ref
+    )
+
+
+def step_kernel(
+    near_at_ref, after_y_ref, pot_ref, big_y_ref, fwd_z_ref, near_ref, bands_ref, back_x_ref,
+    send_ref, stepped_ref, sent_ref, stack_ref, back_ref, pots_ref,
+):
+    near = near_at_ref[0]
+    weigh_rows(
+        1 - near, after_y_ref, pot_ref, big_y_ref, fwd_z_ref, stack_ref, back_ref, pots_ref
+    )
+    half_n = LOCAL * HB
+    block_n = 2 * LANES
+    for start in range(0, HB * 2 * QB, block_n):
+        span = slice(start, start + block_n)
+        image = dot(back_x_ref[near], near_ref[:, span])
+        image = (image + dot(back_x_ref[1 - near], stack_ref[:, span])) * (0.25 / FG**1.5)
         shape = (half_n, block_n)
         row, lane = iota(shape, 0), iota(shape, 1) + start
         mx, my = row % HB - HB // 2, lane // (2 * QB) - HB // 2
@@ -222,7 +228,7 @@
 
 
 def sum_kernel(parts_ref, out_ref):
-    parts = parts_ref[...].astype(F32).reshape(HB, 2 * LOCAL, NB).sum(axis=0)
+    parts = parts_ref[:, HB * 2 * QB :].astype(F32).reshape(HB, 2 * LOCAL, NB).sum(axis=0)
     whole = parts + pltpu.roll(parts, LOCAL, 0)
     out_ref[...] = jnp.broadcast_to(whole[None], (NB // 8, 8, NB)).reshape(NB, NB)
 
@@ -405,7 +411,7 @@
     )
 
 
-GRANT = {"forward": 16, "step": 24, "density": 24}
+GRANT = {"forward": 16, "near": 8, "step": 12, "density": 24}
 
 
 def stages():
@@ -414,24 +420,25 @@
     mega = 1 << 20
     forward = call(
         forward_kernel,
-        (sds((coefs, width), BF16), sds((LOCAL * FG, width), BF16)),
+        (sds((coefs, width), BF16), sds((2, LOCAL * FG // 2, width), BF16)),
         [VM] * 3,
         [((2 * HB, width), F32), ((2 * LOCAL * HB, coefs), BF16)],
         2 * 10**9, 6 * mega, "forward",
     )
+    weigh = [
+        ((LOCAL * FG // 2, width), BF16),
+        ((FG // 2, FG * FG), F32),
+    ]
+    near = call(
+        near_kernel, sds((LOCAL * FG, coefs), BF16), [SM] + [VM] * 4, weigh,
+        2 * 10**9, 4 * mega, "near",
+    )
     step = call(
         step_kernel,
         (sds((LOCAL * HB, coefs), BF16), sds((2 * NB, coefs // 2), BF16)),
-        [SM, VM, ANY, ANY, VM, HBM, VM, VM, VM],
-        [
-            ((LOCAL * FG, width), BF16),
-            ((2 * LOCAL * FG, coefs), BF16),
-            ((2, FG // 2, FG * FG), F32),
-            ((2 * FG, FG * FG // 4), BF16),
-            ((2 * FG, FG * FG // 4), BF16),
-            ((coefs, width), BF16),
-        ],
-        4 * 10**9, 8 * mega, "step", 3,
+        [SM] + [VM] * 8,
+        [((LOCAL * FG, coefs), BF16)] + weigh,
+        2 * 10**9, 4 * mega, "step",
     )
     image = call(
         image_kernel, sds((LOCAL * FG, coefs + NB), BF16), [VM] * 2,
@@ -444,13 +451,8 @@
         [((NB, coefs), BF16), ((2 * NB, NB), BF16), ((2 * NB, coefs // 2), BF16)],
         2 * 10**8, 2 * mega, "gram", 2, (ANY, VM), {1: 0},
     )
-    total = pl.pallas_call(
-        sum_kernel,
-        grid=(1,),
-        out_shape=sds((NB, NB), F32),
-        in_specs=[pl.BlockSpec((2 * NB, NB), lambda i: (0, coefs // NB))],
-        out_specs=pl.BlockSpec((NB, NB), lambda i: (0, 0)),
-        name="total",
+    total = call(
+        sum_kernel, sds((NB, NB), F32), [VM], [], 10**6, mega // 8, "total",
     )
     newton = call(
         newton_kernel,
@@ -475,7 +477,7 @@
         last_kernel, sds((2, FG * FG), F32), [SM, SM, ANY],
         [((FG, LANES), F32), ((FRAGS, FG + 32, LANES), BF16)], 10**7, mega // 2, "last", 1,
     )
-    return forward, step, image, gram, total, newton, density, last
+    return forward, near, step, image, gram, total, newton, density, last
 
 
 def exchange(values, axis, groups=None):
@@ -486,13 +488,13 @@
 
 def per_device(bands_in, potential_in, hartree, patch_list):
     fwd_x, fwd_x_send, back_x, fwd_y, fwd_z, send = dft_tables()
-    forward, step, image, gram, total, newton, density, last = stages()
+    forward, near, step, image, gram, total, newton, density, last = stages()
     coefs = HB * 2 * QB
     groups = lax.axis_size("band")
     chips = groups // 2
     planes = FG // groups
     own = lax.axis_index("frag").astype(jnp.int32).reshape(1)
-    near = (lax.axis_index("band") & 1).astype(jnp.int32).reshape(1)
+    near_at = (lax.axis_index("band") & 1).astype(jnp.int32).reshape(1)
 
     pot = potential_in.astype(BF16).reshape(1, planes * 4, FG * FG // 4)
     along = [[2 * z + x for z in range(chips)] for x in (0, 1)]
@@ -501,8 +503,9 @@
     pot_far = lax.ppermute(pot_near, "band", [(i, i ^ 1) for i in range(groups)])
     bands = bands_in.reshape(LOCAL * HB, coefs)
     big_y, after_y = forward(bands, fwd_x, fwd_y)
+    near_rows = near(near_at, after_y, pot_near, big_y, fwd_z)
     stepped_own, stepped_send = step(
-        near, after_y, pot_near, pot_far, bands, big_y, fwd_z, back_x, send
+        near_at, after_y, pot_far, big_y, fwd_z, near_rows, bands, back_x, send
     )
     received = exchange(stepped_send.reshape(groups, 2 * LOCAL, coefs // 2), "band")
     image_send = image(stepped_own, fwd_x_send)

time: 187 us -> 188 us (level)
  blocking collectives: 85.5 us -> 55.2 us
  starting transfers between devices: 29.9 us -> 44.4 us
  waiting for transfers between devices: 35 us -> 49.2 us
  local copies, waits for them, and re-layouts: 6.88 us -> 11.7 us
  Pallas kernels: 27.2 us -> 24.8 us
    all_to_all x3 -> x2, blocking collectives: 85.5 us -> 55.2 us  [exchange(): lax.all_to_all(values, axis, split_axis=0, concat_axis=0, tiled=True, axi...]
    all_to_all x3 -> x4, starting transfers between devices: 26.8 us -> 41.2 us  [exchange(): lax.all_to_all(values, axis, split_axis=0, concat_axis=0, tiled=True, axi...]
    all_to_all x3 -> x4, waiting for transfers between devices: 35 us -> 49.2 us  [exchange(): lax.all_to_all(values, axis, split_axis=0, concat_axis=0, tiled=True, axi...]
    unnamed x23 -> x25, local copies, waits for them, and re-layouts: 3.94 us -> 8.09 us
    pallas_call x1 -> x2, Pallas kernels: 7.77 us -> 6.9 us  [the longest x1 4.04 us: per_device(): step(near_at, after_y, pot_far, big_y, fwd_z, near_rows, bands, back_x, s...]
  transfers between devices with their start and end apart: 4 -> 5, of which waited for: 3 -> 4; matrix products, arithmetic and copies ran while one was open for 2% -> 2% of each run, Pallas kernels for 6% -> 7%
where the time goes in v4:
time: 188 us; the launch traced here: 187 us
  blocking collectives  55.2 us (29%)
  waiting for transfers between devices  49.2 us (26%)
  starting transfers between devices  44.4 us (24%)
  Pallas kernels  24.8 us (13%)
  local copies, waits for them, and re-layouts  11.7 us (6%)
    all_to_all x2, blocking collectives, exchange(): lax.all_to_all(values, axis, split_axis=0, concat_axis=0, tiled=True, axi...  55.2 us
    all_to_all x4, waiting for transfers between devices, exchange(): lax.all_to_all(values, axis, split_axis=0, concat_axis=0, tiled=True, axi...  49.2 us
    all_to_all x4, starting transfers between devices, exchange(): lax.all_to_all(values, axis, split_axis=0, concat_axis=0, tiled=True, axi...  41.2 us
    unnamed x25, local copies, waits for them, and re-layouts  8.09 us
    pallas_call x1, Pallas kernels, per_device(): pieces = density(patch_list, own, parts, inverse, big_y, fwd_z, hartree)  7.79 us
    pallas_call x1, Pallas kernels, per_device(): step(near_at, after_y, pot_far, big_y, fwd_z, near_rows, bands, back_x, s...  4.04 us
    pallas_call x1, Pallas kernels, per_device(): phi, inverse = newton(whole, stepped)  4.01 us
  transfers between devices with their start and end apart: 5, of which 4 were waited for; matrix products, arithmetic and copies ran while one was open for 2% of the time, Pallas kernels for 7%

profile of v4, /device:TPU:1, one launch (start us, length us, event | category | flops | bytes accessed | tf_op | source)
XLA Modules:
  0.0 187.0 jit_solution(9564834291297958514)
XLA Ops:
  0.6 0.8 convert_element_type.30
  1.4 0.7 broadcast_in_dim.8
  2.1 0.0 copy-start.2
  2.2 15.9 %all-to-all-start = ((bf16[16,8,1024]{2,1,0:T(8,128)(2,1)}), bf16[16,8,1024]{2,1,0:T(8,128)(2,1)S(1)}, u32[]{:S(2)}, u32[]{:S(2)}) async-start(bf16[16,8,1024]{2,1,0:T(8,128)(2,1)} %broadcast_in_dim.8), calls=%async_computation | async-start | bytes 524288 | tf_op jit(solution)/shard_map/all_to_all | solution.py:484
  18.0 1.1 reshape.53.bands_ref
  19.2 12.6 %all-to-all-done = bf16[16,8,1024]{2,1,0:T(8,128)(2,1)S(1)} async-done(((bf16[16,8,1024]{2,1,0:T(8,128)(2,1)}), bf16[16,8,1024]{2,1,0:T(8,128)(2,1)S(1)}, u32[]{:S(2)}, u32[]{:S(2)}) %all-to-all-start) | async-done | bytes 262176 | tf_op jit(solution)/shard_map/all_to_all | solution.py:484
  31.8 3.1 %collective-permute-start = (bf16[128,1024]{1,0:T(8,128)(2,1)S(1)}, bf16[128,1024]{1,0:T(8,128)(2,1)S(1)}, u32[]{:S(2)}, u32[]{:S(2)}) collective-permute-start(bf16[128,1024]{1,0:T(8,128)(2,1)S(1)} %bitcast.19), channel_id=1, source_target_pairs={{0,1},{1,0},{2,3},{3,2},{4,5},{5,4},{6,7},{7,6},{8,9},{9,8},{10,11... | collective-permute-start | bytes 786440 | tf_op jit(solution)/shard_map/ppermute | solution.py:503
  34.9 0.0 copy-start.5
  34.9 0.9 copy-done.5
  35.8 0.0 copy-start.6
  35.8 0.7 copy-done.6
  36.5 2.8 %shard_map.113 = (bf16[1024,2048]{1,0:T(8,128)(2,1)S(1)}, bf16[2,128,2048]{2,1,0:T(8,128)(2,1)S(1)}) custom-call(bf16[128,1024]{1,0:T(8,128)(2,1)S(1)} %reshape.53.bands_ref, bf16[256,256]{1,0:T(8,128)(2,1)S(1)} %copy-done.5, bf16[64,128]{1,0:T(8,128)(2,1)S(1)} %copy-done.6), custom_call_target="tpu_custom_call" | custom-call | flops 2000000000 | bytes 6291456 | tf_op jit(solution)/shard_map/pallas_call | solution.py:505
  39.4 0.0 copy-start.7
  39.4 1.9 %copy-done.7 = bf16[1024,2048]{1,0:T(8,128)(2,1)} copy-done((bf16[1024,2048]{1,0:T(8,128)(2,1)}, bf16[1024,2048]{1,0:T(8,128)(2,1)S(1)}, u32[]{:S(2)}) %copy-start.7) | copy-done | bytes 4194328
  41.3 0.0 copy-start.3
  41.3 0.0 copy-done.2
  41.3 0.0 copy-start.8
  41.3 2.2 %copy-done.8 = bf16[1024,2048]{1,0:T(8,128)(2,1)S(1)} copy-done((bf16[1024,2048]{1,0:T(8,128)(2,1)S(1)}, bf16[1024,2048]{1,0:T(8,128)(2,1)}, u32[]{:S(2)}) %copy-start.8) | copy-done | bytes 4194328
  43.5 0.0 copy-start.9
  43.5 2.9 %shard_map.114.near_ref = bf16[256,1024]{1,0:T(8,128)(2,1)S(1)} custom-call(s32[1]{0:T(128)} %bitcast.1.near_at_ref, bf16[2,128,2048]{2,1,0:T(8,128)(2,1)S(1)} %get-tuple-element.12.after_y_ref, bf16[128,1024]{1,0:T(8,128)(2,1)S(1)} %bitcast.20, bf16[1024,2048]{1,0:T(8,128)(2,1)S(1)} %copy-done.8, bf16[128,512]{1,0:T(8,128)(2,1)S(1)} %copy-done.2), custom_call_target="tpu_custom_call" | custom-call | flops 2000000000 | bytes 4194304 | tf_op jit(solution)/shard_map/pallas_call | solution.py:506
  46.4 0.0 copy-start
  46.4 0.0 collective-permute-done.pot_ref
  46.4 0.0 copy-done.3
  46.4 0.0 copy-done.4
  46.5 0.0 copy-done.9
  46.5 4.0 %shard_map.115 = (bf16[128,1024]{1,0:T(8,128)(2,1)S(1)}, bf16[256,512]{1,0:T(8,128)(2,1)}) custom-call(s32[1]{0:T(128)} %bitcast.1.near_at_ref, bf16[2,128,2048]{2,1,0:T(8,128)(2,1)S(1)} %get-tuple-element.12.after_y_ref, bf16[128,1024]{1,0:T(8,128)(2,1)S(1)} %collective-permute-done.pot_ref, bf16[1024,2048]{1,0:T(8,128)(2,1)S(1)} %copy-done.9, ...), custom_call_target="tpu_custom_call" | custom-call | flops 2000000000 | bytes 4194304 | tf_op jit(solution)/shard_map/pallas_call | solution.py:507
  50.5 0.0 copy-start.11
  50.5 10.7 %all-to-all-start.1 = ((bf16[32,8,512]{2,1,0:T(8,128)(2,1)}), bf16[32,8,512]{2,1,0:T(8,128)(2,1)S(1)}, u32[]{:S(2)}, u32[]{:S(2)}) async-start(bf16[32,8,512]{2,1,0:T(8,128)(2,1)} %bitcast.3), calls=%async_computation.1 | async-start | bytes 524288 | tf_op jit(solution)/shard_map/all_to_all | solution.py:484
  61.3 0.0 copy-done
  61.3 0.4 shard_map.116.image_any
  61.7 19.6 %all-to-all-done.1 = bf16[32,8,512]{2,1,0:T(8,128)(2,1)S(1)} async-done(((bf16[32,8,512]{2,1,0:T(8,128)(2,1)}), bf16[32,8,512]{2,1,0:T(8,128)(2,1)S(1)}, u32[]{:S(2)}, u32[]{:S(2)}) %all-to-all-start.1) | async-done | bytes 262176 | tf_op jit(solution)/shard_map/all_to_all | solution.py:484
  81.3 1.0 shard_map.117
  82.3 37.8 %all_to_all.30 = bf16[32,8,1152]{2,1,0:T(8,128)(2,1)S(1)} all-to-all(bf16[32,8,1152]{2,1,0:T(8,128)(2,1)S(1)} %bitcast.14), channel_id=1, replica_groups=mesh['frag'=16,'band'=32] {'band'}, dimensions={0} | all-to-all | bytes 1179648 | tf_op jit(solution)/shard_map/all_to_all | solution.py:484
  120.2 17.4 %all_to_all.31 = f32[32,4,128]{2,1,0:T(4,128)S(1)} all-to-all(f32[32,4,128]{2,1,0:T(4,128)S(1)} %bitcast.18), channel_id=1, replica_groups=mesh['frag'=16,'band'=32] {'band'}, dimensions={0} | all-to-all | bytes 131072 | tf_op jit(solution)/shard_map/all_to_all | solution.py:484
  137.5 4.0 %shard_map.119 = (bf16[256,512]{1,0:T(8,128)(2,1)}, bf16[512,128]{1,0:T(8,128)(2,1)S(1)}) custom-call(f32[128,128]{1,0:T(8,128)S(1)} %bitcast.21, bf16[128,1024]{1,0:T(8,128)(2,1)S(1)} %get-tuple-element.17.stepped_ref), custom_call_target="tpu_custom_call" | custom-call | flops 1000000000 | bytes 1048576 | tf_op jit(solution)/shard_map/pallas_call | solution.py:515
  141.5 3.9 %all-to-all-start.4 = ((bf16[32,8,512]{2,1,0:T(8,128)(2,1)}), bf16[32,8,512]{2,1,0:T(8,128)(2,1)S(1)}, u32[]{:S(2)}, u32[]{:S(2)}) async-start(bf16[32,8,512]{2,1,0:T(8,128)(2,1)} %bitcast.9), calls=%async_computation.4 | async-start | bytes 524288 | tf_op jit(solution)/shard_map/all_to_all | solution.py:484
  145.4 0.0 copy-done.11
  145.4 0.1 copy.13.place_ref
  145.5 0.0 copy-done.1
  145.5 2.2 %copy-done.10 = bf16[1024,2048]{1,0:T(8,128)(2,1)S(1)} copy-done((bf16[1024,2048]{1,0:T(8,128)(2,1)S(1)}, bf16[1024,2048]{1,0:T(8,128)(2,1)}, u32[]{:S(2)}) %copy-start.10) | copy-done | bytes 4194328
  147.7 7.8 %shard_map.120 = bf16[16,96,128]{2,1,0:T(8,128)(2,1)} custom-call(s32[16,3]{1,0:T(8,128)S(1)} %copy.13.place_ref, s32[1]{0:T(128)} %bitcast.own_ref, bf16[256,1152]{1,0:T(8,128)(2,1)S(1)} %bitcast.16, bf16[512,128]{1,0:T(8,128)(2,1)S(1)} %get-tuple-element.18.inv_ref, bf16[1024,2048]{1,0:T(8,128)(2,1)S(1)} %copy-done.10, bf16[128,512]{1,0:T(8,128)(2,1)S(1)} %copy-done.2, ...), custom_call_target="tpu_custom_call" | custom-call | flops 4000000000 | bytes 6291456 | tf_op jit(solution)/shard_map/pallas_call | solution.py:517
  155.5 9.0 %all-to-all-done.4 = bf16[32,8,512]{2,1,0:T(8,128)(2,1)S(1)} async-done(((bf16[32,8,512]{2,1,0:T(8,128)(2,1)}), bf16[32,8,512]{2,1,0:T(8,128)(2,1)S(1)}, u32[]{:S(2)}, u32[]{:S(2)}) %all-to-all-start.4) | async-done | bytes 262176 | tf_op jit(solution)/shard_map/all_to_all | solution.py:484
  164.4 10.8 %all-to-all-start.5 = ((bf16[16,96,128]{2,1,0:T(8,128)(2,1)}), bf16[16,96,128]{2,1,0:T(8,128)(2,1)S(1)}, u32[]{:S(2)}, u32[]{:S(2)}) async-start(bf16[16,96,128]{2,1,0:T(8,128)(2,1)} %shard_map.120), calls=%async_computation.5 | async-start | bytes 786432 | tf_op jit(solution)/shard_map/all_to_all | solution.py:484
  175.2 0.2 reshape.69
  175.4 0.3 copy.17
  175.7 1.3 reshape.66
  177.0 8.0 %all-to-all-done.5.pieces_any = bf16[16,96,128]{2,1,0:T(8,128)(2,1)S(1)} async-done(((bf16[16,96,128]{2,1,0:T(8,128)(2,1)}), bf16[16,96,128]{2,1,0:T(8,128)(2,1)S(1)}, u32[]{:S(2)}, u32[]{:S(2)}) %all-to-all-start.5) | async-done | bytes 393248 | tf_op jit(solution)/shard_map/all_to_all | solution.py:484
  185.0 1.9 %shard_map.121 = f32[2,4096]{1,0:T(2,128)} custom-call(s32[16,3]{1,0:T(8,128)S(1)} %copy.13.place_ref, s32[1]{0:T(128)} %bitcast.own_ref, bf16[16,96,128]{2,1,0:T(8,128)(2,1)S(1)} %all-to-all-done.5.pieces_any), custom_call_target="tpu_custom_call" | custom-call | flops 10000000 | bytes 524288 | tf_op jit(solution)/shard_map/pallas_call | solution.py:519
  (5 shorter events, 0.1 us)
Async XLA Ops:
  2.1 39.2 %copy-start.2 = (bf16[128,512]{1,0:T(8,128)(2,1)S(1)}, bf16[128,512]{1,0:T(8,128)(2,1)}, u32[]{:S(2)}) copy-start(bf16[128,512]{1,0:T(8,128)(2,1)} %constant.34.fwd_z_ref) | copy-start | bytes 393220
  2.2 29.6 %all-to-all-start = ((bf16[16,8,1024]{2,1,0:T(8,128)(2,1)}), bf16[16,8,1024]{2,1,0:T(8,128)(2,1)S(1)}, u32[]{:S(2)}, u32[]{:S(2)}) async-start(bf16[16,8,1024]{2,1,0:T(8,128)(2,1)} %broadcast_in_dim.8), calls=%async_computation | async-start | bytes 524288 | tf_op jit(solution)/shard_map/all_to_all | solution.py:484
  31.8 14.6 %collective-permute-start = (bf16[128,1024]{1,0:T(8,128)(2,1)S(1)}, bf16[128,1024]{1,0:T(8,128)(2,1)S(1)}, u32[]{:S(2)}, u32[]{:S(2)}) collective-permute-start(bf16[128,1024]{1,0:T(8,128)(2,1)S(1)} %bitcast.19), channel_id=1, source_target_pairs={{0,1},{1,0},{2,3},{3,2},{4,5},{5,4},{6,7},{7,6},{8,9},{9,8},{10,11... | collective-permute-start | bytes 786440 | tf_op jit(solution)/shard_map/ppermute | solution.py:503
  34.9 0.9 copy-start.5
  35.8 0.7 copy-start.6
  39.4 1.9 %copy-start.7 = (bf16[1024,2048]{1,0:T(8,128)(2,1)}, bf16[1024,2048]{1,0:T(8,128)(2,1)S(1)}, u32[]{:S(2)}) copy-start(bf16[1024,2048]{1,0:T(8,128)(2,1)S(1)} %get-tuple-element.13.big_y_ref) | copy-start | bytes 12582916
  41.3 5.1 %copy-start.3 = (bf16[2,128,256]{2,1,0:T(8,128)(2,1)S(1)}, bf16[2,128,256]{2,1,0:T(8,128)(2,1)}, u32[]{:S(2)}) copy-start(bf16[2,128,256]{2,1,0:T(8,128)(2,1)} %constant.35.back_x_ref) | copy-start | bytes 393220
  41.3 5.1 %copy-start.4 = (bf16[256,256]{1,0:T(8,128)(2,1)S(1)}, bf16[256,256]{1,0:T(8,128)(2,1)}, u32[]{:S(2)}) copy-start(bf16[256,256]{1,0:T(8,128)(2,1)} %constant.36.send_ref) | copy-start | bytes 393220
  41.3 2.2 %copy-start.8 = (bf16[1024,2048]{1,0:T(8,128)(2,1)S(1)}, bf16[1024,2048]{1,0:T(8,128)(2,1)}, u32[]{:S(2)}) copy-start(bf16[1024,2048]{1,0:T(8,128)(2,1)} %copy-done.7) | copy-start | bytes 12582916
  43.5 2.9 %copy-start.9 = (bf16[1024,2048]{1,0:T(8,128)(2,1)S(1)}, bf16[1024,2048]{1,0:T(8,128)(2,1)}, u32[]{:S(2)}) copy-start(bf16[1024,2048]{1,0:T(8,128)(2,1)} %copy-done.7) | copy-start | bytes 12582916
  46.4 14.8 %copy-start = (bf16[256,256]{1,0:T(8,128)(2,1)S(1)}, bf16[256,256]{1,0:T(8,128)(2,1)}, u32[]{:S(2)}) copy-start(bf16[256,256]{1,0:T(8,128)(2,1)} %constant.37.fwd_x_ref) | copy-start | bytes 393220
  50.5 94.9 %copy-start.11 = (s32[16,3]{0,1:T(4,128)S(1)}, s32[16,3]{0,1:T(4,128)}, u32[]{:S(2)}) copy-start(s32[16,3]{0,1:T(4,128)} %param.13) | copy-start | bytes 580
  50.5 95.0 %copy-start.1 = (f32[2,8,128]{2,1,0:T(8,128)S(1)}, f32[2,8,128]{2,1,0:T(8,128)}, u32[]{:S(2)}) copy-start(f32[2,8,128]{2,1,0:T(8,128)} %tile_ref.1) | copy-start | bytes 24580
  50.5 30.8 %all-to-all-start.1 = ((bf16[32,8,512]{2,1,0:T(8,128)(2,1)}), bf16[32,8,512]{2,1,0:T(8,128)(2,1)S(1)}, u32[]{:S(2)}, u32[]{:S(2)}) async-start(bf16[32,8,512]{2,1,0:T(8,128)(2,1)} %bitcast.3), calls=%async_computation.1 | async-start | bytes 524288 | tf_op jit(solution)/shard_map/all_to_all | solution.py:484
  141.5 22.9 %all-to-all-start.4 = ((bf16[32,8,512]{2,1,0:T(8,128)(2,1)}), bf16[32,8,512]{2,1,0:T(8,128)(2,1)S(1)}, u32[]{:S(2)}, u32[]{:S(2)}) async-start(bf16[32,8,512]{2,1,0:T(8,128)(2,1)} %bitcast.9), calls=%async_computation.4 | async-start | bytes 524288 | tf_op jit(solution)/shard_map/all_to_all | solution.py:484
  145.5 2.2 %copy-start.10 = (bf16[1024,2048]{1,0:T(8,128)(2,1)S(1)}, bf16[1024,2048]{1,0:T(8,128)(2,1)}, u32[]{:S(2)}) copy-start(bf16[1024,2048]{1,0:T(8,128)(2,1)} %copy-done.7) | copy-start | bytes 12582916
  164.4 20.5 %all-to-all-start.5 = ((bf16[16,96,128]{2,1,0:T(8,128)(2,1)}), bf16[16,96,128]{2,1,0:T(8,128)(2,1)S(1)}, u32[]{:S(2)}, u32[]{:S(2)}) async-start(bf16[16,96,128]{2,1,0:T(8,128)(2,1)} %shard_map.120), calls=%async_computation.5 | async-start | bytes 786432 | tf_op jit(solution)/shard_map/all_to_all | solution.py:484

commit v5 on v4

--- a/solution.py
+++ b/solution.py
@@ -41,12 +41,11 @@
     cos_z, sin_z = np.cos(turn_z), np.sin(turn_z)
     same = np.eye(LOCAL)
     fwd_x = np.stack([np.einsum("ab,xk->axbk", same, t) for t in (cos_xy, sin_xy)], axis=2)
-    fwd_x = fwd_x.reshape(LOCAL, FG // 4, 2, 2, 2 * LOCAL * HB)
-    fwd_x_send = fwd_x.transpose(1, 2, 3, 0, 4).reshape(LOCAL * FG, -1)
-    fwd_x = fwd_x.transpose(2, 0, 1, 3, 4).reshape(LOCAL * FG, -1)
+    fwd_x = fwd_x.reshape(LOCAL * FG, 2 * LOCAL * HB)
+    fwd_x_send = fwd_x.reshape(LOCAL, FG // 2, 2, -1).transpose(1, 2, 0, 3)
+    fwd_x_send = fwd_x_send.reshape(LOCAL * FG, -1)
     back_x = np.stack([np.einsum("ab,xk->akbx", same, t) for t in (cos_xy, -sin_xy)], axis=2)
-    back_x = back_x.reshape(LOCAL * HB, 2, LOCAL, FG // 4, 2, 2).transpose(4, 0, 1, 2, 3, 5)
-    back_x = back_x.reshape(2, LOCAL * HB, LOCAL * FG)
+    back_x = back_x.reshape(LOCAL * HB, 2 * LOCAL * FG)
     fwd_y = np.stack(
         [np.stack([cos_xy.T, sin_xy.T], axis=2), np.stack([-sin_xy.T, cos_xy.T], axis=2)], axis=1
     ).reshape(2 * HB, 2 * FG)
@@ -90,7 +89,8 @@
 
 def forward_kernel(bands_ref, fwd_x_ref, fwd_y_ref, big_y_ref, out_ref, rows_ref, stack_ref):
     width = FG * 2 * QB
-    spread = (iota((2 * FG, width), 1) // QB == iota((2 * FG, width), 0)).astype(F32).astype(BF16)
+    half_w = width // 2
+    spread = onehot(iota((2 * FG, width), 1) // QB == iota((2 * FG, width), 0))
     rows_ref[...] = dot(fwd_y_ref[...], spread)
     same = iota((QB, width), 1) % QB == iota((QB, width), 0)
 
@@ -98,7 +98,10 @@
     def _(row):
         line = jnp.broadcast_to(rows_ref[pl.ds(row, 1), :], (QB, width))
         start = pl.multiple_of(row * QB, QB)
-        big_y_ref[pl.ds(start, QB), :] = jnp.where(same, line, 0.0).astype(BF16)
+        lines = jnp.where(same, line, 0.0).astype(BF16)
+        for at in range(8):
+            block = lines[:, at * 256 : (at + 1) * 256]
+            big_y_ref[at % 2, pl.ds(start, QB), at // 2 * 256 : (at // 2 + 1) * 256] = block
 
     rows_n = LOCAL * HB
     stack_ref[:rows_n, :] = bands_ref[...]
@@ -106,14 +109,10 @@
         block = bands_ref[:, start : start + LANES].astype(F32)
         stack_ref[rows_n:, start : start + LANES] = times_i(block).astype(BF16)
     after_x = dot(fwd_x_ref[...], stack_ref[...]).astype(BF16)
-    half_n = LOCAL * FG // 2
-
-    @pl.loop(0, width // 512, unroll=4)
-    def _(at):
-        span = pl.ds(pl.multiple_of(at * 512, 512), 512)
-        block = dot(after_x, big_y_ref[:, span]).astype(BF16)
-        out_ref[0, :, span] = block[:half_n]
-        out_ref[1, :, span] = block[half_n:]
+    for half in (0, 1):
+        for start in range(0, half_w, 512):
+            span = slice(start, start + 512)
+            out_ref[half, :, span] = dot(after_x, big_y_ref[half, :, span]).astype(BF16)
 
 
 def spread_parts(pair):
@@ -122,55 +121,51 @@
     return jnp.where(low, pair, turned), jnp.where(low, turned, pair)
 
 
-def weigh_rows(at_half, after_y_ref, pot_ref, big_y_ref, fwd_z_ref, stack_ref, back_ref, pots_ref):
+def weigh_half(half, after_y_ref, pot_ref, fwd_z_ref, back_ref, pots_ref):
     fwd_z = fwd_z_ref[...]
-    quarter = FG * FG // 4
-    pick_shape = (FG // 2, 2 * FG)
+    quarter = FG * FG // 8
+    pick_shape = (FG, LOCAL * FG)
     for at in range(4):
         pick = onehot(iota(pick_shape, 0) * 4 + at == iota(pick_shape, 1))
         pots_ref[:, at * quarter : (at + 1) * quarter] = dot(pick, pot_ref[...])
 
-    for at in range(FG // LOCAL):
+    for at in range(FG // LOCAL // 2):
         span = slice(at * LANES, (at + 1) * LANES)
-        grid_vals = dot(after_y_ref[at_half, :, span], fwd_z) * (4.0 / FG**1.5)
+        grid_vals = dot(after_y_ref[half, :, span], fwd_z) * (4.0 / FG**1.5)
         pot = pots_ref[:, at * 2 * LANES : (at + 1) * 2 * LANES]
         parts = [*spread_parts(pot[:, :LANES]), *spread_parts(pot[:, LANES:])]
         pots = jnp.concatenate([jnp.concatenate(parts, axis=1)] * LOCAL, axis=0)
         back_ref[:, span] = dot_t((grid_vals * pots).astype(BF16), fwd_z).astype(BF16)
 
-    rows_n = LOCAL * FG // 2
+
+def near_kernel(
+    near_at_ref, after_y_ref, pot_ref, big_y_ref, fwd_z_ref, sum_ref, back_ref, pots_ref
+):
+    near = near_at_ref[0]
+    weigh_half(near, after_y_ref, pot_ref, fwd_z_ref, back_ref, pots_ref)
     block_n = 2 * LANES
     for start in range(0, HB * 2 * QB, block_n):
         span = slice(start, start + block_n)
-        block = dot_t(back_ref[...], big_y_ref[span, :])
+        sum_ref[:, span] = dot_t(back_ref[...], big_y_ref[near, span, :])
+
+
+def step_kernel(
+    near_at_ref, after_y_ref, pot_ref, big_y_ref, fwd_z_ref, sum_ref, bands_ref, back_x_ref,
+    send_ref, stepped_ref, sent_ref, stack_ref, back_ref, pots_ref,
+):
+    far = 1 - near_at_ref[0]
+    weigh_half(far, after_y_ref, pot_ref, fwd_z_ref, back_ref, pots_ref)
+    rows_n = LOCAL * FG
+    half_n = LOCAL * HB
+    block_n = 2 * LANES
+    for start in range(0, HB * 2 * QB, block_n):
+        span = slice(start, start + block_n)
+        block = sum_ref[:, span] + dot_t(back_ref[...], big_y_ref[far, span, :])
         stack_ref[:rows_n, span] = block.astype(BF16)
         for low in range(start, start + block_n, LANES):
             turned = times_i(block[:, low - start : low - start + LANES])
             stack_ref[rows_n:, low : low + LANES] = turned.astype(BF16)
-
-
-def near_kernel(
-    near_at_ref, after_y_ref, pot_ref, big_y_ref, fwd_z_ref, stack_ref, back_ref, pots_ref
-):
-    weigh_rows(
-        near_at_ref[0], after_y_ref, pot_ref, big_y_ref, fwd_z_ref, stack_ref, back_ref, pots_ref
-    )
-
-
-def step_kernel(
-    near_at_ref, after_y_ref, pot_ref, big_y_ref, fwd_z_ref, near_ref, bands_ref, back_x_ref,
-    send_ref, stepped_ref, sent_ref, stack_ref, back_ref, pots_ref,
-):
-    near = near_at_ref[0]
-    weigh_rows(
-        1 - near, after_y_ref, pot_ref, big_y_ref, fwd_z_ref, stack_ref, back_ref, pots_ref
-    )
-    half_n = LOCAL * HB
-    block_n = 2 * LANES
-    for start in range(0, HB * 2 * QB, block_n):
-        span = slice(start, start + block_n)
-        image = dot(back_x_ref[near], near_ref[:, span])
-        image = (image + dot(back_x_ref[1 - near], stack_ref[:, span])) * (0.25 / FG**1.5)
+        image = dot(back_x_ref[...], stack_ref[:, span]) * (0.25 / FG**1.5)
         shape = (half_n, block_n)
         row, lane = iota(shape, 0), iota(shape, 1) + start
         mx, my = row % HB - HB // 2, lane // (2 * QB) - HB // 2
@@ -313,12 +308,13 @@
     )
     both = dot(left, stack_ref[...])
     phi_ref[...] = (both[:rows_n] + both[rows_n:]).astype(BF16)
-    width = FG * 2 * QB
-
-    @pl.loop(0, width // 512, unroll=4)
-    def _(at):
-        span = pl.ds(pl.multiple_of(at * 512, 512), 512)
-        after_y_ref[:, span] = dot(phi_ref[...], big_y_ref[:, span]).astype(BF16)
+    half_w = FG * QB
+    for half in (0, 1):
+        for start in range(0, half_w, 512):
+            block = dot(phi_ref[...], big_y_ref[half, :, start : start + 512])
+            for low in (0, 256):
+                at = (start + low) * 2 + half * 256
+                after_y_ref[:, at : at + 256] = block[:, low : low + 256].astype(BF16)
 
     low = iota((1, LANES), 1) < FG
 
@@ -345,6 +341,7 @@
     same_plane = row // FG == col // FG
     rows_shape = (FG, FG)
     rows_row, rows_col = iota(rows_shape, 0), iota(rows_shape, 1)
+    tiles = [jnp.concatenate(halves(tile_ref[plane]), axis=0) for plane in (0, 1)]
     for to in range(FRAGS):
         shift_y = place_ref[to, 1] - own_y + GY
         shift_z = place_ref[to, 2] - own_z + GZ
@@ -352,30 +349,29 @@
         moved = dot(dens, cols.astype(F32).astype(BF16)).astype(BF16)
         rows = (rows_row + shift_y) % GY == rows_col
         out_ref[to, :FG, :] = dot(rows.astype(F32).astype(BF16), moved).astype(BF16)
-        for at, part in enumerate(halves(tile_ref[...].reshape(2 * 8, GZ))):
-            out_ref[to, FG + at * 16 : FG + (at + 1) * 16, :] = part
+        to_z = place_ref[to, 2]
+        tile = jnp.zeros((2 * 8, LANES), F32)
+        for plane in (0, 1):
+            cols = onehot((col // FG == plane) & ((col % FG + to_z) % GZ == row))
+            tile += dot(tiles[plane], cols)
+        out_ref[to, FG:, :] = tile.astype(BF16)
 
 
 def last_kernel(place_ref, own_ref, pieces_any, out_ref, total_ref, pieces_ref, sem):
     pieces_copy = pltpu.make_async_copy(pieces_any, pieces_ref, sem)
     pieces_copy.start()
     own = own_ref[0]
-    own_y, own_z = place_ref[own, 1], place_ref[own, 2]
+    own_y = place_ref[own, 1]
     pieces_copy.wait()
     patched = jnp.zeros((FG, LANES), F32)
     for at in range(FRAGS):
         patched += pieces_ref[at, :FG, :].astype(F32)
     rows = onehot((iota((FG, GY), 0) + own_y) % GY == iota((FG, GY), 1))
-    shape = (GZ, LANES)
-    row, col = iota(shape, 0), iota(shape, 1)
+    tiles = pieces_ref[:, FG:, :].astype(F32)
     total = jnp.zeros((FG, LANES), F32)
-    tiles = pieces_ref[:, FG:, :].astype(F32)
-    for plane in (0, 1):
-        cols = onehot((col // FG == plane) & ((col % FG + own_z) % GZ == row))
-        for part in (0, 1):
-            start = part * 16 + plane * 8
-            tile = tiles[:, start : start + 8, :].reshape(GY, GZ).astype(BF16)
-            total += dot(dot(rows, tile).astype(BF16), cols)
+    for part in (0, 1):
+        tile = tiles[:, part * 8 : (part + 1) * 8, :].reshape(GY, LANES)
+        total += dot(rows, tile.astype(BF16))
     power = jnp.exp(jnp.log(patched * patched + SOFTEN) * (-1.0 / 3.0))
     total_ref[...] = total - SLATER * patched * power
     even = total_ref[pl.ds(0, FG // 2, stride=2), :]
@@ -411,7 +407,7 @@
     )
 
 
-GRANT = {"forward": 16, "near": 8, "step": 12, "density": 24}
+GRANT = {"forward": 16, "near": 8, "step": 10, "density": 24}
 
 
 def stages():
@@ -420,24 +416,24 @@
     mega = 1 << 20
     forward = call(
         forward_kernel,
-        (sds((coefs, width), BF16), sds((2, LOCAL * FG // 2, width), BF16)),
+        (sds((2, coefs, width // 2), BF16), sds((2, LOCAL * FG, width // 2), BF16)),
         [VM] * 3,
         [((2 * HB, width), F32), ((2 * LOCAL * HB, coefs), BF16)],
         2 * 10**9, 6 * mega, "forward",
     )
     weigh = [
-        ((LOCAL * FG // 2, width), BF16),
-        ((FG // 2, FG * FG), F32),
+        ((LOCAL * FG, width // 2), BF16),
+        ((FG, FG * FG // 2), F32),
     ]
     near = call(
-        near_kernel, sds((LOCAL * FG, coefs), BF16), [SM] + [VM] * 4, weigh,
+        near_kernel, sds((LOCAL * FG, coefs), F32), [SM] + [VM] * 4, weigh,
         2 * 10**9, 4 * mega, "near",
     )
     step = call(
         step_kernel,
         (sds((LOCAL * HB, coefs), BF16), sds((2 * NB, coefs // 2), BF16)),
         [SM] + [VM] * 8,
-        [((LOCAL * FG, coefs), BF16)] + weigh,
+        [((2 * LOCAL * FG, coefs), BF16)] + weigh,
         2 * 10**9, 4 * mega, "step",
     )
     image = call(
@@ -463,7 +459,7 @@
     )
     density = call(
         density_kernel,
-        sds((FRAGS, FG + 32, LANES), BF16),
+        sds((FRAGS, FG + 16, LANES), BF16),
         [SM, SM] + [VM] * 5,
         [
             ((4 * NB, coefs), BF16),
@@ -475,15 +471,13 @@
     )
     last = call(
         last_kernel, sds((2, FG * FG), F32), [SM, SM, ANY],
-        [((FG, LANES), F32), ((FRAGS, FG + 32, LANES), BF16)], 10**7, mega // 2, "last", 1,
+        [((FG, LANES), F32), ((FRAGS, FG + 16, LANES), BF16)], 10**7, mega // 2, "last", 1,
     )
     return forward, near, step, image, gram, total, newton, density, last
 
 
-def exchange(values, axis, groups=None):
-    return lax.all_to_all(
-        values, axis, split_axis=0, concat_axis=0, tiled=True, axis_index_groups=groups
-    )
+def exchange(values, axis):
+    return lax.all_to_all(values, axis, split_axis=0, concat_axis=0, tiled=True)
 
 
 def per_device(bands_in, potential_in, hartree, patch_list):
@@ -496,10 +490,10 @@
     own = lax.axis_index("frag").astype(jnp.int32).reshape(1)
     near_at = (lax.axis_index("band") & 1).astype(jnp.int32).reshape(1)
 
-    pot = potential_in.astype(BF16).reshape(1, planes * 4, FG * FG // 4)
-    along = [[2 * z + x for z in range(chips)] for x in (0, 1)]
-    pot_near = exchange(jnp.broadcast_to(pot, (chips, *pot.shape[1:])), "band", along)
-    pot_near = pot_near.reshape(2 * FG, FG * FG // 4)
+    pot = potential_in.astype(BF16).reshape(planes * 4, FG * FG // 4)
+    pot = jnp.stack([pot[:, : FG * FG // 8], pot[:, FG * FG // 8 :]])[None]
+    pot = jnp.broadcast_to(pot, (chips, *pot.shape[1:])).reshape(groups, *pot.shape[2:])
+    pot_near = exchange(pot, "band").reshape(4 * FG, FG * FG // 8)
     pot_far = lax.ppermute(pot_near, "band", [(i, i ^ 1) for i in range(groups)])
     bands = bands_in.reshape(LOCAL * HB, coefs)
     big_y, after_y = forward(bands, fwd_x, fwd_y)

time: 188 us -> 186 us (0.989)
  starting transfers between devices: 44.4 us -> 38.4 us
  waiting for transfers between devices: 49.2 us -> 54 us
    all_to_all x4, starting transfers between devices: 41.2 us -> 36.1 us  [exchange(): return lax.all_to_all(values, axis, split_axis=0, concat_axis=0, tiled=True)]
    all_to_all x4, waiting for transfers between devices: 49.2 us -> 54 us  [exchange(): return lax.all_to_all(values, axis, split_axis=0, concat_axis=0, tiled=True)]
where the time goes in v5:
time: 186 us
  blocking collectives  55.9 us (30%)
  waiting for transfers between devices  54 us (29%)
  starting transfers between devices  38.4 us (21%)
  Pallas kernels  23.7 us (13%)
  local copies, waits for them, and re-layouts  11.7 us (6%)
    all_to_all x2, blocking collectives, exchange(): return lax.all_to_all(values, axis, split_axis=0, concat_axis=0, tiled=True)  55.9 us
    all_to_all x4, waiting for transfers between devices, exchange(): return lax.all_to_all(values, axis, split_axis=0, concat_axis=0, tiled=True)  54 us
    all_to_all x4, starting transfers between devices, exchange(): return lax.all_to_all(values, axis, split_axis=0, concat_axis=0, tiled=True)  36.1 us
    unnamed x25, local copies, waits for them, and re-layouts  8.08 us
    pallas_call x1, Pallas kernels, per_device(): pieces = density(patch_list, own, parts, inverse, big_y, fwd_z, hartree)  6.98 us
    pallas_call x1, Pallas kernels, per_device(): step(near_at, after_y, pot_far, big_y, fwd_z, near_rows, bands, back_x, s...  4.71 us
    pallas_call x1, Pallas kernels, per_device(): phi, inverse = newton(whole, stepped)  4.01 us
  transfers between devices with their start and end apart: 5, of which 4 were waited for; matrix products, arithmetic and copies ran while one was open for 2% of the time, Pallas kernels for 7%

profile of v5, /device:TPU:1, one launch (start us, length us, event | category | flops | bytes accessed | tf_op | source)
XLA Modules:
  0.0 185.5 jit_solution(4546855504823907190)
XLA Ops:
  0.6 0.8 convert_element_type.30
  1.4 0.7 broadcast_in_dim.2
  2.2 17.1 %all-to-all-start = ((bf16[32,8,512]{2,1,0:T(8,128)(2,1)}), bf16[32,8,512]{2,1,0:T(8,128)(2,1)S(1)}, u32[]{:S(2)}, u32[]{:S(2)}) async-start(bf16[32,8,512]{2,1,0:T(8,128)(2,1)} %bitcast.4), calls=%async_computation | async-start | bytes 524288 | tf_op jit(solution)/shard_map/all_to_all | solution.py:480
  19.3 1.1 reshape.58.bands_ref
  20.4 19.3 %all-to-all-done = bf16[32,8,512]{2,1,0:T(8,128)(2,1)S(1)} async-done(((bf16[32,8,512]{2,1,0:T(8,128)(2,1)}), bf16[32,8,512]{2,1,0:T(8,128)(2,1)S(1)}, u32[]{:S(2)}, u32[]{:S(2)}) %all-to-all-start) | async-done | bytes 262176 | tf_op jit(solution)/shard_map/all_to_all | solution.py:480
  39.7 2.3 %collective-permute-start = (bf16[256,512]{1,0:T(8,128)(2,1)S(1)}, bf16[256,512]{1,0:T(8,128)(2,1)S(1)}, u32[]{:S(2)}, u32[]{:S(2)}) collective-permute-start(bf16[256,512]{1,0:T(8,128)(2,1)S(1)} %bitcast.24), channel_id=1, source_target_pairs={{0,1},{1,0},{2,3},{3,2},{4,5},{5,4},{6,7},{7,6},{8,9},{9,8},{10,11... | collective-permute-start | bytes 786440 | tf_op jit(solution)/shard_map/ppermute | solution.py:497
  42.0 0.0 copy-start.5
  42.0 0.9 copy-done.5
  42.9 0.0 copy-start.6
  42.9 0.7 copy-done.6
  43.6 2.8 %shard_map.113 = (bf16[2,1024,1024]{2,1,0:T(8,128)(2,1)S(1)}, bf16[2,256,1024]{2,1,0:T(8,128)(2,1)S(1)}) custom-call(bf16[128,1024]{1,0:T(8,128)(2,1)S(1)} %reshape.58.bands_ref, bf16[256,256]{1,0:T(8,128)(2,1)S(1)} %copy-done.5, bf16[64,128]{1,0:T(8,128)(2,1)S(1)} %copy-done.6), custom_call_target="tpu_custom_call" | custom-call | flops 2000000000 | bytes 6291456 | tf_op jit(solution)/shard_map/pallas_call | solution.py:499
  46.4 0.0 copy-start.7
  46.4 1.9 %copy-done.7 = bf16[2,1024,1024]{2,1,0:T(8,128)(2,1)} copy-done((bf16[2,1024,1024]{2,1,0:T(8,128)(2,1)}, bf16[2,1024,1024]{2,1,0:T(8,128)(2,1)S(1)}, u32[]{:S(2)}) %copy-start.7) | copy-done | bytes 4194328
  48.3 0.0 copy-start.3
  48.3 0.0 copy-start.4
  48.3 0.0 copy-done.2
  48.3 0.0 copy-start.8
  48.3 2.2 %copy-done.8 = bf16[2,1024,1024]{2,1,0:T(8,128)(2,1)S(1)} copy-done((bf16[2,1024,1024]{2,1,0:T(8,128)(2,1)S(1)}, bf16[2,1024,1024]{2,1,0:T(8,128)(2,1)}, u32[]{:S(2)}) %copy-start.8) | copy-done | bytes 4194328
  50.6 0.0 copy-start.9
  50.6 2.2 %shard_map.114.sum_ref = f32[256,1024]{1,0:T(8,128)S(1)} custom-call(s32[1]{0:T(128)} %bitcast.1.near_at_ref, bf16[2,256,1024]{2,1,0:T(8,128)(2,1)S(1)} %get-tuple-element.12.after_y_ref, bf16[256,512]{1,0:T(8,128)(2,1)S(1)} %bitcast.25, bf16[2,1024,1024]{2,1,0:T(8,128)(2,1)S(1)} %copy-done.8, bf16[128,512]{1,0:T(8,128)(2,1)S(1)} %copy-done.2), custom_call_target="tpu_custom_call" | custom-call | flops 2000000000 | bytes 4194304 | tf_op jit(solution)/shard_map/pallas_call | solution.py:500
  52.7 0.0 copy-start
  52.7 0.0 collective-permute-done.pot_ref
  52.7 0.0 copy-done.3
  52.8 0.0 copy-done.4
  52.8 0.0 copy-done.9
  52.8 4.7 %shard_map.115 = (bf16[128,1024]{1,0:T(8,128)(2,1)S(1)}, bf16[256,512]{1,0:T(8,128)(2,1)}) custom-call(s32[1]{0:T(128)} %bitcast.1.near_at_ref, bf16[2,256,1024]{2,1,0:T(8,128)(2,1)S(1)} %get-tuple-element.12.after_y_ref, bf16[256,512]{1,0:T(8,128)(2,1)S(1)} %collective-permute-done.pot_ref, bf16[2,1024,1024]{2,1,0:T(8,128)(2,1)S(1)} %copy-done.9, ...), custom_call_target="tpu_custom_call" | custom-call | flops 2000000000 | bytes 4194304 | tf_op jit(solution)/shard_map/pallas_call | solution.py:501
  57.5 0.0 copy-start.11
  57.5 4.5 %all-to-all-start.1 = ((bf16[32,8,512]{2,1,0:T(8,128)(2,1)}), bf16[32,8,512]{2,1,0:T(8,128)(2,1)S(1)}, u32[]{:S(2)}, u32[]{:S(2)}) async-start(bf16[32,8,512]{2,1,0:T(8,128)(2,1)} %bitcast.6), calls=%async_computation.1 | async-start | bytes 524288 | tf_op jit(solution)/shard_map/all_to_all | solution.py:480
  62.0 0.0 copy-done
  62.0 0.4 shard_map.116.image_any
  62.4 17.8 %all-to-all-done.1 = bf16[32,8,512]{2,1,0:T(8,128)(2,1)S(1)} async-done(((bf16[32,8,512]{2,1,0:T(8,128)(2,1)}), bf16[32,8,512]{2,1,0:T(8,128)(2,1)S(1)}, u32[]{:S(2)}, u32[]{:S(2)}) %all-to-all-start.1) | async-done | bytes 262176 | tf_op jit(solution)/shard_map/all_to_all | solution.py:480
  80.2 1.0 shard_map.117
  81.2 38.3 %all_to_all.30 = bf16[32,8,1152]{2,1,0:T(8,128)(2,1)S(1)} all-to-all(bf16[32,8,1152]{2,1,0:T(8,128)(2,1)S(1)} %bitcast.19), channel_id=1, replica_groups=mesh['frag'=16,'band'=32] {'band'}, dimensions={0} | all-to-all | bytes 1179648 | tf_op jit(solution)/shard_map/all_to_all | solution.py:480
  119.5 17.6 %all_to_all.31 = f32[32,4,128]{2,1,0:T(4,128)S(1)} all-to-all(f32[32,4,128]{2,1,0:T(4,128)S(1)} %bitcast.23), channel_id=1, replica_groups=mesh['frag'=16,'band'=32] {'band'}, dimensions={0} | all-to-all | bytes 131072 | tf_op jit(solution)/shard_map/all_to_all | solution.py:480
  137.1 4.0 %shard_map.119 = (bf16[256,512]{1,0:T(8,128)(2,1)}, bf16[512,128]{1,0:T(8,128)(2,1)S(1)}) custom-call(f32[128,128]{1,0:T(8,128)S(1)} %bitcast.26, bf16[128,1024]{1,0:T(8,128)(2,1)S(1)} %get-tuple-element.17.stepped_ref), custom_call_target="tpu_custom_call" | custom-call | flops 1000000000 | bytes 1048576 | tf_op jit(solution)/shard_map/pallas_call | solution.py:509
  141.1 3.9 %all-to-all-start.4 = ((bf16[32,8,512]{2,1,0:T(8,128)(2,1)}), bf16[32,8,512]{2,1,0:T(8,128)(2,1)S(1)}, u32[]{:S(2)}, u32[]{:S(2)}) async-start(bf16[32,8,512]{2,1,0:T(8,128)(2,1)} %bitcast.12), calls=%async_computation.4 | async-start | bytes 524288 | tf_op jit(solution)/shard_map/all_to_all | solution.py:480
  145.0 0.0 copy-done.11
  145.0 0.1 copy.13.place_ref
  145.1 0.0 copy-done.1
  145.1 2.2 %copy-done.10 = bf16[2,1024,1024]{2,1,0:T(8,128)(2,1)S(1)} copy-done((bf16[2,1024,1024]{2,1,0:T(8,128)(2,1)S(1)}, bf16[2,1024,1024]{2,1,0:T(8,128)(2,1)}, u32[]{:S(2)}) %copy-start.10) | copy-done | bytes 4194328
  147.3 7.0 %shard_map.120 = bf16[16,80,128]{2,1,0:T(8,128)(2,1)} custom-call(s32[16,3]{1,0:T(8,128)S(1)} %copy.13.place_ref, s32[1]{0:T(128)} %bitcast.own_ref, bf16[256,1152]{1,0:T(8,128)(2,1)S(1)} %bitcast.21, bf16[512,128]{1,0:T(8,128)(2,1)S(1)} %get-tuple-element.18.inv_ref, bf16[2,1024,1024]{2,1,0:T(8,128)(2,1)S(1)} %copy-done.10, bf16[128,512]{1,0:T(8,128)(2,1)S(1)} %copy-done.2, ...), custom_call_target="tpu_custom_call" | custom-call | flops 4000000000 | bytes 6291456 | tf_op jit(solution)/shard_map/pallas_call | solution.py:511
  154.3 9.6 %all-to-all-done.4 = bf16[32,8,512]{2,1,0:T(8,128)(2,1)S(1)} async-done(((bf16[32,8,512]{2,1,0:T(8,128)(2,1)}), bf16[32,8,512]{2,1,0:T(8,128)(2,1)S(1)}, u32[]{:S(2)}, u32[]{:S(2)}) %all-to-all-start.4) | async-done | bytes 262176 | tf_op jit(solution)/shard_map/all_to_all | solution.py:480
  163.9 10.7 %all-to-all-start.5 = ((bf16[16,80,128]{2,1,0:T(8,128)(2,1)}), bf16[16,80,128]{2,1,0:T(8,128)(2,1)S(1)}, u32[]{:S(2)}, u32[]{:S(2)}) async-start(bf16[16,80,128]{2,1,0:T(8,128)(2,1)} %shard_map.120), calls=%async_computation.5 | async-start | bytes 655360 | tf_op jit(solution)/shard_map/all_to_all | solution.py:480
  174.6 0.2 reshape.76
  174.7 0.3 copy.17
  175.0 1.3 reshape.73
  176.3 7.4 %all-to-all-done.5.pieces_any = bf16[16,80,128]{2,1,0:T(8,128)(2,1)S(1)} async-done(((bf16[16,80,128]{2,1,0:T(8,128)(2,1)}), bf16[16,80,128]{2,1,0:T(8,128)(2,1)S(1)}, u32[]{:S(2)}, u32[]{:S(2)}) %all-to-all-start.5) | async-done | bytes 327712 | tf_op jit(solution)/shard_map/all_to_all | solution.py:480
  183.7 1.6 shard_map.121
  (7 shorter events, 0.1 us)
Async XLA Ops:
  2.2 46.2 %copy-start.2 = (bf16[128,512]{1,0:T(8,128)(2,1)S(1)}, bf16[128,512]{1,0:T(8,128)(2,1)}, u32[]{:S(2)}) copy-start(bf16[128,512]{1,0:T(8,128)(2,1)} %constant.34.fwd_z_ref) | copy-start | bytes 393220
  2.2 37.5 %all-to-all-start = ((bf16[32,8,512]{2,1,0:T(8,128)(2,1)}), bf16[32,8,512]{2,1,0:T(8,128)(2,1)S(1)}, u32[]{:S(2)}, u32[]{:S(2)}) async-start(bf16[32,8,512]{2,1,0:T(8,128)(2,1)} %bitcast.4), calls=%async_computation | async-start | bytes 524288 | tf_op jit(solution)/shard_map/all_to_all | solution.py:480
  39.7 13.1 %collective-permute-start = (bf16[256,512]{1,0:T(8,128)(2,1)S(1)}, bf16[256,512]{1,0:T(8,128)(2,1)S(1)}, u32[]{:S(2)}, u32[]{:S(2)}) collective-permute-start(bf16[256,512]{1,0:T(8,128)(2,1)S(1)} %bitcast.24), channel_id=1, source_target_pairs={{0,1},{1,0},{2,3},{3,2},{4,5},{5,4},{6,7},{7,6},{8,9},{9,8},{10,11... | collective-permute-start | bytes 786440 | tf_op jit(solution)/shard_map/ppermute | solution.py:497
  42.0 0.9 copy-start.5
  42.9 0.7 copy-start.6
  46.4 1.9 %copy-start.7 = (bf16[2,1024,1024]{2,1,0:T(8,128)(2,1)}, bf16[2,1024,1024]{2,1,0:T(8,128)(2,1)S(1)}, u32[]{:S(2)}) copy-start(bf16[2,1024,1024]{2,1,0:T(8,128)(2,1)S(1)} %get-tuple-element.13.big_y_ref) | copy-start | bytes 12582916
  48.3 4.4 %copy-start.3 = (bf16[128,512]{1,0:T(8,128)(2,1)S(1)}, bf16[128,512]{1,0:T(8,128)(2,1)}, u32[]{:S(2)}) copy-start(bf16[128,512]{1,0:T(8,128)(2,1)} %constant.35.back_x_ref) | copy-start | bytes 393220
  48.3 4.4 %copy-start.4 = (bf16[256,256]{1,0:T(8,128)(2,1)S(1)}, bf16[256,256]{1,0:T(8,128)(2,1)}, u32[]{:S(2)}) copy-start(bf16[256,256]{1,0:T(8,128)(2,1)} %constant.36.send_ref) | copy-start | bytes 393220
  48.3 2.2 %copy-start.8 = (bf16[2,1024,1024]{2,1,0:T(8,128)(2,1)S(1)}, bf16[2,1024,1024]{2,1,0:T(8,128)(2,1)}, u32[]{:S(2)}) copy-start(bf16[2,1024,1024]{2,1,0:T(8,128)(2,1)} %copy-done.7) | copy-start | bytes 12582916
  50.6 2.2 %copy-start.9 = (bf16[2,1024,1024]{2,1,0:T(8,128)(2,1)S(1)}, bf16[2,1024,1024]{2,1,0:T(8,128)(2,1)}, u32[]{:S(2)}) copy-start(bf16[2,1024,1024]{2,1,0:T(8,128)(2,1)} %copy-done.7) | copy-start | bytes 12582916
  52.7 9.2 %copy-start = (bf16[256,256]{1,0:T(8,128)(2,1)S(1)}, bf16[256,256]{1,0:T(8,128)(2,1)}, u32[]{:S(2)}) copy-start(bf16[256,256]{1,0:T(8,128)(2,1)} %constant.37.fwd_x_ref) | copy-start | bytes 393220
  57.5 87.5 %copy-start.11 = (s32[16,3]{0,1:T(4,128)S(1)}, s32[16,3]{0,1:T(4,128)}, u32[]{:S(2)}) copy-start(s32[16,3]{0,1:T(4,128)} %param.13) | copy-start | bytes 580
  57.5 87.6 %copy-start.1 = (f32[2,8,128]{2,1,0:T(8,128)S(1)}, f32[2,8,128]{2,1,0:T(8,128)}, u32[]{:S(2)}) copy-start(f32[2,8,128]{2,1,0:T(8,128)} %tile_ref.1) | copy-start | bytes 24580
  57.5 22.7 %all-to-all-start.1 = ((bf16[32,8,512]{2,1,0:T(8,128)(2,1)}), bf16[32,8,512]{2,1,0:T(8,128)(2,1)S(1)}, u32[]{:S(2)}, u32[]{:S(2)}) async-start(bf16[32,8,512]{2,1,0:T(8,128)(2,1)} %bitcast.6), calls=%async_computation.1 | async-start | bytes 524288 | tf_op jit(solution)/shard_map/all_to_all | solution.py:480
  141.1 22.7 %all-to-all-start.4 = ((bf16[32,8,512]{2,1,0:T(8,128)(2,1)}), bf16[32,8,512]{2,1,0:T(8,128)(2,1)S(1)}, u32[]{:S(2)}, u32[]{:S(2)}) async-start(bf16[32,8,512]{2,1,0:T(8,128)(2,1)} %bitcast.12), calls=%async_computation.4 | async-start | bytes 524288 | tf_op jit(solution)/shard_map/all_to_all | solution.py:480
  145.1 2.2 %copy-start.10 = (bf16[2,1024,1024]{2,1,0:T(8,128)(2,1)S(1)}, bf16[2,1024,1024]{2,1,0:T(8,128)(2,1)}, u32[]{:S(2)}) copy-start(bf16[2,1024,1024]{2,1,0:T(8,128)(2,1)} %copy-done.7) | copy-start | bytes 12582916
  163.9 19.9 %all-to-all-start.5 = ((bf16[16,80,128]{2,1,0:T(8,128)(2,1)}), bf16[16,80,128]{2,1,0:T(8,128)(2,1)S(1)}, u32[]{:S(2)}, u32[]{:S(2)}) async-start(bf16[16,80,128]{2,1,0:T(8,128)(2,1)} %shard_map.120), calls=%async_computation.5 | async-start | bytes 655360 | tf_op jit(solution)/shard_map/all_to_all | solution.py:480

commit v6 on v5

--- a/solution.py
+++ b/solution.py
@@ -190,16 +190,13 @@
     image_ref[:, coefs:] = jnp.zeros((2 * NB, NB), BF16)
 
 
-def gram_kernel(received_any, image_any, out_any, stepped_ref, conj_ref, extra_ref, received_ref, sems):
-    received_copy = pltpu.make_async_copy(received_any, received_ref, sems.at[0])
-    received_copy.start()
+def gram_kernel(received_ref, image_any, out_any, stepped_ref, conj_ref, extra_ref, sem):
     coefs = HB * 2 * QB
     half_w = coefs // 2
     shape = (NB, 2 * NB)
     row, col = iota(shape, 0), iota(shape, 1)
     at = row // LOCAL * 2 * LOCAL + row % LOCAL
     picks = [onehot(col == at + half * LOCAL) for half in (0, 1)]
-    received_copy.wait()
     for half in (0, 1):
         rows = dot(picks[half], received_ref[...])
         stepped_ref[:, half * half_w : (half + 1) * half_w] = rows.astype(BF16)
@@ -217,7 +214,7 @@
     at = col // LOCAL * 2 * LOCAL + col % LOCAL
     spread = dot(onehot(row == at), upper) + dot(onehot(row == at + LOCAL), lower)
     extra_ref[...] = spread.astype(BF16)
-    extra_copy = pltpu.make_async_copy(extra_ref, out_any.at[:, coefs:], sems.at[1])
+    extra_copy = pltpu.make_async_copy(extra_ref, out_any.at[:, coefs:], sem)
     extra_copy.start()
     extra_copy.wait()
 
@@ -357,12 +354,9 @@
         out_ref[to, FG:, :] = tile.astype(BF16)
 
 
-def last_kernel(place_ref, own_ref, pieces_any, out_ref, total_ref, pieces_ref, sem):
-    pieces_copy = pltpu.make_async_copy(pieces_any, pieces_ref, sem)
-    pieces_copy.start()
+def last_kernel(place_ref, own_ref, pieces_ref, out_ref, total_ref):
     own = own_ref[0]
     own_y = place_ref[own, 1]
-    pieces_copy.wait()
     patched = jnp.zeros((FG, LANES), F32)
     for at in range(FRAGS):
         patched += pieces_ref[at, :FG, :].astype(F32)
@@ -443,9 +437,9 @@
     gram = call(
         gram_kernel,
         (sds((2 * NB, coefs + NB), BF16), sds((NB, coefs), BF16)),
-        [ANY, ANY],
-        [((NB, coefs), BF16), ((2 * NB, NB), BF16), ((2 * NB, coefs // 2), BF16)],
-        2 * 10**8, 2 * mega, "gram", 2, (ANY, VM), {1: 0},
+        [VM, ANY],
+        [((NB, coefs), BF16), ((2 * NB, NB), BF16)],
+        2 * 10**8, 2 * mega, "gram", 1, (ANY, VM), {1: 0},
     )
     total = call(
         sum_kernel, sds((NB, NB), F32), [VM], [], 10**6, mega // 8, "total",
@@ -470,8 +464,8 @@
         4 * 10**9, 6 * mega, "density",
     )
     last = call(
-        last_kernel, sds((2, FG * FG), F32), [SM, SM, ANY],
-        [((FG, LANES), F32), ((FRAGS, FG + 16, LANES), BF16)], 10**7, mega // 2, "last", 1,
+        last_kernel, sds((2, FG * FG), F32), [SM, SM, VM], [((FG, LANES), F32)],
+        10**7, mega // 2, "last",
     )
     return forward, near, step, image, gram, total, newton, density, last
 

time: 186 us -> 186 us (level)
  no operation moved by 1% of the time
where the time goes in v6:
time: 186 us; the launch traced here: 185 us
  blocking collectives  55.9 us (30%)
  waiting for transfers between devices  54 us (29%)
  starting transfers between devices  38.4 us (21%)
  Pallas kernels  23.5 us (13%)
  local copies, waits for them, and re-layouts  11.7 us (6%)
    all_to_all x2, blocking collectives, exchange(): return lax.all_to_all(values, axis, split_axis=0, concat_axis=0, tiled=True)  55.9 us
    all_to_all x4, waiting for transfers between devices, exchange(): return lax.all_to_all(values, axis, split_axis=0, concat_axis=0, tiled=True)  54 us
    all_to_all x4, starting transfers between devices, exchange(): return lax.all_to_all(values, axis, split_axis=0, concat_axis=0, tiled=True)  36.1 us
    unnamed x25, local copies, waits for them, and re-layouts  8.08 us
    pallas_call x1, Pallas kernels, per_device(): pieces = density(patch_list, own, parts, inverse, big_y, fwd_z, hartree)  6.98 us
    pallas_call x1, Pallas kernels, per_device(): step(near_at, after_y, pot_far, big_y, fwd_z, near_rows, bands, back_x, s...  4.71 us
    pallas_call x1, Pallas kernels, per_device(): phi, inverse = newton(whole, stepped)  4 us
  transfers between devices with their start and end apart: 5, of which 4 were waited for; matrix products, arithmetic and copies ran while one was open for 2% of the time, Pallas kernels for 7%

profile of v6, /device:TPU:1, one launch (start us, length us, event | category | flops | bytes accessed | tf_op | source)
XLA Modules:
  0.0 185.2 jit_solution(6305609261842931505)
XLA Ops:
  0.6 0.8 convert_element_type.30
  1.4 0.7 broadcast_in_dim.2
  2.2 17.1 %all-to-all-start = ((bf16[32,8,512]{2,1,0:T(8,128)(2,1)}), bf16[32,8,512]{2,1,0:T(8,128)(2,1)S(1)}, u32[]{:S(2)}, u32[]{:S(2)}) async-start(bf16[32,8,512]{2,1,0:T(8,128)(2,1)} %bitcast.4), calls=%async_computation | async-start | bytes 524288 | tf_op jit(solution)/shard_map/all_to_all | solution.py:474
  19.3 1.1 reshape.58.bands_ref
  20.4 19.3 %all-to-all-done = bf16[32,8,512]{2,1,0:T(8,128)(2,1)S(1)} async-done(((bf16[32,8,512]{2,1,0:T(8,128)(2,1)}), bf16[32,8,512]{2,1,0:T(8,128)(2,1)S(1)}, u32[]{:S(2)}, u32[]{:S(2)}) %all-to-all-start) | async-done | bytes 262176 | tf_op jit(solution)/shard_map/all_to_all | solution.py:474
  39.7 2.3 %collective-permute-start = (bf16[256,512]{1,0:T(8,128)(2,1)S(1)}, bf16[256,512]{1,0:T(8,128)(2,1)S(1)}, u32[]{:S(2)}, u32[]{:S(2)}) collective-permute-start(bf16[256,512]{1,0:T(8,128)(2,1)S(1)} %bitcast.24), channel_id=1, source_target_pairs={{0,1},{1,0},{2,3},{3,2},{4,5},{5,4},{6,7},{7,6},{8,9},{9,8},{10,11... | collective-permute-start | bytes 786440 | tf_op jit(solution)/shard_map/ppermute | solution.py:491
  42.0 0.0 copy-start.5
  42.0 0.9 copy-done.5
  42.9 0.0 copy-start.6
  42.9 0.7 copy-done.6
  43.6 2.8 %shard_map.113 = (bf16[2,1024,1024]{2,1,0:T(8,128)(2,1)S(1)}, bf16[2,256,1024]{2,1,0:T(8,128)(2,1)S(1)}) custom-call(bf16[128,1024]{1,0:T(8,128)(2,1)S(1)} %reshape.58.bands_ref, bf16[256,256]{1,0:T(8,128)(2,1)S(1)} %copy-done.5, bf16[64,128]{1,0:T(8,128)(2,1)S(1)} %copy-done.6), custom_call_target="tpu_custom_call" | custom-call | flops 2000000000 | bytes 6291456 | tf_op jit(solution)/shard_map/pallas_call | solution.py:493
  46.4 0.0 copy-start.7
  46.4 1.9 %copy-done.7 = bf16[2,1024,1024]{2,1,0:T(8,128)(2,1)} copy-done((bf16[2,1024,1024]{2,1,0:T(8,128)(2,1)}, bf16[2,1024,1024]{2,1,0:T(8,128)(2,1)S(1)}, u32[]{:S(2)}) %copy-start.7) | copy-done | bytes 4194328
  48.3 0.0 copy-start.3
  48.3 0.0 copy-start.4
  48.3 0.0 copy-done.2
  48.3 0.0 copy-start.8
  48.3 2.2 %copy-done.8 = bf16[2,1024,1024]{2,1,0:T(8,128)(2,1)S(1)} copy-done((bf16[2,1024,1024]{2,1,0:T(8,128)(2,1)S(1)}, bf16[2,1024,1024]{2,1,0:T(8,128)(2,1)}, u32[]{:S(2)}) %copy-start.8) | copy-done | bytes 4194328
  50.6 0.0 copy-start.9
  50.6 2.2 %shard_map.114.sum_ref = f32[256,1024]{1,0:T(8,128)S(1)} custom-call(s32[1]{0:T(128)} %bitcast.1.near_at_ref, bf16[2,256,1024]{2,1,0:T(8,128)(2,1)S(1)} %get-tuple-element.12.after_y_ref, bf16[256,512]{1,0:T(8,128)(2,1)S(1)} %bitcast.25, bf16[2,1024,1024]{2,1,0:T(8,128)(2,1)S(1)} %copy-done.8, bf16[128,512]{1,0:T(8,128)(2,1)S(1)} %copy-done.2), custom_call_target="tpu_custom_call" | custom-call | flops 2000000000 | bytes 4194304 | tf_op jit(solution)/shard_map/pallas_call | solution.py:494
  52.7 0.0 copy-start
  52.7 0.0 collective-permute-done.pot_ref
  52.7 0.0 copy-done.3
  52.8 0.0 copy-done.4
  52.8 0.0 copy-done.9
  52.8 4.7 %shard_map.115 = (bf16[128,1024]{1,0:T(8,128)(2,1)S(1)}, bf16[256,512]{1,0:T(8,128)(2,1)}) custom-call(s32[1]{0:T(128)} %bitcast.1.near_at_ref, bf16[2,256,1024]{2,1,0:T(8,128)(2,1)S(1)} %get-tuple-element.12.after_y_ref, bf16[256,512]{1,0:T(8,128)(2,1)S(1)} %collective-permute-done.pot_ref, bf16[2,1024,1024]{2,1,0:T(8,128)(2,1)S(1)} %copy-done.9, ...), custom_call_target="tpu_custom_call" | custom-call | flops 2000000000 | bytes 4194304 | tf_op jit(solution)/shard_map/pallas_call | solution.py:495
  57.5 0.0 copy-start.11
  57.5 4.5 %all-to-all-start.1 = ((bf16[32,8,512]{2,1,0:T(8,128)(2,1)}), bf16[32,8,512]{2,1,0:T(8,128)(2,1)S(1)}, u32[]{:S(2)}, u32[]{:S(2)}) async-start(bf16[32,8,512]{2,1,0:T(8,128)(2,1)} %bitcast.6), calls=%async_computation.1 | async-start | bytes 524288 | tf_op jit(solution)/shard_map/all_to_all | solution.py:474
  62.0 0.0 copy-done
  62.0 0.4 shard_map.116.image_any
  62.4 17.8 %all-to-all-done.1 = bf16[32,8,512]{2,1,0:T(8,128)(2,1)S(1)} async-done(((bf16[32,8,512]{2,1,0:T(8,128)(2,1)}), bf16[32,8,512]{2,1,0:T(8,128)(2,1)S(1)}, u32[]{:S(2)}, u32[]{:S(2)}) %all-to-all-start.1) | async-done | bytes 262176 | tf_op jit(solution)/shard_map/all_to_all | solution.py:474
  80.2 0.9 shard_map.117
  81.1 38.3 %all_to_all.30 = bf16[32,8,1152]{2,1,0:T(8,128)(2,1)S(1)} all-to-all(bf16[32,8,1152]{2,1,0:T(8,128)(2,1)S(1)} %bitcast.19), channel_id=1, replica_groups=mesh['frag'=16,'band'=32] {'band'}, dimensions={0} | all-to-all | bytes 1179648 | tf_op jit(solution)/shard_map/all_to_all | solution.py:474
  119.4 17.6 %all_to_all.31 = f32[32,4,128]{2,1,0:T(4,128)S(1)} all-to-all(f32[32,4,128]{2,1,0:T(4,128)S(1)} %bitcast.23), channel_id=1, replica_groups=mesh['frag'=16,'band'=32] {'band'}, dimensions={0} | all-to-all | bytes 131072 | tf_op jit(solution)/shard_map/all_to_all | solution.py:474
  137.1 4.0 %shard_map.119 = (bf16[256,512]{1,0:T(8,128)(2,1)}, bf16[512,128]{1,0:T(8,128)(2,1)S(1)}) custom-call(f32[128,128]{1,0:T(8,128)S(1)} %bitcast.26, bf16[128,1024]{1,0:T(8,128)(2,1)S(1)} %get-tuple-element.17.stepped_ref), custom_call_target="tpu_custom_call" | custom-call | flops 1000000000 | bytes 1048576 | tf_op jit(solution)/shard_map/pallas_call | solution.py:503
  141.1 3.9 %all-to-all-start.4 = ((bf16[32,8,512]{2,1,0:T(8,128)(2,1)}), bf16[32,8,512]{2,1,0:T(8,128)(2,1)S(1)}, u32[]{:S(2)}, u32[]{:S(2)}) async-start(bf16[32,8,512]{2,1,0:T(8,128)(2,1)} %bitcast.12), calls=%async_computation.4 | async-start | bytes 524288 | tf_op jit(solution)/shard_map/all_to_all | solution.py:474
  145.0 0.0 copy-done.11
  145.0 0.1 copy.13.place_ref
  145.1 0.0 copy-done.1
  145.1 2.2 %copy-done.10 = bf16[2,1024,1024]{2,1,0:T(8,128)(2,1)S(1)} copy-done((bf16[2,1024,1024]{2,1,0:T(8,128)(2,1)S(1)}, bf16[2,1024,1024]{2,1,0:T(8,128)(2,1)}, u32[]{:S(2)}) %copy-start.10) | copy-done | bytes 4194328
  147.2 7.0 %shard_map.120 = bf16[16,80,128]{2,1,0:T(8,128)(2,1)} custom-call(s32[16,3]{1,0:T(8,128)S(1)} %copy.13.place_ref, s32[1]{0:T(128)} %bitcast.own_ref, bf16[256,1152]{1,0:T(8,128)(2,1)S(1)} %bitcast.21, bf16[512,128]{1,0:T(8,128)(2,1)S(1)} %get-tuple-element.18.inv_ref, bf16[2,1024,1024]{2,1,0:T(8,128)(2,1)S(1)} %copy-done.10, bf16[128,512]{1,0:T(8,128)(2,1)S(1)} %copy-done.2, ...), custom_call_target="tpu_custom_call" | custom-call | flops 4000000000 | bytes 6291456 | tf_op jit(solution)/shard_map/pallas_call | solution.py:505
  154.2 9.6 %all-to-all-done.4 = bf16[32,8,512]{2,1,0:T(8,128)(2,1)S(1)} async-done(((bf16[32,8,512]{2,1,0:T(8,128)(2,1)}), bf16[32,8,512]{2,1,0:T(8,128)(2,1)S(1)}, u32[]{:S(2)}, u32[]{:S(2)}) %all-to-all-start.4) | async-done | bytes 262176 | tf_op jit(solution)/shard_map/all_to_all | solution.py:474
  163.8 10.7 %all-to-all-start.5 = ((bf16[16,80,128]{2,1,0:T(8,128)(2,1)}), bf16[16,80,128]{2,1,0:T(8,128)(2,1)S(1)}, u32[]{:S(2)}, u32[]{:S(2)}) async-start(bf16[16,80,128]{2,1,0:T(8,128)(2,1)} %shard_map.120), calls=%async_computation.5 | async-start | bytes 655360 | tf_op jit(solution)/shard_map/all_to_all | solution.py:474
  174.5 0.2 reshape.76
  174.7 0.3 copy.17
  174.9 1.3 reshape.73
  176.3 7.4 %all-to-all-done.5.pieces_ref = bf16[16,80,128]{2,1,0:T(8,128)(2,1)S(1)} async-done(((bf16[16,80,128]{2,1,0:T(8,128)(2,1)}), bf16[16,80,128]{2,1,0:T(8,128)(2,1)S(1)}, u32[]{:S(2)}, u32[]{:S(2)}) %all-to-all-start.5) | async-done | bytes 327712 | tf_op jit(solution)/shard_map/all_to_all | solution.py:474
  183.7 1.5 shard_map.121
  (7 shorter events, 0.1 us)
Async XLA Ops:
  2.2 46.2 %copy-start.2 = (bf16[128,512]{1,0:T(8,128)(2,1)S(1)}, bf16[128,512]{1,0:T(8,128)(2,1)}, u32[]{:S(2)}) copy-start(bf16[128,512]{1,0:T(8,128)(2,1)} %constant.34.fwd_z_ref) | copy-start | bytes 393220
  2.2 37.5 %all-to-all-start = ((bf16[32,8,512]{2,1,0:T(8,128)(2,1)}), bf16[32,8,512]{2,1,0:T(8,128)(2,1)S(1)}, u32[]{:S(2)}, u32[]{:S(2)}) async-start(bf16[32,8,512]{2,1,0:T(8,128)(2,1)} %bitcast.4), calls=%async_computation | async-start | bytes 524288 | tf_op jit(solution)/shard_map/all_to_all | solution.py:474
  39.7 13.1 %collective-permute-start = (bf16[256,512]{1,0:T(8,128)(2,1)S(1)}, bf16[256,512]{1,0:T(8,128)(2,1)S(1)}, u32[]{:S(2)}, u32[]{:S(2)}) collective-permute-start(bf16[256,512]{1,0:T(8,128)(2,1)S(1)} %bitcast.24), channel_id=1, source_target_pairs={{0,1},{1,0},{2,3},{3,2},{4,5},{5,4},{6,7},{7,6},{8,9},{9,8},{10,11... | collective-permute-start | bytes 786440 | tf_op jit(solution)/shard_map/ppermute | solution.py:491
  42.0 0.9 copy-start.5
  42.9 0.7 copy-start.6
  46.4 1.9 %copy-start.7 = (bf16[2,1024,1024]{2,1,0:T(8,128)(2,1)}, bf16[2,1024,1024]{2,1,0:T(8,128)(2,1)S(1)}, u32[]{:S(2)}) copy-start(bf16[2,1024,1024]{2,1,0:T(8,128)(2,1)S(1)} %get-tuple-element.13.big_y_ref) | copy-start | bytes 12582916
  48.3 4.4 %copy-start.3 = (bf16[128,512]{1,0:T(8,128)(2,1)S(1)}, bf16[128,512]{1,0:T(8,128)(2,1)}, u32[]{:S(2)}) copy-start(bf16[128,512]{1,0:T(8,128)(2,1)} %constant.35.back_x_ref) | copy-start | bytes 393220
  48.3 4.4 %copy-start.4 = (bf16[256,256]{1,0:T(8,128)(2,1)S(1)}, bf16[256,256]{1,0:T(8,128)(2,1)}, u32[]{:S(2)}) copy-start(bf16[256,256]{1,0:T(8,128)(2,1)} %constant.36.send_ref) | copy-start | bytes 393220
  48.3 2.2 %copy-start.8 = (bf16[2,1024,1024]{2,1,0:T(8,128)(2,1)S(1)}, bf16[2,1024,1024]{2,1,0:T(8,128)(2,1)}, u32[]{:S(2)}) copy-start(bf16[2,1024,1024]{2,1,0:T(8,128)(2,1)} %copy-done.7) | copy-start | bytes 12582916
  50.6 2.2 %copy-start.9 = (bf16[2,1024,1024]{2,1,0:T(8,128)(2,1)S(1)}, bf16[2,1024,1024]{2,1,0:T(8,128)(2,1)}, u32[]{:S(2)}) copy-start(bf16[2,1024,1024]{2,1,0:T(8,128)(2,1)} %copy-done.7) | copy-start | bytes 12582916
  52.7 9.2 %copy-start = (bf16[256,256]{1,0:T(8,128)(2,1)S(1)}, bf16[256,256]{1,0:T(8,128)(2,1)}, u32[]{:S(2)}) copy-start(bf16[256,256]{1,0:T(8,128)(2,1)} %constant.37.fwd_x_ref) | copy-start | bytes 393220
  57.5 87.5 %copy-start.11 = (s32[16,3]{0,1:T(4,128)S(1)}, s32[16,3]{0,1:T(4,128)}, u32[]{:S(2)}) copy-start(s32[16,3]{0,1:T(4,128)} %param.13) | copy-start | bytes 580
  57.5 87.6 %copy-start.1 = (f32[2,8,128]{2,1,0:T(8,128)S(1)}, f32[2,8,128]{2,1,0:T(8,128)}, u32[]{:S(2)}) copy-start(f32[2,8,128]{2,1,0:T(8,128)} %tile_ref.1) | copy-start | bytes 24580
  57.5 22.7 %all-to-all-start.1 = ((bf16[32,8,512]{2,1,0:T(8,128)(2,1)}), bf16[32,8,512]{2,1,0:T(8,128)(2,1)S(1)}, u32[]{:S(2)}, u32[]{:S(2)}) async-start(bf16[32,8,512]{2,1,0:T(8,128)(2,1)} %bitcast.6), calls=%async_computation.1 | async-start | bytes 524288 | tf_op jit(solution)/shard_map/all_to_all | solution.py:474
  141.1 22.7 %all-to-all-start.4 = ((bf16[32,8,512]{2,1,0:T(8,128)(2,1)}), bf16[32,8,512]{2,1,0:T(8,128)(2,1)S(1)}, u32[]{:S(2)}, u32[]{:S(2)}) async-start(bf16[32,8,512]{2,1,0:T(8,128)(2,1)} %bitcast.12), calls=%async_computation.4 | async-start | bytes 524288 | tf_op jit(solution)/shard_map/all_to_all | solution.py:474
  145.1 2.2 %copy-start.10 = (bf16[2,1024,1024]{2,1,0:T(8,128)(2,1)S(1)}, bf16[2,1024,1024]{2,1,0:T(8,128)(2,1)}, u32[]{:S(2)}) copy-start(bf16[2,1024,1024]{2,1,0:T(8,128)(2,1)} %copy-done.7) | copy-start | bytes 12582916
  163.8 19.9 %all-to-all-start.5 = ((bf16[16,80,128]{2,1,0:T(8,128)(2,1)}), bf16[16,80,128]{2,1,0:T(8,128)(2,1)S(1)}, u32[]{:S(2)}, u32[]{:S(2)}) async-start(bf16[16,80,128]{2,1,0:T(8,128)(2,1)} %shard_map.120), calls=%async_computation.5 | async-start | bytes 655360 | tf_op jit(solution)/shard_map/all_to_all | solution.py:474

commit v7 on v6

--- a/solution.py
+++ b/solution.py
@@ -44,8 +44,8 @@
     fwd_x = fwd_x.reshape(LOCAL * FG, 2 * LOCAL * HB)
     fwd_x_send = fwd_x.reshape(LOCAL, FG // 2, 2, -1).transpose(1, 2, 0, 3)
     fwd_x_send = fwd_x_send.reshape(LOCAL * FG, -1)
-    back_x = np.stack([np.einsum("ab,xk->akbx", same, t) for t in (cos_xy, -sin_xy)], axis=2)
-    back_x = back_x.reshape(LOCAL * HB, 2 * LOCAL * FG)
+    back_x = np.stack([np.einsum("ab,xk->akbx", same, t) for t in (cos_xy, -sin_xy)], axis=0)
+    back_x = back_x.reshape(2 * LOCAL * HB, LOCAL * FG)
     fwd_y = np.stack(
         [np.stack([cos_xy.T, sin_xy.T], axis=2), np.stack([-sin_xy.T, cos_xy.T], axis=2)], axis=1
     ).reshape(2 * HB, 2 * FG)
@@ -151,21 +151,18 @@
 
 def step_kernel(
     near_at_ref, after_y_ref, pot_ref, big_y_ref, fwd_z_ref, sum_ref, bands_ref, back_x_ref,
-    send_ref, stepped_ref, sent_ref, stack_ref, back_ref, pots_ref,
+    send_ref, stepped_ref, sent_ref, back_ref, pots_ref,
 ):
     far = 1 - near_at_ref[0]
     weigh_half(far, after_y_ref, pot_ref, fwd_z_ref, back_ref, pots_ref)
-    rows_n = LOCAL * FG
     half_n = LOCAL * HB
     block_n = 2 * LANES
     for start in range(0, HB * 2 * QB, block_n):
         span = slice(start, start + block_n)
         block = sum_ref[:, span] + dot_t(back_ref[...], big_y_ref[far, span, :])
-        stack_ref[:rows_n, span] = block.astype(BF16)
-        for low in range(start, start + block_n, LANES):
-            turned = times_i(block[:, low - start : low - start + LANES])
-            stack_ref[rows_n:, low : low + LANES] = turned.astype(BF16)
-        image = dot(back_x_ref[...], stack_ref[:, span]) * (0.25 / FG**1.5)
+        both = dot(back_x_ref[...], block.astype(BF16))
+        turned = [times_i(both[half_n:, low : low + LANES]) for low in (0, LANES)]
+        image = (both[:half_n] + jnp.concatenate(turned, axis=1)) * (0.25 / FG**1.5)
         shape = (half_n, block_n)
         row, lane = iota(shape, 0), iota(shape, 1) + start
         mx, my = row % HB - HB // 2, lane // (2 * QB) - HB // 2
@@ -427,7 +424,7 @@
         step_kernel,
         (sds((LOCAL * HB, coefs), BF16), sds((2 * NB, coefs // 2), BF16)),
         [SM] + [VM] * 8,
-        [((2 * LOCAL * FG, coefs), BF16)] + weigh,
+        weigh,
         2 * 10**9, 4 * mega, "step",
     )
     image = call(

time: 186 us -> 186 us (level)
  no operation moved by 1% of the time
where the time goes in v7:
time: 186 us; the launch traced here: 185 us
  blocking collectives  55.9 us (30%)
  waiting for transfers between devices  54 us (29%)
  starting transfers between devices  38.6 us (21%)
  Pallas kernels  23.1 us (12%)
  local copies, waits for them, and re-layouts  11.7 us (6%)
    all_to_all x2, blocking collectives, exchange(): return lax.all_to_all(values, axis, split_axis=0, concat_axis=0, tiled=True)  55.9 us
    all_to_all x4, waiting for transfers between devices, exchange(): return lax.all_to_all(values, axis, split_axis=0, concat_axis=0, tiled=True)  54 us
    all_to_all x4, starting transfers between devices, exchange(): return lax.all_to_all(values, axis, split_axis=0, concat_axis=0, tiled=True)  36.3 us
    unnamed x25, local copies, waits for them, and re-layouts  8.08 us
    pallas_call x1, Pallas kernels, per_device(): pieces = density(patch_list, own, parts, inverse, big_y, fwd_z, hartree)  6.98 us
    pallas_call x1, Pallas kernels, per_device(): step(near_at, after_y, pot_far, big_y, fwd_z, near_rows, bands, back_x, s...  4.29 us
    pallas_call x1, Pallas kernels, per_device(): phi, inverse = newton(whole, stepped)  4.01 us
  transfers between devices with their start and end apart: 5, of which 4 were waited for; matrix products, arithmetic and copies ran while one was open for 2% of the time, Pallas kernels for 7%

profile of v7, /device:TPU:1, one launch (start us, length us, event | category | flops | bytes accessed | tf_op | source)
XLA Modules:
  0.0 184.9 jit_solution(2671138025653657704)
XLA Ops:
  0.6 0.8 convert_element_type.30
  1.4 0.7 broadcast_in_dim.2
  2.2 17.1 %all-to-all-start = ((bf16[32,8,512]{2,1,0:T(8,128)(2,1)}), bf16[32,8,512]{2,1,0:T(8,128)(2,1)S(1)}, u32[]{:S(2)}, u32[]{:S(2)}) async-start(bf16[32,8,512]{2,1,0:T(8,128)(2,1)} %bitcast.4), calls=%async_computation | async-start | bytes 524288 | tf_op jit(solution)/shard_map/all_to_all | solution.py:471
  19.3 1.1 reshape.58.bands_ref
  20.4 19.3 %all-to-all-done = bf16[32,8,512]{2,1,0:T(8,128)(2,1)S(1)} async-done(((bf16[32,8,512]{2,1,0:T(8,128)(2,1)}), bf16[32,8,512]{2,1,0:T(8,128)(2,1)S(1)}, u32[]{:S(2)}, u32[]{:S(2)}) %all-to-all-start) | async-done | bytes 262176 | tf_op jit(solution)/shard_map/all_to_all | solution.py:471
  39.7 2.3 %collective-permute-start = (bf16[256,512]{1,0:T(8,128)(2,1)S(1)}, bf16[256,512]{1,0:T(8,128)(2,1)S(1)}, u32[]{:S(2)}, u32[]{:S(2)}) collective-permute-start(bf16[256,512]{1,0:T(8,128)(2,1)S(1)} %bitcast.24), channel_id=1, source_target_pairs={{0,1},{1,0},{2,3},{3,2},{4,5},{5,4},{6,7},{7,6},{8,9},{9,8},{10,11... | collective-permute-start | bytes 786440 | tf_op jit(solution)/shard_map/ppermute | solution.py:488
  42.0 0.0 copy-start.5
  42.0 0.9 copy-done.5
  42.9 0.0 copy-start.6
  42.9 0.7 copy-done.6
  43.6 2.8 %shard_map.113 = (bf16[2,1024,1024]{2,1,0:T(8,128)(2,1)S(1)}, bf16[2,256,1024]{2,1,0:T(8,128)(2,1)S(1)}) custom-call(bf16[128,1024]{1,0:T(8,128)(2,1)S(1)} %reshape.58.bands_ref, bf16[256,256]{1,0:T(8,128)(2,1)S(1)} %copy-done.5, bf16[64,128]{1,0:T(8,128)(2,1)S(1)} %copy-done.6), custom_call_target="tpu_custom_call" | custom-call | flops 2000000000 | bytes 6291456 | tf_op jit(solution)/shard_map/pallas_call | solution.py:490
  46.4 0.0 copy-start.7
  46.4 1.9 %copy-done.7 = bf16[2,1024,1024]{2,1,0:T(8,128)(2,1)} copy-done((bf16[2,1024,1024]{2,1,0:T(8,128)(2,1)}, bf16[2,1024,1024]{2,1,0:T(8,128)(2,1)S(1)}, u32[]{:S(2)}) %copy-start.7) | copy-done | bytes 4194328
  48.3 0.0 copy-start.3
  48.3 0.0 copy-start.4
  48.3 0.0 copy-done.2
  48.3 0.0 copy-start.8
  48.3 2.2 %copy-done.8 = bf16[2,1024,1024]{2,1,0:T(8,128)(2,1)S(1)} copy-done((bf16[2,1024,1024]{2,1,0:T(8,128)(2,1)S(1)}, bf16[2,1024,1024]{2,1,0:T(8,128)(2,1)}, u32[]{:S(2)}) %copy-start.8) | copy-done | bytes 4194328
  50.6 0.0 copy-start.9
  50.6 2.2 %shard_map.114.sum_ref = f32[256,1024]{1,0:T(8,128)S(1)} custom-call(s32[1]{0:T(128)} %bitcast.1.near_at_ref, bf16[2,256,1024]{2,1,0:T(8,128)(2,1)S(1)} %get-tuple-element.12.after_y_ref, bf16[256,512]{1,0:T(8,128)(2,1)S(1)} %bitcast.25, bf16[2,1024,1024]{2,1,0:T(8,128)(2,1)S(1)} %copy-done.8, bf16[128,512]{1,0:T(8,128)(2,1)S(1)} %copy-done.2), custom_call_target="tpu_custom_call" | custom-call | flops 2000000000 | bytes 4194304 | tf_op jit(solution)/shard_map/pallas_call | solution.py:491
  52.7 0.0 copy-start
  52.7 0.0 collective-permute-done.pot_ref
  52.7 0.0 copy-done.3
  52.8 0.0 copy-done.4
  52.8 0.0 copy-done.9
  52.8 4.3 %shard_map.115 = (bf16[128,1024]{1,0:T(8,128)(2,1)S(1)}, bf16[256,512]{1,0:T(8,128)(2,1)}) custom-call(s32[1]{0:T(128)} %bitcast.1.near_at_ref, bf16[2,256,1024]{2,1,0:T(8,128)(2,1)S(1)} %get-tuple-element.12.after_y_ref, bf16[256,512]{1,0:T(8,128)(2,1)S(1)} %collective-permute-done.pot_ref, bf16[2,1024,1024]{2,1,0:T(8,128)(2,1)S(1)} %copy-done.9, ...), custom_call_target="tpu_custom_call" | custom-call | flops 2000000000 | bytes 4194304 | tf_op jit(solution)/shard_map/pallas_call | solution.py:492
  57.1 0.0 copy-start.11
  57.1 4.5 %all-to-all-start.1 = ((bf16[32,8,512]{2,1,0:T(8,128)(2,1)}), bf16[32,8,512]{2,1,0:T(8,128)(2,1)S(1)}, u32[]{:S(2)}, u32[]{:S(2)}) async-start(bf16[32,8,512]{2,1,0:T(8,128)(2,1)} %bitcast.6), calls=%async_computation.1 | async-start | bytes 524288 | tf_op jit(solution)/shard_map/all_to_all | solution.py:471
  61.5 0.0 copy-done
  61.6 0.4 shard_map.116.image_any
  62.0 17.8 %all-to-all-done.1 = bf16[32,8,512]{2,1,0:T(8,128)(2,1)S(1)} async-done(((bf16[32,8,512]{2,1,0:T(8,128)(2,1)}), bf16[32,8,512]{2,1,0:T(8,128)(2,1)S(1)}, u32[]{:S(2)}, u32[]{:S(2)}) %all-to-all-start.1) | async-done | bytes 262176 | tf_op jit(solution)/shard_map/all_to_all | solution.py:471
  79.8 0.9 shard_map.117
  80.7 38.2 %all_to_all.30 = bf16[32,8,1152]{2,1,0:T(8,128)(2,1)S(1)} all-to-all(bf16[32,8,1152]{2,1,0:T(8,128)(2,1)S(1)} %bitcast.19), channel_id=1, replica_groups=mesh['frag'=16,'band'=32] {'band'}, dimensions={0} | all-to-all | bytes 1179648 | tf_op jit(solution)/shard_map/all_to_all | solution.py:471
  119.0 17.6 %all_to_all.31 = f32[32,4,128]{2,1,0:T(4,128)S(1)} all-to-all(f32[32,4,128]{2,1,0:T(4,128)S(1)} %bitcast.23), channel_id=1, replica_groups=mesh['frag'=16,'band'=32] {'band'}, dimensions={0} | all-to-all | bytes 131072 | tf_op jit(solution)/shard_map/all_to_all | solution.py:471
  136.6 4.0 %shard_map.119 = (bf16[256,512]{1,0:T(8,128)(2,1)}, bf16[512,128]{1,0:T(8,128)(2,1)S(1)}) custom-call(f32[128,128]{1,0:T(8,128)S(1)} %bitcast.26, bf16[128,1024]{1,0:T(8,128)(2,1)S(1)} %get-tuple-element.17.stepped_ref), custom_call_target="tpu_custom_call" | custom-call | flops 1000000000 | bytes 1048576 | tf_op jit(solution)/shard_map/pallas_call | solution.py:500
  140.6 4.1 %all-to-all-start.4 = ((bf16[32,8,512]{2,1,0:T(8,128)(2,1)}), bf16[32,8,512]{2,1,0:T(8,128)(2,1)S(1)}, u32[]{:S(2)}, u32[]{:S(2)}) async-start(bf16[32,8,512]{2,1,0:T(8,128)(2,1)} %bitcast.12), calls=%async_computation.4 | async-start | bytes 524288 | tf_op jit(solution)/shard_map/all_to_all | solution.py:471
  144.7 0.0 copy-done.11
  144.7 0.1 copy.13.place_ref
  144.8 0.0 copy-done.1
  144.8 2.2 %copy-done.10 = bf16[2,1024,1024]{2,1,0:T(8,128)(2,1)S(1)} copy-done((bf16[2,1024,1024]{2,1,0:T(8,128)(2,1)S(1)}, bf16[2,1024,1024]{2,1,0:T(8,128)(2,1)}, u32[]{:S(2)}) %copy-start.10) | copy-done | bytes 4194328
  147.0 7.0 %shard_map.120 = bf16[16,80,128]{2,1,0:T(8,128)(2,1)} custom-call(s32[16,3]{1,0:T(8,128)S(1)} %copy.13.place_ref, s32[1]{0:T(128)} %bitcast.own_ref, bf16[256,1152]{1,0:T(8,128)(2,1)S(1)} %bitcast.21, bf16[512,128]{1,0:T(8,128)(2,1)S(1)} %get-tuple-element.18.inv_ref, bf16[2,1024,1024]{2,1,0:T(8,128)(2,1)S(1)} %copy-done.10, bf16[128,512]{1,0:T(8,128)(2,1)S(1)} %copy-done.2, ...), custom_call_target="tpu_custom_call" | custom-call | flops 4000000000 | bytes 6291456 | tf_op jit(solution)/shard_map/pallas_call | solution.py:502
  154.0 9.6 %all-to-all-done.4 = bf16[32,8,512]{2,1,0:T(8,128)(2,1)S(1)} async-done(((bf16[32,8,512]{2,1,0:T(8,128)(2,1)}), bf16[32,8,512]{2,1,0:T(8,128)(2,1)S(1)}, u32[]{:S(2)}, u32[]{:S(2)}) %all-to-all-start.4) | async-done | bytes 262176 | tf_op jit(solution)/shard_map/all_to_all | solution.py:471
  163.5 10.7 %all-to-all-start.5 = ((bf16[16,80,128]{2,1,0:T(8,128)(2,1)}), bf16[16,80,128]{2,1,0:T(8,128)(2,1)S(1)}, u32[]{:S(2)}, u32[]{:S(2)}) async-start(bf16[16,80,128]{2,1,0:T(8,128)(2,1)} %shard_map.120), calls=%async_computation.5 | async-start | bytes 655360 | tf_op jit(solution)/shard_map/all_to_all | solution.py:471
  174.3 0.2 reshape.76
  174.4 0.3 copy.17
  174.7 1.3 reshape.73
  176.0 7.4 %all-to-all-done.5.pieces_ref = bf16[16,80,128]{2,1,0:T(8,128)(2,1)S(1)} async-done(((bf16[16,80,128]{2,1,0:T(8,128)(2,1)}), bf16[16,80,128]{2,1,0:T(8,128)(2,1)S(1)}, u32[]{:S(2)}, u32[]{:S(2)}) %all-to-all-start.5) | async-done | bytes 327712 | tf_op jit(solution)/shard_map/all_to_all | solution.py:471
  183.4 1.5 shard_map.121
  (7 shorter events, 0.1 us)
Async XLA Ops:
  2.2 46.2 %copy-start.2 = (bf16[128,512]{1,0:T(8,128)(2,1)S(1)}, bf16[128,512]{1,0:T(8,128)(2,1)}, u32[]{:S(2)}) copy-start(bf16[128,512]{1,0:T(8,128)(2,1)} %constant.34.fwd_z_ref) | copy-start | bytes 393220
  2.2 37.5 %all-to-all-start = ((bf16[32,8,512]{2,1,0:T(8,128)(2,1)}), bf16[32,8,512]{2,1,0:T(8,128)(2,1)S(1)}, u32[]{:S(2)}, u32[]{:S(2)}) async-start(bf16[32,8,512]{2,1,0:T(8,128)(2,1)} %bitcast.4), calls=%async_computation | async-start | bytes 524288 | tf_op jit(solution)/shard_map/all_to_all | solution.py:471
  39.7 13.1 %collective-permute-start = (bf16[256,512]{1,0:T(8,128)(2,1)S(1)}, bf16[256,512]{1,0:T(8,128)(2,1)S(1)}, u32[]{:S(2)}, u32[]{:S(2)}) collective-permute-start(bf16[256,512]{1,0:T(8,128)(2,1)S(1)} %bitcast.24), channel_id=1, source_target_pairs={{0,1},{1,0},{2,3},{3,2},{4,5},{5,4},{6,7},{7,6},{8,9},{9,8},{10,11... | collective-permute-start | bytes 786440 | tf_op jit(solution)/shard_map/ppermute | solution.py:488
  42.0 0.9 copy-start.5
  42.9 0.7 copy-start.6
  46.4 1.9 %copy-start.7 = (bf16[2,1024,1024]{2,1,0:T(8,128)(2,1)}, bf16[2,1024,1024]{2,1,0:T(8,128)(2,1)S(1)}, u32[]{:S(2)}) copy-start(bf16[2,1024,1024]{2,1,0:T(8,128)(2,1)S(1)} %get-tuple-element.13.big_y_ref) | copy-start | bytes 12582916
  48.3 4.4 %copy-start.3 = (bf16[256,256]{1,0:T(8,128)(2,1)S(1)}, bf16[256,256]{1,0:T(8,128)(2,1)}, u32[]{:S(2)}) copy-start(bf16[256,256]{1,0:T(8,128)(2,1)} %constant.35.back_x_ref) | copy-start | bytes 393220
  48.3 4.4 %copy-start.4 = (bf16[256,256]{1,0:T(8,128)(2,1)S(1)}, bf16[256,256]{1,0:T(8,128)(2,1)}, u32[]{:S(2)}) copy-start(bf16[256,256]{1,0:T(8,128)(2,1)} %constant.36.send_ref) | copy-start | bytes 393220
  48.3 2.2 %copy-start.8 = (bf16[2,1024,1024]{2,1,0:T(8,128)(2,1)S(1)}, bf16[2,1024,1024]{2,1,0:T(8,128)(2,1)}, u32[]{:S(2)}) copy-start(bf16[2,1024,1024]{2,1,0:T(8,128)(2,1)} %copy-done.7) | copy-start | bytes 12582916
  50.6 2.2 %copy-start.9 = (bf16[2,1024,1024]{2,1,0:T(8,128)(2,1)S(1)}, bf16[2,1024,1024]{2,1,0:T(8,128)(2,1)}, u32[]{:S(2)}) copy-start(bf16[2,1024,1024]{2,1,0:T(8,128)(2,1)} %copy-done.7) | copy-start | bytes 12582916
  52.7 8.8 %copy-start = (bf16[256,256]{1,0:T(8,128)(2,1)S(1)}, bf16[256,256]{1,0:T(8,128)(2,1)}, u32[]{:S(2)}) copy-start(bf16[256,256]{1,0:T(8,128)(2,1)} %constant.37.fwd_x_ref) | copy-start | bytes 393220
  57.1 87.7 %copy-start.11 = (s32[16,3]{0,1:T(4,128)S(1)}, s32[16,3]{0,1:T(4,128)}, u32[]{:S(2)}) copy-start(s32[16,3]{0,1:T(4,128)} %param.13) | copy-start | bytes 580
  57.1 87.7 %copy-start.1 = (f32[2,8,128]{2,1,0:T(8,128)S(1)}, f32[2,8,128]{2,1,0:T(8,128)}, u32[]{:S(2)}) copy-start(f32[2,8,128]{2,1,0:T(8,128)} %tile_ref.1) | copy-start | bytes 24580
  57.1 22.7 %all-to-all-start.1 = ((bf16[32,8,512]{2,1,0:T(8,128)(2,1)}), bf16[32,8,512]{2,1,0:T(8,128)(2,1)S(1)}, u32[]{:S(2)}, u32[]{:S(2)}) async-start(bf16[32,8,512]{2,1,0:T(8,128)(2,1)} %bitcast.6), calls=%async_computation.1 | async-start | bytes 524288 | tf_op jit(solution)/shard_map/all_to_all | solution.py:471
  140.6 22.9 %all-to-all-start.4 = ((bf16[32,8,512]{2,1,0:T(8,128)(2,1)}), bf16[32,8,512]{2,1,0:T(8,128)(2,1)S(1)}, u32[]{:S(2)}, u32[]{:S(2)}) async-start(bf16[32,8,512]{2,1,0:T(8,128)(2,1)} %bitcast.12), calls=%async_computation.4 | async-start | bytes 524288 | tf_op jit(solution)/shard_map/all_to_all | solution.py:471
  144.8 2.2 %copy-start.10 = (bf16[2,1024,1024]{2,1,0:T(8,128)(2,1)S(1)}, bf16[2,1024,1024]{2,1,0:T(8,128)(2,1)}, u32[]{:S(2)}) copy-start(bf16[2,1024,1024]{2,1,0:T(8,128)(2,1)} %copy-done.7) | copy-start | bytes 12582916
  163.5 19.9 %all-to-all-start.5 = ((bf16[16,80,128]{2,1,0:T(8,128)(2,1)}), bf16[16,80,128]{2,1,0:T(8,128)(2,1)S(1)}, u32[]{:S(2)}, u32[]{:S(2)}) async-start(bf16[16,80,128]{2,1,0:T(8,128)(2,1)} %shard_map.120), calls=%async_computation.5 | async-start | bytes 655360 | tf_op jit(solution)/shard_map/all_to_all | solution.py:471
